TPU v7x, 512 devices: a whole 4x4x16 slice. The times are simulated.
512 devices in a mesh: snode: 128 (over z, x, core), rhs: 4 (over y).
Axes of the slice: x: 4, y: 4, z: 16, core: 2. Of those that a mesh axis runs over, the one named last changes fastest.
Arguments:
- right_sides: float32 [3, 256, 256, 512], P(None, 'snode', None, 'rhs'), may hold values from -6 to 6
- diag_inverse: float32 [3, 256, 256, 256], P(None, 'snode', 'rhs')
- off_diagonal: bfloat16 [2, 256, 1024, 256], P(None, 'snode'), may hold values from -0.125 to 0.125
- target_snode: int32 [2, 256, 64], P(None, 'snode'), may hold values from 0 to 255, as said below
- target_block: int32 [2, 256, 64], P(None, 'snode'), may hold values from 0 to 15
Outputs:
- solution: float32 [3, 256, 256, 512], P(None, 'snode', None, 'rhs')
Inputs may be any that keep to these rules, and one draw needn't show every extreme that they name: `target_snode`: each entry is a supernode's position in the next level; the supernodes at positions i * 2 to i * 2 + 1 belong to index i of snode. Of one level's blocks held by one index of snode, at most 2 name supernodes of any one index, and some index receives exactly 2 from every index in every level.
All inputs are finite; a program needn't handle non-finite values.
Results may differ from a plain program's by a relative error of at most 0.0038.
Values may be sent and summed in bfloat16 or wider, within the bound.
No kernel may reach another device: no remote copies, remote signals or barrier semaphores. Data moves between devices by JAX's collectives and lax.ppermute only.
A program may use at most 64 MiB of HBM per device.

v0:
```python
import jax
import jax.numpy as jnp
from jax import lax
from jax.sharding import PartitionSpec as P

BR = 16


def on_device(right_sides, diag_inverse, off_diagonal, target_snode, target_block):
    precise = lax.Precision.HIGHEST
    levels = right_sides.shape[0]
    local_nodes = right_sides.shape[1]
    order_size = right_sides.shape[2]
    columns = right_sides.shape[3]
    per_node = target_snode.shape[2]
    row_blocks = order_size // BR
    devices = lax.axis_size("snode")
    outgoing = local_nodes * per_node
    capacity = 2 * outgoing // devices
    slot_count = devices * capacity
    local_rows = local_nodes * row_blocks
    front_count = 1
    front_width = columns // front_count
    full_diag = [
        lax.all_gather(diag_inverse[height], "rhs", axis=1, tiled=True) for height in range(levels)
    ]
    block_order = lax.iota(jnp.int32, outgoing)
    slot_ids = lax.iota(jnp.int32, slot_count)
    row_ids = lax.iota(jnp.int32, local_rows)
    routes = []
    for height in range(levels - 1):
        flat_target = target_snode[height].reshape(outgoing)
        owner_dev = flat_target // local_nodes
        target_code = flat_target % local_nodes * row_blocks + target_block[height].reshape(
            outgoing
        )
        earlier = (owner_dev[:, None] == owner_dev[None, :]) & (
            block_order[None, :] < block_order[:, None]
        )
        destination = owner_dev * capacity + jnp.sum(earlier.astype(jnp.int32), axis=1)
        placed = destination[None, :] == slot_ids[:, None]
        source = jnp.max(jnp.where(placed, block_order[None, :], -1), axis=1)
        slot_code = jnp.max(jnp.where(placed, target_code[None, :], -1), axis=1).reshape(
            devices, capacity
        )
        routes.append((destination, source, slot_code))
    residual_list = [right_sides[0]]
    lower_sols = [[]]
    arrivals = [[]]
    for height in range(levels):
        front = 0
        solve_result = jnp.einsum(
            "svw,swr->svr", full_diag[height], residual_list[front], precision=precise
        )
        lower_sols[front].append(solve_result)
        if height + 1 < levels:
            destination, source, slot_code = routes[height]
            update = jnp.einsum(
                "skw,swr->skr",
                off_diagonal[height],
                solve_result.astype(jnp.bfloat16),
                preferred_element_type=jnp.float32,
            )
            update = update.astype(jnp.bfloat16).reshape(outgoing, BR * front_width)
            outbound = jnp.where(
                (source >= 0)[:, None], update[jnp.maximum(source, 0)], jnp.zeros((), jnp.bfloat16)
            )
            outbound = outbound.reshape(devices, capacity, BR * front_width)
            inbound, inbound_code = (
                lax.all_to_all(outbound, "snode", split_axis=0, concat_axis=0, tiled=True),
                lax.all_to_all(slot_code, "snode", split_axis=0, concat_axis=0, tiled=True),
            )
            arrived = inbound_code.reshape(slot_count)
            arrivals[front].append(arrived)
            gather_table = (arrived[None, :] == row_ids[:, None]).astype(jnp.bfloat16)
            summed = jnp.dot(
                gather_table,
                inbound.reshape(slot_count, BR * front_width),
                preferred_element_type=jnp.float32,
            )
            summed = summed.reshape(local_nodes, order_size, front_width)
            upcoming = right_sides[height + 1]
            residual_list[front] = upcoming - summed
    answer = [[None] * levels]
    for height in range(levels - 1, -1, -1):
        front = 0
        if height == levels - 1:
            carried = lower_sols[front][height]
        else:
            destination, source, slot_code = routes[height]
            above_rows = (
                answer[front][height + 1].astype(jnp.bfloat16).reshape(local_rows, BR * front_width)
            )
            arrived = arrivals[front][height]
            outbound = jnp.where(
                (arrived >= 0)[:, None],
                above_rows[jnp.maximum(arrived, 0)],
                jnp.zeros((), jnp.bfloat16),
            )
            outbound = outbound.reshape(devices, capacity, BR * front_width)
            returned = lax.all_to_all(outbound, "snode", split_axis=0, concat_axis=0, tiled=True)
            block_rows = returned.reshape(slot_count, BR * front_width)[destination]
            block_rows = block_rows.reshape(local_nodes, per_node * BR, front_width)
            carried = lower_sols[front][height] - jnp.einsum(
                "skw,skr->swr", off_diagonal[height], block_rows, preferred_element_type=jnp.float32
            )
        result = jnp.einsum("swv,swr->svr", full_diag[height], carried, precision=precise)
        answer[front][height] = result
    stacked = [answer[0][height] for height in range(levels)]
    return jnp.stack(stacked, axis=0)


def solution(mesh):
    in_specs = (
        P(None, "snode", None, "rhs"),
        P(None, "snode", "rhs", None),
        P(None, "snode", None, None),
        P(None, "snode", None),
        P(None, "snode", None),
    )
    out_specs = P(None, "snode", None, "rhs")
    return jax.shard_map(
        on_device, mesh=mesh, in_specs=in_specs, out_specs=out_specs, check_vma=False
    )
```

profile of v0, /device:TPU:11, one launch (start us, length us, event | category | flops | bytes accessed | tf_op | source)
XLA Modules:
  0.0 372.7 jit_solution(11072806632343055890)
XLA Ops:
  0.0 0.8 fusion.41
  2.8 19.7 %all-to-all-start = ((s32[128,1,2]{2,1,0:T(1,128)}), s32[128,1,2]{2,1,0:T(1,128)S(1)}, u32[]{:S(2)}, u32[]{:S(2)}) async-start(s32[128,1,2]{2,1,0:T(1,128)} %bitcast.2), calls=%async_computation | async-start | bytes 131072 | tf_op jit(solution)/shard_map/all_to_all | solution.py:71
  22.6 1.7 fusion.40
  24.3 11.0 %all-gather = f32[1,2,256,256]{3,2,1,0:T(8,128)S(1)} all-gather(f32[1,2,64,256]{3,2,1,0:T(8,128)S(1)} %get-tuple-element.13), channel_id=2, replica_groups=mesh['snode'=128,'rhs'=4] {'rhs'}, dimensions={2}, use_global_device_ids=true | all-gather | bytes 655360 | tf_op jit(solution)/shard_map/all_gather | solution.py:25
  35.7 1.6 fusion.20
  38.6 1.0 copy.54
  39.6 1.3 reshape.482
  40.9 2.3 gather_fusion
  43.2 1.7 gather.27
  45.1 0.8 all_to_all.27
  45.9 18.8 %all-to-all-start.2 = ((s32[128,1,2]{2,1,0:T(1,128)}), s32[128,1,2]{2,1,0:T(1,128)S(1)}, u32[]{:S(2)}, u32[]{:S(2)}) async-start(s32[128,1,2]{2,1,0:T(1,128)} %bitcast.8), calls=%async_computation.2 | async-start | bytes 131072 | tf_op jit(solution)/shard_map/all_to_all | solution.py:71
  64.7 2.0 broadcast_select_fusion.2
  66.7 11.8 %all-to-all-done.2 = s32[128,1,2]{2,1,0:T(1,128)S(1)} async-done(((s32[128,1,2]{2,1,0:T(1,128)}), s32[128,1,2]{2,1,0:T(1,128)S(1)}, u32[]{:S(2)}, u32[]{:S(2)}) %all-to-all-start.2) | async-done | bytes 1056 | tf_op jit(solution)/shard_map/all_to_all | solution.py:71
  78.5 7.8 %all-to-all-start.1 = ((bf16[128,2,2048]{2,1,0:T(2,128)(2,1)}), bf16[128,2,2048]{2,1,0:T(2,128)(2,1)}, u32[]{:S(2)}, u32[]{:S(2)}) async-start(bf16[128,2,2048]{2,1,0:T(2,128)(2,1)} %broadcast_select_fusion.2), calls=%async_computation.1 | async-start | bytes 2097152 | tf_op jit(solution)/shard_map/all_to_all | solution.py:70
  87.1 11.3 %all-gather.1 = f32[1,2,256,256]{3,2,1,0:T(8,128)S(1)} all-gather(f32[1,2,64,256]{3,2,1,0:T(8,128)S(1)} %get-tuple-element.15), channel_id=3, replica_groups=mesh['snode'=128,'rhs'=4] {'rhs'}, dimensions={2}, use_global_device_ids=true | all-gather | bytes 655360 | tf_op jit(solution)/shard_map/all_gather | solution.py:25
  98.9 1.9 maximum_reduce_fusion
  101.0 39.5 %all-to-all-done.1 = bf16[128,2,2048]{2,1,0:T(2,128)(2,1)} async-done(((bf16[128,2,2048]{2,1,0:T(2,128)(2,1)}), bf16[128,2,2048]{2,1,0:T(2,128)(2,1)}, u32[]{:S(2)}, u32[]{:S(2)}) %all-to-all-start.1) | async-done | bytes 1048608 | tf_op jit(solution)/shard_map/all_to_all | solution.py:70
  140.5 2.3 reshape.483
  142.7 1.5 fusion.30
  144.3 1.7 fusion.17
  147.0 2.5 gather_fusion.1
  149.4 1.7 gather.29
  151.2 2.0 broadcast_select_fusion
  153.2 8.1 %all-to-all-start.3 = ((bf16[128,2,2048]{2,1,0:T(2,128)(2,1)}), bf16[128,2,2048]{2,1,0:T(2,128)(2,1)}, u32[]{:S(2)}, u32[]{:S(2)}) async-start(bf16[128,2,2048]{2,1,0:T(2,128)(2,1)} %broadcast_select_fusion), calls=%async_computation.3 | async-start | bytes 2097152 | tf_op jit(solution)/shard_map/all_to_all | solution.py:70
  161.4 11.1 %all-gather.2 = f32[1,2,256,256]{3,2,1,0:T(8,128)S(1)} all-gather(f32[1,2,64,256]{3,2,1,0:T(8,128)S(1)} %copy-done.11), channel_id=4, replica_groups=mesh['snode'=128,'rhs'=4] {'rhs'}, dimensions={2}, use_global_device_ids=true | all-gather | bytes 655360 | tf_op jit(solution)/shard_map/all_gather | solution.py:25
  173.7 41.8 %all-to-all-done.3 = bf16[128,2,2048]{2,1,0:T(2,128)(2,1)} async-done(((bf16[128,2,2048]{2,1,0:T(2,128)(2,1)}), bf16[128,2,2048]{2,1,0:T(2,128)(2,1)}, u32[]{:S(2)}, u32[]{:S(2)}) %all-to-all-start.3) | async-done | bytes 1048608 | tf_op jit(solution)/shard_map/all_to_all | solution.py:70
  215.5 2.3 reshape.486
  217.7 1.5 fusion.31
  219.3 1.7 fusion.13
  221.0 1.1 bitcast_convert_fusion.1
  222.3 1.5 gather_fusion.2
  223.8 1.5 gather.31
  225.3 3.3 broadcast_select_fusion.1
  228.6 8.3 %all-to-all-start.4 = ((bf16[128,2,2048]{2,1,0:T(2,128)(2,1)}), bf16[128,2,2048]{2,1,0:T(2,128)(2,1)}, u32[]{:S(2)}, u32[]{:S(2)}) async-start(bf16[128,2,2048]{2,1,0:T(2,128)(2,1)} %broadcast_select_fusion.1), calls=%async_computation.4 | async-start | bytes 2097152 | tf_op jit(solution)/shard_map/all_to_all | solution.py:101
  238.1 52.9 %all-to-all-done.4 = bf16[128,2,2048]{2,1,0:T(2,128)(2,1)} async-done(((bf16[128,2,2048]{2,1,0:T(2,128)(2,1)}), bf16[128,2,2048]{2,1,0:T(2,128)(2,1)}, u32[]{:S(2)}, u32[]{:S(2)}) %all-to-all-start.4) | async-done | bytes 1048608 | tf_op jit(solution)/shard_map/all_to_all | solution.py:101
  291.0 1.5 reshape.489
  292.5 1.7 gather_fusion.3
  294.2 1.3 reshape.490
  295.9 1.2 bitcast_convert_fusion
  297.3 1.5 gather_fusion.4
  298.8 1.5 gather.34
  300.3 3.2 broadcast_select_fusion.3
  303.5 8.1 %all-to-all-start.5 = ((bf16[128,2,2048]{2,1,0:T(2,128)(2,1)}), bf16[128,2,2048]{2,1,0:T(2,128)(2,1)}, u32[]{:S(2)}, u32[]{:S(2)}) async-start(bf16[128,2,2048]{2,1,0:T(2,128)(2,1)} %broadcast_select_fusion.3), calls=%async_computation.5 | async-start | bytes 2097152 | tf_op jit(solution)/shard_map/all_to_all | solution.py:101
  311.7 54.0 %all-to-all-done.5 = bf16[128,2,2048]{2,1,0:T(2,128)(2,1)} async-done(((bf16[128,2,2048]{2,1,0:T(2,128)(2,1)}), bf16[128,2,2048]{2,1,0:T(2,128)(2,1)}, u32[]{:S(2)}, u32[]{:S(2)}) %all-to-all-start.5) | async-done | bytes 1048608 | tf_op jit(solution)/shard_map/all_to_all | solution.py:101
  365.7 1.5 reshape.492
  367.2 1.7 gather_fusion.5
  368.9 1.3 reshape.493
  371.5 1.1 copy.67
  (102 shorter events, 10.8 us)
Async XLA Ops:
  0.0 37.9 %copy-start = (bf16[2,2,1024,256]{3,2,1,0:T(8,128)(2,1)S(1)}, bf16[2,2,1024,256]{3,2,1,0:T(8,128)(2,1)}, u32[]{:S(2)}) copy-start(bf16[2,2,1024,256]{3,2,1,0:T(8,128)(2,1)} %param.7) | copy-start | bytes 6291460
  0.8 1.1 copy-start.15
  0.9 37.6 %copy-start.17 = (s32[1,2,64]{2,1,0:T(2,128)}, s32[1,2,64]{2,1,0:T(2,128)S(1)}, u32[]{:S(2)}) copy-start(s32[1,2,64]{2,1,0:T(2,128)S(1)} %get-tuple-element.16) | copy-start | bytes 1540
  1.9 22.4 %copy-start.19 = (s32[128]{0:T(128)}, s32[128]{0:T(128)S(1)}, u32[]{:S(2)}) copy-start(s32[128]{0:T(128)S(1)} %convert_reduce_fusion.1) | copy-start | bytes 1540
  2.8 43.1 %all-to-all-start = ((s32[128,1,2]{2,1,0:T(1,128)}), s32[128,1,2]{2,1,0:T(1,128)S(1)}, u32[]{:S(2)}, u32[]{:S(2)}) async-start(s32[128,1,2]{2,1,0:T(1,128)} %bitcast.2), calls=%async_computation | async-start | bytes 131072 | tf_op jit(solution)/shard_map/all_to_all | solution.py:71
  35.3 3.3 copy-start.1
  35.6 5.2 %copy-start.21 = (s32[128]{0:T(128)}, s32[128]{0:T(128)S(1)}, u32[]{:S(2)}) copy-start(s32[128]{0:T(128)S(1)} %convert_reduce_fusion) | copy-start | bytes 1540
  37.2 0.7 copy-start.5
  45.9 53.0 %copy-start.9 = (s32[128,1,2]{2,1,0:T(1,128)}, s32[128,1,2]{2,1,0:T(1,128)S(1)}, u32[]{:S(2)}) copy-start(s32[128,1,2]{2,1,0:T(1,128)S(1)} %all-to-all-done) | copy-start | bytes 3076
  45.9 32.6 %all-to-all-start.2 = ((s32[128,1,2]{2,1,0:T(1,128)}), s32[128,1,2]{2,1,0:T(1,128)S(1)}, u32[]{:S(2)}, u32[]{:S(2)}) async-start(s32[128,1,2]{2,1,0:T(1,128)} %bitcast.8), calls=%async_computation.2 | async-start | bytes 131072 | tf_op jit(solution)/shard_map/all_to_all | solution.py:71
  78.5 61.9 %all-to-all-start.1 = ((bf16[128,2,2048]{2,1,0:T(2,128)(2,1)}), bf16[128,2,2048]{2,1,0:T(2,128)(2,1)}, u32[]{:S(2)}, u32[]{:S(2)}) async-start(bf16[128,2,2048]{2,1,0:T(2,128)(2,1)} %broadcast_select_fusion.2), calls=%async_computation.1 | async-start | bytes 2097152 | tf_op jit(solution)/shard_map/all_to_all | solution.py:70
  98.3 46.0 %copy-start.3 = (f32[1,2,256,256]{3,2,1,0:T(8,128)}, f32[1,2,256,256]{3,2,1,0:T(8,128)S(1)}, u32[]{:S(2)}) copy-start(f32[1,2,256,256]{3,2,1,0:T(8,128)S(1)} %all-gather.1) | copy-start | bytes 1572868
  151.2 21.4 %copy-start.13 = (s32[128,2]{1,0:T(8,128)S(1)}, s32[128,2]{1,0:T(8,128)}, u32[]{:S(2)}) copy-start(s32[128,2]{1,0:T(8,128)} %get-tuple-element.29) | copy-start | bytes 3076
  153.2 8.2 %copy-start.11 = (f32[1,2,64,256]{3,2,1,0:T(8,128)S(1)}, f32[1,2,64,256]{3,2,1,0:T(8,128)}, u32[]{:S(2)}) copy-start(f32[1,2,64,256]{3,2,1,0:T(8,128)} %get-tuple-element.14) | copy-start | bytes 393220
  153.2 19.3 %copy-start.14 = (s32[128,2]{1,0:T(8,128)S(1)}, s32[128,2]{1,0:T(8,128)}, u32[]{:S(2)}) copy-start(s32[128,2]{1,0:T(8,128)} %get-tuple-element.28) | copy-start | bytes 3076
  153.2 62.3 %all-to-all-start.3 = ((bf16[128,2,2048]{2,1,0:T(2,128)(2,1)}), bf16[128,2,2048]{2,1,0:T(2,128)(2,1)}, u32[]{:S(2)}, u32[]{:S(2)}) async-start(bf16[128,2,2048]{2,1,0:T(2,128)(2,1)} %broadcast_select_fusion), calls=%async_computation.3 | async-start | bytes 2097152 | tf_op jit(solution)/shard_map/all_to_all | solution.py:70
  225.3 11.6 %copy-start.18 = (s32[1,2,64]{2,1,0:T(2,128)S(1)}, s32[1,2,64]{2,1,0:T(2,128)}, u32[]{:S(2)}) copy-start(s32[1,2,64]{2,1,0:T(2,128)} %copy-done.17) | copy-start | bytes 1540
  225.3 11.7 %copy-start.22 = (s32[128]{0:T(128)S(1)}, s32[128]{0:T(128)}, u32[]{:S(2)}) copy-start(s32[128]{0:T(128)} %copy-done.21) | copy-start | bytes 1540
  225.3 11.7 %copy-start.12 = (s32[128,2]{1,0:T(8,128)S(1)}, s32[128,2]{1,0:T(8,128)}, u32[]{:S(2)}) copy-start(s32[128,2]{1,0:T(8,128)} %get-tuple-element.5) | copy-start | bytes 3076
  225.3 11.8 %copy-start.10 = (s32[128,1,2]{2,1,0:T(1,128)S(1)}, s32[128,1,2]{2,1,0:T(1,128)}, u32[]{:S(2)}) copy-start(s32[128,1,2]{2,1,0:T(1,128)} %copy-done.9) | copy-start | bytes 3076
  228.6 62.4 %all-to-all-start.4 = ((bf16[128,2,2048]{2,1,0:T(2,128)(2,1)}), bf16[128,2,2048]{2,1,0:T(2,128)(2,1)}, u32[]{:S(2)}, u32[]{:S(2)}) async-start(bf16[128,2,2048]{2,1,0:T(2,128)(2,1)} %broadcast_select_fusion.1), calls=%async_computation.4 | async-start | bytes 2097152 | tf_op jit(solution)/shard_map/all_to_all | solution.py:101
  294.2 1.7 copy-start.4
  300.3 11.3 %copy-start.16 = (s32[1,2,64]{2,1,0:T(2,128)S(1)}, s32[1,2,64]{2,1,0:T(2,128)}, u32[]{:S(2)}) copy-start(s32[1,2,64]{2,1,0:T(2,128)} %copy-done.15) | copy-start | bytes 1540
  300.3 11.4 %copy-start.20 = (s32[128]{0:T(128)S(1)}, s32[128]{0:T(128)}, u32[]{:S(2)}) copy-start(s32[128]{0:T(128)} %copy-done.19) | copy-start | bytes 1540
  303.5 62.2 %all-to-all-start.5 = ((bf16[128,2,2048]{2,1,0:T(2,128)(2,1)}), bf16[128,2,2048]{2,1,0:T(2,128)(2,1)}, u32[]{:S(2)}, u32[]{:S(2)}) async-start(bf16[128,2,2048]{2,1,0:T(2,128)(2,1)} %broadcast_select_fusion.3), calls=%async_computation.5 | async-start | bytes 2097152 | tf_op jit(solution)/shard_map/all_to_all | solution.py:101
  367.2 3.1 copy-start.6
  368.9 1.9 copy-start.2
  370.3 1.2 copy-start.7
  370.3 1.2 copy-start.8
where the time goes:
time: 374 us; the launch traced here: 373 us
  waiting for transfers between devices  200 us (53%)
  starting transfers between devices  70.7 us (19%)
  local copies, waits for them, and re-layouts  40.2 us (11%)
  blocking collectives  33.4 us (9%)
  other arithmetic  15.2 us (4%)
  matrix products  12.7 us (3%)
    all_to_all x4, waiting for transfers between devices, on_device(): lax.all_to_all(outbound, 'snode', split_axis=0, concat_axis=0, tiled=True)  188 us
    all_to_all x2, starting transfers between devices, on_device(): lax.all_to_all(slot_code, 'snode', split_axis=0, concat_axis=0, tiled=True)  38.5 us
    all_gather x3, blocking collectives, on_device(): lax.all_gather(diag_inverse[height], 'rhs', axis=1, tiled=True)  33.4 us
    all_to_all x4, starting transfers between devices, on_device(): lax.all_to_all(outbound, 'snode', split_axis=0, concat_axis=0, tiled=True)  32.2 us
    all_to_all x2, waiting for transfers between devices, on_device(): lax.all_to_all(slot_code, 'snode', split_axis=0, concat_axis=0, tiled=True)  11.9 us
    gather x4, local copies, waits for them, and re-layouts, on_device(): update[jnp.maximum(source, 0)]  8.3 us
  transfers between devices with their start and end apart: 6, of which 5 were waited for; matrix products, arithmetic and copies ran while one was open for 5% of the time, Pallas kernels for 0%

commit v1 on v0

v1 whole, which is shorter than its diff:
```python
import functools

import jax
import jax.numpy as jnp
from jax import lax
from jax.experimental import pallas as pl
from jax.experimental.pallas import tpu as pltpu
from jax.sharding import PartitionSpec as P

BR = 16
F32 = jnp.float32
BF16 = jnp.bfloat16
PRECISE = lax.Precision.HIGHEST


def low_lanes(shape):
    return lax.broadcasted_iota(jnp.int32, shape, len(shape) - 1) < shape[-1] // 2


def swap_lanes(x):
    return pltpu.roll(x, x.shape[-1] // 2, axis=x.ndim - 1)


def doubled(x):
    return jnp.where(low_lanes(x.shape), x, swap_lanes(x))


def pick_half(x, half):
    swapped = swap_lanes(x)
    low = low_lanes(x.shape)
    return jnp.where(low, x, swapped) if half == 0 else jnp.where(low, swapped, x)


def fold(x):
    lanes = x.shape[-1]
    parts = x.reshape(x.shape[0] // BR, 2, BR // 2, lanes)
    top, bottom = parts[:, 0], parts[:, 1]
    return jnp.where(low_lanes(top.shape), top, bottom)


def unfold(x):
    lanes = x.shape[-1]
    blocks = x.reshape(x.shape[0] // (BR // 2), BR // 2, lanes)
    swapped = pltpu.roll(x, lanes // 2, axis=1).reshape(blocks.shape)
    low = low_lanes(blocks.shape)
    top = jnp.where(low, blocks, swapped)
    bottom = jnp.where(low, swapped, blocks)
    return jnp.stack([top, bottom], axis=1).reshape(2 * x.shape[0], lanes)


def whole_diag(diag_ref, s):
    parts = [diag_ref[y, s] for y in range(diag_ref.shape[0])]
    return jnp.concatenate(parts, axis=0)


def solve(diag, x):
    return lax.dot_general(
        diag, x, (((1,), (0,)), ((), ())), precision=PRECISE, preferred_element_type=F32
    )


def solve_transposed(diag, x):
    return lax.dot_general(
        diag, x, (((0,), (0,)), ((), ())), precision=PRECISE, preferred_element_type=F32
    )


def place(table_ref, index_ref, out_ref):
    slots = out_ref.shape[0]

    def body(i, _):
        out_ref[i] = table_ref[index_ref[i]].astype(BF16)
        return 0

    lax.fori_loop(0, slots, body, 0, unroll=8)


def send_updates(nodes, low_ref, off_ref, source_ref, out_ref, table_ref):
    per_node = off_ref.shape[1] // BR
    for s in range(nodes):
        update = jnp.dot(off_ref[s], low_ref[s].astype(BF16), preferred_element_type=F32)
        table_ref[pl.ds(s * per_node, per_node)] = fold(update)
    table_ref[nodes * per_node] = jnp.zeros(table_ref.shape[1:], F32)
    place(table_ref, source_ref, out_ref)


def send_rows(nodes, sol_ref, code_ref, out_ref, table_ref):
    blocks = sol_ref.shape[1] // BR
    for s in range(nodes):
        table_ref[pl.ds(s * blocks, blocks)] = fold(sol_ref[s])
    table_ref[nodes * blocks] = jnp.zeros(table_ref.shape[1:], F32)
    place(table_ref, code_ref, out_ref)


def summed_updates(inbound_ref, gather_ref):
    slots, half_block, lanes = inbound_ref.shape
    rows = inbound_ref[...].astype(F32).reshape(slots * half_block, lanes).astype(BF16)
    return jnp.dot(gather_ref[...], rows, preferred_element_type=F32)


def first_kernel(half, source_ref, diag_ref, rhs_ref, off_ref, low_ref, out_ref, table_ref):
    nodes = rhs_ref.shape[0]
    for s in range(nodes):
        low_ref[s] = solve(whole_diag(diag_ref, s), pick_half(rhs_ref[s], half))
    send_updates(nodes, low_ref, off_ref, source_ref, out_ref, table_ref)


def lower_solve(half, inbound_ref, gather_ref, diag_ref, rhs_ref, low_ref):
    nodes, order, _ = rhs_ref.shape
    total = summed_updates(inbound_ref, gather_ref)
    part = order // 2
    for s in range(nodes):
        residual = pick_half(rhs_ref[s], half) - unfold(total[s * part : (s + 1) * part])
        low_ref[s] = solve(whole_diag(diag_ref, s), residual)


def middle_kernel(
    half, source_ref, inbound_ref, gather_ref, diag_ref, rhs_ref, off_ref, low_ref, out_ref, table_ref
):
    lower_solve(half, inbound_ref, gather_ref, diag_ref, rhs_ref, low_ref)
    send_updates(rhs_ref.shape[0], low_ref, off_ref, source_ref, out_ref, table_ref)


def top_kernel(
    half, code_ref, inbound_ref, gather_ref, diag_ref, rhs_ref, sol_ref, out_ref, low_ref, table_ref
):
    lower_solve(half, inbound_ref, gather_ref, diag_ref, rhs_ref, low_ref)
    nodes = rhs_ref.shape[0]
    for s in range(nodes):
        sol_ref[s] = solve_transposed(whole_diag(diag_ref, s), low_ref[s])
    send_rows(nodes, sol_ref, code_ref, out_ref, table_ref)


def upper_solve(dest_ref, inbound_ref, diag_ref, off_ref, low_ref, sol_ref, rows_ref):
    nodes = off_ref.shape[0]
    per_node = off_ref.shape[1] // BR
    order = off_ref.shape[2]

    def body(k, _):
        rows_ref[k] = inbound_ref[dest_ref[k]].astype(F32)
        return 0

    lax.fori_loop(0, nodes * per_node, body, 0, unroll=8)
    for s in range(nodes):
        blocks = rows_ref[pl.ds(s * per_node, per_node)]
        rows = unfold(blocks.reshape(per_node * BR // 2, blocks.shape[-1])).astype(BF16)
        taken = lax.dot_general(
            off_ref[s], rows, (((0,), (0,)), ((), ())), preferred_element_type=F32
        )
        sol_ref[s] = solve_transposed(whole_diag(diag_ref, s), low_ref[s] - taken)


def upper_kernel(
    dest_ref, code_ref, inbound_ref, diag_ref, off_ref, low_ref, sol_ref, out_ref, rows_ref, table_ref
):
    upper_solve(dest_ref, inbound_ref, diag_ref, off_ref, low_ref, sol_ref, rows_ref)
    send_rows(off_ref.shape[0], sol_ref, code_ref, out_ref, table_ref)


def last_kernel(dest_ref, inbound_ref, diag_ref, off_ref, low_ref, sol_ref, rows_ref):
    upper_solve(dest_ref, inbound_ref, diag_ref, off_ref, low_ref, sol_ref, rows_ref)


def call(kernel, name, scalars, arrays, outs, scratch, flops):
    moved = sum(a.size * a.dtype.itemsize for a in arrays)
    moved += sum(o.size * o.dtype.itemsize for o in outs)
    return pl.pallas_call(
        kernel,
        name=name,
        out_shape=outs,
        in_specs=[pl.BlockSpec(memory_space=pltpu.SMEM)] * len(scalars)
        + [pl.BlockSpec(memory_space=pltpu.VMEM)] * len(arrays),
        out_specs=[pl.BlockSpec(memory_space=pltpu.VMEM)] * len(outs),
        scratch_shapes=scratch,
        compiler_params=pltpu.CompilerParams(vmem_limit_bytes=24 << 20),
        cost_estimate=pl.CostEstimate(flops=flops, bytes_accessed=moved, transcendentals=0),
    )(*scalars, *arrays)


def on_device(right_sides, diag_inverse, off_diagonal, target_snode, target_block):
    levels, nodes, order, lanes = right_sides.shape
    per_node = target_snode.shape[2]
    row_blocks = order // BR
    devices = lax.axis_size("snode")
    outgoing = nodes * per_node
    capacity = 2 * outgoing // devices
    slots = devices * capacity
    local_rows = nodes * row_blocks
    half_block = BR // 2
    halves = range(2)

    block_order = lax.iota(jnp.int32, outgoing)
    slot_ids = lax.iota(jnp.int32, slots)
    sources, destinations, codes = [], [], []
    for h in range(levels - 1):
        flat_target = target_snode[h].reshape(outgoing)
        owner = flat_target // nodes
        row = flat_target % nodes * row_blocks + target_block[h].reshape(outgoing)
        earlier = (owner[:, None] == owner[None, :]) & (block_order[None, :] < block_order[:, None])
        destination = owner * capacity + jnp.sum(earlier.astype(jnp.int32), axis=1)
        placed = destination[None, :] == slot_ids[:, None]
        sources.append(jnp.min(jnp.where(placed, block_order[None, :], outgoing), axis=1))
        codes.append(jnp.min(jnp.where(placed, row[None, :], local_rows), axis=1))
        destinations.append(destination)
    outbound_codes = jnp.stack([c.reshape(devices, capacity) for c in codes], axis=1)
    outbound_codes = outbound_codes.reshape(devices, (levels - 1) * capacity)

    def exchange(x):
        return lax.all_to_all(x, "snode", split_axis=0, concat_axis=0, tiled=True)

    diags = [lax.all_gather(diag_inverse[h], "rhs", axis=0, tiled=False) for h in range(levels)]

    vector = jax.ShapeDtypeStruct((nodes, order, lanes), F32)
    payload = jax.ShapeDtypeStruct((slots, half_block, lanes), BF16)
    update_table = pltpu.VMEM((outgoing + 1, half_block, lanes), F32)
    row_table = pltpu.VMEM((local_rows + 1, half_block, lanes), F32)
    low_scratch = pltpu.VMEM((nodes, order, lanes), F32)
    rows_scratch = pltpu.VMEM((outgoing, half_block, lanes), F32)
    flops = 40 * nodes * order * order * lanes

    lower = [[None] * levels for _ in halves]
    answer = [[None] * levels for _ in halves]
    inbound = [None, None]
    for c in halves:
        lower[c][0], out = call(
            functools.partial(first_kernel, c),
            "first",
            [sources[0]],
            [diags[0], right_sides[0], off_diagonal[0]],
            [vector, payload],
            [update_table],
            flops,
        )
        inbound[c] = exchange(out)

    arrived = exchange(outbound_codes).reshape(devices, levels - 1, capacity)
    arrived = [arrived[:, h].reshape(slots) for h in range(levels - 1)]
    gathers = []
    for h in range(levels - 1):
        wanted = (arrived[h][:, None] * half_block + lax.iota(jnp.int32, half_block)[None, :]).reshape(
            slots * half_block
        )
        rows = lax.iota(jnp.int32, local_rows * half_block)
        gathers.append((rows[:, None] == wanted[None, :]).astype(BF16))

    for h in range(1, levels - 1):
        for c in halves:
            lower[c][h], out = call(
                functools.partial(middle_kernel, c),
                "middle",
                [sources[h]],
                [inbound[c], gathers[h - 1], diags[h], right_sides[h], off_diagonal[h]],
                [vector, payload],
                [update_table],
                flops,
            )
            inbound[c] = exchange(out)
    top = levels - 1
    for c in halves:
        answer[c][top], out = call(
            functools.partial(top_kernel, c),
            "top",
            [arrived[top - 1]],
            [inbound[c], gathers[top - 1], diags[top], right_sides[top]],
            [vector, payload],
            [low_scratch, row_table],
            flops,
        )
        inbound[c] = exchange(out)
    for h in range(levels - 2, 0, -1):
        for c in halves:
            answer[c][h], out = call(
                upper_kernel,
                "upper",
                [destinations[h], arrived[h - 1]],
                [inbound[c], diags[h], off_diagonal[h], lower[c][h]],
                [vector, payload],
                [rows_scratch, row_table],
                flops,
            )
            inbound[c] = exchange(out)
    for c in halves:
        (answer[c][0],) = call(
            last_kernel,
            "last",
            [destinations[0]],
            [inbound[c], diags[0], off_diagonal[0], lower[c][0]],
            [vector],
            [rows_scratch],
            flops,
        )
    low = lax.broadcasted_iota(jnp.int32, (nodes, order, lanes), 2) < lanes // 2
    return jnp.stack([jnp.where(low, answer[0][h], answer[1][h]) for h in range(levels)], axis=0)


def solution(mesh):
    in_specs = (
        P(None, "snode", None, "rhs"),
        P(None, "snode", "rhs", None),
        P(None, "snode", None, None),
        P(None, "snode", None),
        P(None, "snode", None),
    )
    out_specs = P(None, "snode", None, "rhs")
    return jax.shard_map(
        on_device, mesh=mesh, in_specs=in_specs, out_specs=out_specs, check_vma=False
    )
```

time: 374 us -> 385 us (1.029)
  the two profiles are of different devices: /device:TPU:11 before, /device:TPU:33 now
where the time goes in v1:
time: 385 us; the launch traced here: 383 us
  waiting for transfers between devices  195 us (51%)
  starting transfers between devices  84.3 us (22%)
  local copies, waits for them, and re-layouts  38.3 us (10%)
  blocking collectives  36 us (9%)
  Pallas kernels  24.7 us (6%)
  other arithmetic  4.19 us (1%)
    all_to_all x9, waiting for transfers between devices, exchange(): return lax.all_to_all(x, 'snode', split_axis=0, concat_axis=0, tiled=True)  195 us
    all_to_all x9, starting transfers between devices, exchange(): return lax.all_to_all(x, 'snode', split_axis=0, concat_axis=0, tiled=True)  84.3 us
    all_gather x3, blocking collectives, on_device(): lax.all_gather(diag_inverse[h], 'rhs', axis=0, tiled=False)  36 us
    unnamed x74, local copies, waits for them, and re-layouts  27.6 us
    pallas_call x10, Pallas kernels, call(): pl.pallas_call(kernel, name=name, out_shape=outs, in_specs=[pl.BlockSpec(...  24.7 us
  transfers between devices with their start and end apart: 9, of which 8 were waited for; matrix products, arithmetic and copies ran while one was open for 2% of the time, Pallas kernels for 6%

profile of v1, /device:TPU:33, one launch (start us, length us, event | category | flops | bytes accessed | tf_op | source)
XLA Modules:
  0.0 383.3 jit_solution(3852191062228731431)
XLA Ops:
  3.7 19.7 %all-to-all-start = ((s32[128,1,4]{2,1,0:T(1,128)}), s32[128,1,4]{2,1,0:T(1,128)}, u32[]{:S(2)}, u32[]{:S(2)}) async-start(s32[128,1,4]{2,1,0:T(1,128)} %copy.17), calls=%async_computation | async-start | bytes 131072 | tf_op jit(solution)/shard_map/all_to_all | solution.py:209
  23.4 1.7 fusion.8
  25.1 11.6 %all_gather.9.diag_ref = f32[4,2,64,256]{3,2,1,0:T(8,128)S(1)} all-gather(f32[1,2,64,256]{3,2,1,0:T(8,128)S(1)} %get-tuple-element.47), channel_id=1, replica_groups=mesh['snode'=128,'rhs'=4] {'rhs'}, dimensions={0}, use_global_device_ids=true | all-gather | bytes 655360 | tf_op jit(solution)/shard_map/all_gather | solution.py:211
  36.8 1.9 slice_bitcast_fusion
  39.5 2.1 first.3
  43.8 17.8 %all-to-all-start.5 = ((bf16[256,8,128]{2,1,0:T(8,128)(2,1)}), bf16[256,8,128]{2,1,0:T(8,128)(2,1)S(1)}, u32[]{:S(2)}, u32[]{:S(2)}) async-start(bf16[256,8,128]{2,1,0:T(8,128)(2,1)} %copy-done.20), calls=%async_computation.5 | async-start | bytes 1048576 | tf_op jit(solution)/shard_map/all_to_all | solution.py:209
  61.6 0.9 copy-done.27
  62.5 2.1 first.2
  66.1 29.2 %all-to-all-done.5.inbound_ref = bf16[256,8,128]{2,1,0:T(8,128)(2,1)S(1)} async-done(((bf16[256,8,128]{2,1,0:T(8,128)(2,1)}), bf16[256,8,128]{2,1,0:T(8,128)(2,1)S(1)}, u32[]{:S(2)}, u32[]{:S(2)}) %all-to-all-start.5) | async-done | bytes 524320 | tf_op jit(solution)/shard_map/all_to_all | solution.py:209
  95.3 6.7 %all-to-all-start.1 = ((bf16[256,8,128]{2,1,0:T(8,128)(2,1)}), bf16[256,8,128]{2,1,0:T(8,128)(2,1)}, u32[]{:S(2)}, u32[]{:S(2)}) async-start(bf16[256,8,128]{2,1,0:T(8,128)(2,1)} %copy-done.9), calls=%async_computation.1 | async-start | bytes 1048576 | tf_op jit(solution)/shard_map/all_to_all | solution.py:209
  101.9 13.5 %all_gather.10.diag_ref = f32[4,2,64,256]{3,2,1,0:T(8,128)} all-gather(f32[1,2,64,256]{3,2,1,0:T(8,128)} %get-tuple-element.48), channel_id=1, replica_groups=mesh['snode'=128,'rhs'=4] {'rhs'}, dimensions={0}, use_global_device_ids=true | all-gather | bytes 655360 | tf_op jit(solution)/shard_map/all_gather | solution.py:211
  119.0 1.0 copy-done
  120.0 1.0 copy-done.6
  121.0 2.4 middle.3
  124.9 10.4 %all-to-all-done.1.inbound_ref = bf16[256,8,128]{2,1,0:T(8,128)(2,1)} async-done(((bf16[256,8,128]{2,1,0:T(8,128)(2,1)}), bf16[256,8,128]{2,1,0:T(8,128)(2,1)}, u32[]{:S(2)}, u32[]{:S(2)}) %all-to-all-start.1) | async-done | bytes 524320 | tf_op jit(solution)/shard_map/all_to_all | solution.py:209
  135.3 7.9 %all-to-all-start.6 = ((bf16[256,8,128]{2,1,0:T(8,128)(2,1)}), bf16[256,8,128]{2,1,0:T(8,128)(2,1)}, u32[]{:S(2)}, u32[]{:S(2)}) async-start(bf16[256,8,128]{2,1,0:T(8,128)(2,1)} %copy-done.19), calls=%async_computation.6 | async-start | bytes 1048576 | tf_op jit(solution)/shard_map/all_to_all | solution.py:209
  143.3 1.0 copy-done.1
  144.3 2.9 middle.2
  148.7 27.9 %all-to-all-done.6.inbound_ref = bf16[256,8,128]{2,1,0:T(8,128)(2,1)} async-done(((bf16[256,8,128]{2,1,0:T(8,128)(2,1)}), bf16[256,8,128]{2,1,0:T(8,128)(2,1)}, u32[]{:S(2)}, u32[]{:S(2)}) %all-to-all-start.6) | async-done | bytes 524320 | tf_op jit(solution)/shard_map/all_to_all | solution.py:209
  176.6 6.2 %all-to-all-start.2 = ((bf16[256,8,128]{2,1,0:T(8,128)(2,1)}), bf16[256,8,128]{2,1,0:T(8,128)(2,1)S(1)}, u32[]{:S(2)}, u32[]{:S(2)}) async-start(bf16[256,8,128]{2,1,0:T(8,128)(2,1)} %copy-done.12), calls=%async_computation.2 | async-start | bytes 1048576 | tf_op jit(solution)/shard_map/all_to_all | solution.py:209
  182.8 10.8 %all_gather.11.diag_ref = f32[4,2,64,256]{3,2,1,0:T(8,128)S(1)} all-gather(f32[1,2,64,256]{3,2,1,0:T(8,128)S(1)} %get-tuple-element.46), channel_id=1, replica_groups=mesh['snode'=128,'rhs'=4] {'rhs'}, dimensions={0}, use_global_device_ids=true | all-gather | bytes 655360 | tf_op jit(solution)/shard_map/all_gather | solution.py:211
  194.9 0.9 copy-done.24
  195.8 3.0 top.3
  198.9 1.0 copy-done.7
  200.7 15.8 %all-to-all-done.2.inbound_ref = bf16[256,8,128]{2,1,0:T(8,128)(2,1)S(1)} async-done(((bf16[256,8,128]{2,1,0:T(8,128)(2,1)}), bf16[256,8,128]{2,1,0:T(8,128)(2,1)S(1)}, u32[]{:S(2)}, u32[]{:S(2)}) %all-to-all-start.2) | async-done | bytes 524320 | tf_op jit(solution)/shard_map/all_to_all | solution.py:209
  217.3 6.8 %all-to-all-start.7 = ((bf16[256,8,128]{2,1,0:T(8,128)(2,1)}), bf16[256,8,128]{2,1,0:T(8,128)(2,1)}, u32[]{:S(2)}, u32[]{:S(2)}) async-start(bf16[256,8,128]{2,1,0:T(8,128)(2,1)} %copy-done.18), calls=%async_computation.7 | async-start | bytes 1048576 | tf_op jit(solution)/shard_map/all_to_all | solution.py:209
  224.1 1.2 copy-done.8
  225.3 1.0 copy-done.11
  226.4 0.9 copy-done.25
  227.3 2.5 top.2
  231.4 26.1 %all-to-all-done.7.inbound_ref = bf16[256,8,128]{2,1,0:T(8,128)(2,1)} async-done(((bf16[256,8,128]{2,1,0:T(8,128)(2,1)}), bf16[256,8,128]{2,1,0:T(8,128)(2,1)}, u32[]{:S(2)}, u32[]{:S(2)}) %all-to-all-start.7) | async-done | bytes 524320 | tf_op jit(solution)/shard_map/all_to_all | solution.py:209
  257.5 6.2 %all-to-all-start.3 = ((bf16[256,8,128]{2,1,0:T(8,128)(2,1)}), bf16[256,8,128]{2,1,0:T(8,128)(2,1)S(1)}, u32[]{:S(2)}, u32[]{:S(2)}) async-start(bf16[256,8,128]{2,1,0:T(8,128)(2,1)} %copy-done.16), calls=%async_computation.3 | async-start | bytes 1048576 | tf_op jit(solution)/shard_map/all_to_all | solution.py:209
  263.7 0.9 copy-done.35
  264.6 2.9 upper.3
  269.0 28.4 %all-to-all-done.3.inbound_ref = bf16[256,8,128]{2,1,0:T(8,128)(2,1)S(1)} async-done(((bf16[256,8,128]{2,1,0:T(8,128)(2,1)}), bf16[256,8,128]{2,1,0:T(8,128)(2,1)S(1)}, u32[]{:S(2)}, u32[]{:S(2)}) %all-to-all-start.3) | async-done | bytes 524320 | tf_op jit(solution)/shard_map/all_to_all | solution.py:209
  298.2 6.8 %all-to-all-start.8 = ((bf16[256,8,128]{2,1,0:T(8,128)(2,1)}), bf16[256,8,128]{2,1,0:T(8,128)(2,1)}, u32[]{:S(2)}, u32[]{:S(2)}) async-start(bf16[256,8,128]{2,1,0:T(8,128)(2,1)} %copy-done.15), calls=%async_computation.8 | async-start | bytes 1048576 | tf_op jit(solution)/shard_map/all_to_all | solution.py:209
  305.0 1.0 copy-done.14
  306.0 0.9 copy-done.33
  307.0 2.4 upper.2
  310.9 27.5 %all-to-all-done.8.inbound_ref = bf16[256,8,128]{2,1,0:T(8,128)(2,1)} async-done(((bf16[256,8,128]{2,1,0:T(8,128)(2,1)}), bf16[256,8,128]{2,1,0:T(8,128)(2,1)}, u32[]{:S(2)}, u32[]{:S(2)}) %all-to-all-start.8) | async-done | bytes 524320 | tf_op jit(solution)/shard_map/all_to_all | solution.py:209
  338.3 6.2 %all-to-all-start.4 = ((bf16[256,8,128]{2,1,0:T(8,128)(2,1)}), bf16[256,8,128]{2,1,0:T(8,128)(2,1)S(1)}, u32[]{:S(2)}, u32[]{:S(2)}) async-start(bf16[256,8,128]{2,1,0:T(8,128)(2,1)} %copy-done.17), calls=%async_computation.4 | async-start | bytes 1048576 | tf_op jit(solution)/shard_map/all_to_all | solution.py:209
  344.6 0.9 copy-done.29
  345.5 2.5 last.3
  348.0 30.3 %all-to-all-done.4.inbound_ref = bf16[256,8,128]{2,1,0:T(8,128)(2,1)S(1)} async-done(((bf16[256,8,128]{2,1,0:T(8,128)(2,1)}), bf16[256,8,128]{2,1,0:T(8,128)(2,1)S(1)}, u32[]{:S(2)}, u32[]{:S(2)}) %all-to-all-start.4) | async-done | bytes 524320 | tf_op jit(solution)/shard_map/all_to_all | solution.py:209
  378.3 0.9 copy-done.31
  379.2 1.9 last.2
  381.2 1.2 select_bitcast_fusion.2
  382.4 0.9 pad_maximum_fusion
  (97 shorter events, 22.7 us)
Async XLA Ops:
  3.7 40.1 %all-to-all-start = ((s32[128,1,4]{2,1,0:T(1,128)}), s32[128,1,4]{2,1,0:T(1,128)}, u32[]{:S(2)}, u32[]{:S(2)}) async-start(s32[128,1,4]{2,1,0:T(1,128)} %copy.17), calls=%async_computation | async-start | bytes 131072 | tf_op jit(solution)/shard_map/all_to_all | solution.py:209
  36.8 24.8 %copy-start.3 = (f32[4,2,64,256]{3,2,1,0:T(8,128)}, f32[4,2,64,256]{3,2,1,0:T(8,128)S(1)}, u32[]{:S(2)}) copy-start(f32[4,2,64,256]{3,2,1,0:T(8,128)S(1)} %all_gather.9.diag_ref) | copy-start | bytes 1572868
  36.8 2.0 copy-start.36
  41.6 0.8 copy-start.20
  42.4 0.7 copy-start.26
  43.1 0.7 copy-start.28
  43.8 51.5 %all-to-all-start.5 = ((bf16[256,8,128]{2,1,0:T(8,128)(2,1)}), bf16[256,8,128]{2,1,0:T(8,128)(2,1)S(1)}, u32[]{:S(2)}, u32[]{:S(2)}) async-start(bf16[256,8,128]{2,1,0:T(8,128)(2,1)} %copy-done.20), calls=%async_computation.5 | async-start | bytes 1048576 | tf_op jit(solution)/shard_map/all_to_all | solution.py:209
  61.6 1.0 copy-start.27
  64.6 0.8 copy-start.9
  65.4 0.7 copy-start.30
  95.3 22.0 %copy-start.5 = (bf16[256,8,128]{2,1,0:T(8,128)(2,1)}, bf16[256,8,128]{2,1,0:T(8,128)(2,1)S(1)}, u32[]{:S(2)}) copy-start(bf16[256,8,128]{2,1,0:T(8,128)(2,1)S(1)} %all-to-all-done.5.inbound_ref) | copy-start | bytes 1572868
  95.3 40.0 %all-to-all-start.1 = ((bf16[256,8,128]{2,1,0:T(8,128)(2,1)}), bf16[256,8,128]{2,1,0:T(8,128)(2,1)}, u32[]{:S(2)}, u32[]{:S(2)}) async-start(bf16[256,8,128]{2,1,0:T(8,128)(2,1)} %copy-done.9), calls=%async_computation.1 | async-start | bytes 1048576 | tf_op jit(solution)/shard_map/all_to_all | solution.py:209
  118.9 1.0 copy-start
  120.0 1.0 copy-start.6
  123.4 0.8 copy-start.19
  124.2 0.7 copy-start.34
  135.3 41.3 %all-to-all-start.6 = ((bf16[256,8,128]{2,1,0:T(8,128)(2,1)}), bf16[256,8,128]{2,1,0:T(8,128)(2,1)}, u32[]{:S(2)}, u32[]{:S(2)}) async-start(bf16[256,8,128]{2,1,0:T(8,128)(2,1)} %copy-done.19), calls=%async_computation.6 | async-start | bytes 1048576 | tf_op jit(solution)/shard_map/all_to_all | solution.py:209
  143.2 1.0 copy-start.1
  147.2 0.8 copy-start.12
  148.0 0.7 copy-start.32
  176.6 39.9 %all-to-all-start.2 = ((bf16[256,8,128]{2,1,0:T(8,128)(2,1)}), bf16[256,8,128]{2,1,0:T(8,128)(2,1)S(1)}, u32[]{:S(2)}, u32[]{:S(2)}) async-start(bf16[256,8,128]{2,1,0:T(8,128)(2,1)} %copy-done.12), calls=%async_computation.2 | async-start | bytes 1048576 | tf_op jit(solution)/shard_map/all_to_all | solution.py:209
  194.9 1.0 copy-start.24
  198.9 1.0 copy-start.7
  199.9 0.8 copy-start.18
  216.5 0.8 copy-start.10
  217.3 46.4 %copy-start.2 = (f32[4,2,64,256]{3,2,1,0:T(8,128)S(1)}, f32[4,2,64,256]{3,2,1,0:T(8,128)}, u32[]{:S(2)}) copy-start(f32[4,2,64,256]{3,2,1,0:T(8,128)} %all_gather.10.diag_ref) | copy-start | bytes 1572868
  217.3 40.2 %all-to-all-start.7 = ((bf16[256,8,128]{2,1,0:T(8,128)(2,1)}), bf16[256,8,128]{2,1,0:T(8,128)(2,1)}, u32[]{:S(2)}, u32[]{:S(2)}) async-start(bf16[256,8,128]{2,1,0:T(8,128)(2,1)} %copy-done.18), calls=%async_computation.7 | async-start | bytes 1048576 | tf_op jit(solution)/shard_map/all_to_all | solution.py:209
  224.1 1.2 copy-start.8
  225.3 1.0 copy-start.11
  226.4 0.9 copy-start.25
  229.9 0.8 copy-start.16
  230.7 0.7 copy-start.21
  257.5 39.9 %all-to-all-start.3 = ((bf16[256,8,128]{2,1,0:T(8,128)(2,1)}), bf16[256,8,128]{2,1,0:T(8,128)(2,1)S(1)}, u32[]{:S(2)}, u32[]{:S(2)}) async-start(bf16[256,8,128]{2,1,0:T(8,128)(2,1)} %copy-done.16), calls=%async_computation.3 | async-start | bytes 1048576 | tf_op jit(solution)/shard_map/all_to_all | solution.py:209
  263.7 1.0 copy-start.35
  267.5 0.8 copy-start.15
  268.3 0.7 copy-start.22
  297.4 0.8 copy-start.13
  298.2 46.4 %copy-start.4 = (f32[4,2,64,256]{3,2,1,0:T(8,128)S(1)}, f32[4,2,64,256]{3,2,1,0:T(8,128)}, u32[]{:S(2)}) copy-start(f32[4,2,64,256]{3,2,1,0:T(8,128)} %copy-done.3) | copy-start | bytes 1572868
  298.2 40.2 %all-to-all-start.8 = ((bf16[256,8,128]{2,1,0:T(8,128)(2,1)}), bf16[256,8,128]{2,1,0:T(8,128)(2,1)}, u32[]{:S(2)}, u32[]{:S(2)}) async-start(bf16[256,8,128]{2,1,0:T(8,128)(2,1)} %copy-done.15), calls=%async_computation.8 | async-start | bytes 1048576 | tf_op jit(solution)/shard_map/all_to_all | solution.py:209
  305.0 1.0 copy-start.14
  306.0 0.9 copy-start.33
  309.4 0.8 copy-start.17
  310.2 0.7 copy-start.23
  338.3 39.9 %all-to-all-start.4 = ((bf16[256,8,128]{2,1,0:T(8,128)(2,1)}), bf16[256,8,128]{2,1,0:T(8,128)(2,1)S(1)}, u32[]{:S(2)}, u32[]{:S(2)}) async-start(bf16[256,8,128]{2,1,0:T(8,128)(2,1)} %copy-done.17), calls=%async_computation.4 | async-start | bytes 1048576 | tf_op jit(solution)/shard_map/all_to_all | solution.py:209
  344.6 1.0 copy-start.29
  378.3 1.0 copy-start.31

commit v2 on v1

v2 whole, which is shorter than its diff:
```python
import functools

import jax
import jax.numpy as jnp
from jax import lax
from jax.experimental import pallas as pl
from jax.experimental.pallas import tpu as pltpu
from jax.sharding import PartitionSpec as P

BR = 16
HALF = BR // 2
F32 = jnp.float32
BF16 = jnp.bfloat16
PRECISE = lax.Precision.HIGHEST


def whole_diag(diag_ref, s):
    parts = [diag_ref[y, s] for y in range(diag_ref.shape[0])]
    return jnp.concatenate(parts, axis=0)


def solve(diag, x):
    return lax.dot_general(
        diag, x, (((1,), (0,)), ((), ())), precision=PRECISE, preferred_element_type=F32
    )


def solve_transposed(diag, x):
    return lax.dot_general(
        diag, x, (((0,), (0,)), ((), ())), precision=PRECISE, preferred_element_type=F32
    )


def place(table_ref, index_ref, out_ref):
    def body(i, _):
        out_ref[i] = table_ref[index_ref[i]]
        return 0

    lax.fori_loop(0, out_ref.shape[0], body, 0, unroll=8)


def send_updates(low_ref, off_ref, source_ref, out_ref, table_ref):
    nodes, rows, _ = off_ref.shape
    lanes = low_ref.shape[2]
    per_node = rows // BR
    for s in range(nodes):
        update = jnp.dot(off_ref[s], low_ref[s].astype(BF16), preferred_element_type=F32)
        table_ref[pl.ds(s * per_node, per_node)] = update.astype(BF16).reshape(per_node, BR, lanes)
    table_ref[nodes * per_node] = jnp.zeros((BR, lanes), BF16)
    place(table_ref, source_ref, out_ref)


def send_rows(solved, code_ref, out_ref, table_ref):
    blocks, _, lanes = table_ref.shape
    per_node = (blocks - 1) // len(solved)
    for s, values in enumerate(solved):
        table_ref[pl.ds(s * per_node, per_node)] = values.astype(BF16).reshape(per_node, BR, lanes)
    table_ref[blocks - 1] = jnp.zeros((BR, lanes), BF16)
    place(table_ref, code_ref, out_ref)


def summed_updates(inbound_ref, gather_ref):
    slots, _, lanes = inbound_ref.shape
    blocks = inbound_ref[...].astype(F32).reshape(slots, 2, HALF, lanes)
    sums = []
    for part in range(2):
        rows = blocks[:, part].reshape(slots * HALF, lanes).astype(BF16)
        sums.append(jnp.dot(gather_ref[...], rows, preferred_element_type=F32))
    return sums


def lower_solve(inbound_ref, gather_ref, diag_ref, rhs_ref, get_rhs):
    nodes, order, lanes = rhs_ref.shape
    sums = summed_updates(inbound_ref, gather_ref)
    get_rhs.wait()
    part = order // 2
    solved = []
    for s in range(nodes):
        pieces = [x[s * part : (s + 1) * part].reshape(order // BR, HALF, lanes) for x in sums]
        total = jnp.stack(pieces, axis=1).reshape(order, lanes)
        solved.append(solve(whole_diag(diag_ref, s), rhs_ref[s] - total))
    return solved


def fetch(h, pairs, sems):
    copies = [
        pltpu.make_async_copy(array.at[h], buffer, sems.at[i])
        for i, (array, buffer) in enumerate(pairs)
    ]
    for copy in copies:
        copy.start()
    return copies


def store_in_place(h, sol_ref, answer_ref, sem):
    copy = pltpu.make_async_copy(sol_ref, answer_ref.at[h], sem)
    copy.start()
    return copy


def first_kernel(
    source_ref, diag_ref, rhs_hbm, off_hbm, low_ref, out_ref, rhs_ref, off_ref, table_ref, sems
):
    get_rhs, get_off = fetch(0, [(rhs_hbm, rhs_ref), (off_hbm, off_ref)], sems)
    get_rhs.wait()
    for s in range(rhs_ref.shape[0]):
        low_ref[s] = solve(whole_diag(diag_ref, s), rhs_ref[s])
    get_off.wait()
    send_updates(low_ref, off_ref, source_ref, out_ref, table_ref)


def middle_kernel(
    h,
    source_ref,
    inbound_ref,
    gather_ref,
    diag_ref,
    rhs_hbm,
    off_hbm,
    low_ref,
    out_ref,
    rhs_ref,
    off_ref,
    table_ref,
    sems,
):
    get_rhs, get_off = fetch(h, [(rhs_hbm, rhs_ref), (off_hbm, off_ref)], sems)
    for s, solved in enumerate(lower_solve(inbound_ref, gather_ref, diag_ref, rhs_ref, get_rhs)):
        low_ref[s] = solved
    get_off.wait()
    send_updates(low_ref, off_ref, source_ref, out_ref, table_ref)


def top_kernel(
    h,
    code_ref,
    inbound_ref,
    gather_ref,
    diag_ref,
    rhs_hbm,
    answer_ref,
    out_ref,
    rhs_ref,
    sol_ref,
    table_ref,
    sems,
):
    (get_rhs,) = fetch(h, [(rhs_hbm, rhs_ref)], sems)
    solved = lower_solve(inbound_ref, gather_ref, diag_ref, rhs_ref, get_rhs)
    for s, lower in enumerate(solved):
        solved[s] = solve_transposed(whole_diag(diag_ref, s), lower)
        sol_ref[s] = solved[s]
    stored = store_in_place(h, sol_ref, answer_ref, sems.at[1])
    send_rows(solved, code_ref, out_ref, table_ref)
    stored.wait()


def upper_solve(
    dest_ref, inbound_ref, diag_ref, off_ref, low_ref, sol_ref, rows_ref, get_off
):
    nodes, rows, _ = off_ref.shape
    per_node = rows // BR
    lanes = low_ref.shape[2]

    def body(k, _):
        rows_ref[k] = inbound_ref[dest_ref[k]]
        return 0

    lax.fori_loop(0, nodes * per_node, body, 0, unroll=8)
    get_off.wait()
    solved = []
    for s in range(nodes):
        block_rows = rows_ref[pl.ds(s * per_node, per_node)].reshape(rows, lanes)
        taken = lax.dot_general(
            off_ref[s], block_rows, (((0,), (0,)), ((), ())), preferred_element_type=F32
        )
        solved.append(solve_transposed(whole_diag(diag_ref, s), low_ref[s] - taken))
        sol_ref[s] = solved[s]
    return solved


def upper_kernel(
    h,
    dest_ref,
    code_ref,
    inbound_ref,
    diag_ref,
    off_hbm,
    low_ref,
    _,
    answer_ref,
    out_ref,
    off_ref,
    sol_ref,
    rows_ref,
    table_ref,
    sems,
):
    (get_off,) = fetch(h, [(off_hbm, off_ref)], sems)
    solved = upper_solve(
        dest_ref, inbound_ref, diag_ref, off_ref, low_ref, sol_ref, rows_ref, get_off
    )
    stored = store_in_place(h, sol_ref, answer_ref, sems.at[1])
    send_rows(solved, code_ref, out_ref, table_ref)
    stored.wait()


def last_kernel(
    dest_ref, inbound_ref, diag_ref, off_hbm, low_ref, _, answer_ref, off_ref, sol_ref, rows_ref, sems
):
    (get_off,) = fetch(0, [(off_hbm, off_ref)], sems)
    upper_solve(dest_ref, inbound_ref, diag_ref, off_ref, low_ref, sol_ref, rows_ref, get_off)
    store_in_place(0, sol_ref, answer_ref, sems.at[1]).wait()


def scalar(x):
    return x, pl.BlockSpec(memory_space=pltpu.SMEM)


def whole(x):
    return x, pl.BlockSpec(memory_space=pltpu.VMEM)


def in_place(x):
    return x, pl.BlockSpec(memory_space=pl.ANY)


def call(kernel, name, operands, outs, scratch, flops, aliases={}):
    arrays = [x for x, _ in operands]
    moved = sum(x.size * x.dtype.itemsize for x, _ in operands + outs)
    return pl.pallas_call(
        kernel,
        name=name,
        out_shape=[jax.ShapeDtypeStruct(x.shape, x.dtype) for x, _ in outs],
        in_specs=[spec for _, spec in operands],
        out_specs=[spec for _, spec in outs],
        scratch_shapes=scratch,
        input_output_aliases=aliases,
        compiler_params=pltpu.CompilerParams(vmem_limit_bytes=24 << 20),
        cost_estimate=pl.CostEstimate(flops=flops, bytes_accessed=moved, transcendentals=0),
    )(*arrays)


def on_device(right_sides, diag_inverse, off_diagonal, target_snode, target_block):
    levels, nodes, order, lanes = right_sides.shape
    per_node = target_snode.shape[2]
    row_blocks = order // BR
    devices = lax.axis_size("snode")
    outgoing = nodes * per_node
    capacity = 2 * outgoing // devices
    slots = devices * capacity
    local_rows = nodes * row_blocks
    me = lax.axis_index("snode")

    diags = [lax.all_gather(diag_inverse[h], "rhs", axis=0, tiled=False) for h in range(levels)]

    block_order = lax.iota(jnp.int32, outgoing)
    slot_ids = lax.iota(jnp.int32, slots)
    sources, destinations, sent = [], [], []
    for h in range(levels - 1):
        flat_target = target_snode[h].reshape(outgoing)
        owner = flat_target // nodes
        row = flat_target % nodes * row_blocks + target_block[h].reshape(outgoing)
        earlier = (owner[:, None] == owner[None, :]) & (block_order[None, :] < block_order[:, None])
        destination = owner * capacity + jnp.sum(earlier.astype(jnp.int32), axis=1)
        placed = destination[None, :] == slot_ids[:, None]
        sources.append(jnp.min(jnp.where(placed, block_order[None, :], outgoing), axis=1))
        destinations.append(destination)
        sent.append(destination * local_rows + row)

    def exchange(x):
        return lax.all_to_all(x, "snode", split_axis=0, concat_axis=0, tiled=True)

    vector = jax.ShapeDtypeStruct((nodes, order, lanes), F32)
    payload = whole(jax.ShapeDtypeStruct((slots, BR, lanes), BF16))
    table = pltpu.VMEM((outgoing + 1, BR, lanes), BF16)
    row_table = pltpu.VMEM((local_rows + 1, BR, lanes), BF16)
    rows_scratch = pltpu.VMEM((outgoing, BR, lanes), BF16)
    flops = 40 * nodes * order * order * lanes

    rhs_buffer = pltpu.VMEM(vector.shape, F32)
    off_buffer = pltpu.VMEM(off_diagonal.shape[1:], BF16)
    sems = pltpu.SemaphoreType.DMA((2,))

    lower = [None] * (levels - 1)
    lower[0], out = call(
        first_kernel,
        "first",
        [scalar(sources[0]), whole(diags[0]), in_place(right_sides), in_place(off_diagonal)],
        [whole(vector), payload],
        [rhs_buffer, off_buffer, table, sems],
        flops,
    )
    inbound = exchange(out)

    everyone = lax.all_gather(jnp.stack(sent), "snode", axis=0, tiled=False)
    arrived, gathers = [], []
    for h in range(levels - 1):
        slot = everyone[:, h] // local_rows
        row = everyone[:, h] % local_rows
        found = [
            jnp.min(jnp.where(slot == me * capacity + i, row, local_rows), axis=1)
            for i in range(capacity)
        ]
        code = jnp.stack(found, axis=1).reshape(slots)
        arrived.append(code)
        wanted = (code[:, None] * HALF + lax.iota(jnp.int32, HALF)[None, :]).reshape(slots * HALF)
        rows = lax.iota(jnp.int32, local_rows * HALF)
        gathers.append((rows[:, None] == wanted[None, :]).astype(BF16))

    for h in range(1, levels - 1):
        lower[h], out = call(
            functools.partial(middle_kernel, h),
            "middle",
            [scalar(sources[h]), whole(inbound), whole(gathers[h - 1]), whole(diags[h])]
            + [in_place(right_sides), in_place(off_diagonal)],
            [whole(vector), payload],
            [rhs_buffer, off_buffer, table, sems],
            flops,
        )
        inbound = exchange(out)
    top = levels - 1
    answer = jax.ShapeDtypeStruct(right_sides.shape, F32)
    answer, out = call(
        functools.partial(top_kernel, top),
        "top",
        [scalar(arrived[top - 1]), whole(inbound), whole(gathers[top - 1]), whole(diags[top])]
        + [in_place(right_sides)],
        [in_place(answer), payload],
        [rhs_buffer, rhs_buffer, row_table, sems],
        flops,
    )
    inbound = exchange(out)
    for h in range(levels - 2, 0, -1):
        answer, out = call(
            functools.partial(upper_kernel, h),
            "upper",
            [scalar(destinations[h]), scalar(arrived[h - 1]), whole(inbound), whole(diags[h])]
            + [in_place(off_diagonal), whole(lower[h]), in_place(answer)],
            [in_place(answer), payload],
            [off_buffer, rhs_buffer, rows_scratch, row_table, sems],
            flops,
            {6: 0},
        )
        inbound = exchange(out)
    (answer,) = call(
        last_kernel,
        "last",
        [scalar(destinations[0]), whole(inbound), whole(diags[0])]
        + [in_place(off_diagonal), whole(lower[0]), in_place(answer)],
        [in_place(answer)],
        [off_buffer, rhs_buffer, rows_scratch, sems],
        flops,
        {5: 0},
    )
    return answer


def solution(mesh):
    in_specs = (
        P(None, "snode", None, "rhs"),
        P(None, "snode", "rhs", None),
        P(None, "snode", None, None),
        P(None, "snode", None),
        P(None, "snode", None),
    )
    out_specs = P(None, "snode", None, "rhs")
    return jax.shard_map(
        on_device, mesh=mesh, in_specs=in_specs, out_specs=out_specs, check_vma=False
    )
```

time: 385 us -> 401 us (1.042)
  blocking collectives: 36 us -> 277 us
  waiting for transfers between devices: 195 us -> 37 us
  starting transfers between devices: 84.3 us -> 38.6 us
  local copies, waits for them, and re-layouts: 38.3 us -> 22.6 us
  Pallas kernels: 24.7 us -> 14.7 us
  other arithmetic: 4.19 us -> 10.1 us
    all_to_all x9 -> x2, waiting for transfers between devices: 195 us -> 37 us  [exchange(): return lax.all_to_all(x, 'snode', split_axis=0, concat_axis=0, tiled=True)]
    all_to_all x0 -> x2, blocking collectives: none -> 124 us  [exchange(): return lax.all_to_all(x, 'snode', split_axis=0, concat_axis=0, tiled=True)]
    all_gather x0 -> x1, blocking collectives: none -> 116 us  [on_device(): everyone = lax.all_gather(jnp.stack(sent), 'snode', axis=0, tiled=False)]
    all_to_all x9 -> x2, starting transfers between devices: 84.3 us -> 38.6 us  [exchange(): return lax.all_to_all(x, 'snode', split_axis=0, concat_axis=0, tiled=True)]
    unnamed x74 -> x34, local copies, waits for them, and re-layouts: 27.6 us -> 10.8 us
    pallas_call x10 -> x5, Pallas kernels: 24.7 us -> 14.7 us  [call(): pl.pallas_call(kernel, name=name, out_shape=[jax.ShapeDtypeStruct(x.shape...]
  transfers between devices with their start and end apart: 9 -> 2, of which waited for: 8 -> 1; matrix products, arithmetic and copies ran while one was open for 2% -> 5% of each run, Pallas kernels for 6% -> 0%
where the time goes in v2:
time: 401 us; the launch traced here: 400 us
  blocking collectives  277 us (69%)
  starting transfers between devices  38.6 us (10%)
  waiting for transfers between devices  37 us (9%)
  local copies, waits for them, and re-layouts  22.6 us (6%)
  Pallas kernels  14.7 us (4%)
  other arithmetic  10.1 us (3%)
    all_to_all x2, blocking collectives, exchange(): return lax.all_to_all(x, 'snode', split_axis=0, concat_axis=0, tiled=True)  124 us
    all_gather x1, blocking collectives, on_device(): everyone = lax.all_gather(jnp.stack(sent), 'snode', axis=0, tiled=False)  116 us
    all_to_all x2, starting transfers between devices, exchange(): return lax.all_to_all(x, 'snode', split_axis=0, concat_axis=0, tiled=True)  38.6 us
    all_to_all x2, waiting for transfers between devices, exchange(): return lax.all_to_all(x, 'snode', split_axis=0, concat_axis=0, tiled=True)  37 us
    all_gather x3, blocking collectives, on_device(): lax.all_gather(diag_inverse[h], 'rhs', axis=0, tiled=False)  36.5 us
    pallas_call x5, Pallas kernels, call(): pl.pallas_call(kernel, name=name, out_shape=[jax.ShapeDtypeStruct(x.shape...  14.7 us
    unnamed x34, local copies, waits for them, and re-layouts  10.8 us
  transfers between devices with their start and end apart: 2, of which 1 were waited for; matrix products, arithmetic and copies ran while one was open for 5% of the time, Pallas kernels for 0%

profile of v2, /device:TPU:33, one launch (start us, length us, event | category | flops | bytes accessed | tf_op | source)
XLA Modules:
  0.0 400.3 jit_solution(3094682119461783721)
XLA Ops:
  0.0 0.7 fusion.19
  0.8 0.2 convert_reduce_fusion.1
  1.1 1.7 fusion.16
  2.8 11.8 %all_gather.17.diag_ref = f32[4,2,64,256]{3,2,1,0:T(8,128)S(1)} all-gather(f32[1,2,64,256]{3,2,1,0:T(8,128)S(1)} %get-tuple-element.26), channel_id=1, replica_groups=mesh['snode'=128,'rhs'=4] {'rhs'}, dimensions={0}, use_global_device_ids=true | all-gather | bytes 655360 | tf_op jit(solution)/shard_map/all_gather | solution.py:255
  14.6 1.6 copy-done
  16.2 1.1 copy-done.2
  17.3 2.1 first.1
  19.5 1.0 copy-done.9
  20.5 0.7 copy-done.11
  21.2 21.5 %all-to-all-start = ((bf16[256,16,128]{2,1,0:T(8,128)(2,1)}), bf16[256,16,128]{2,1,0:T(8,128)(2,1)}, u32[]{:S(2)}, u32[]{:S(2)}) async-start(bf16[256,16,128]{2,1,0:T(8,128)(2,1)} %copy-done.9), calls=%async_computation | async-start | bytes 2097152 | tf_op jit(solution)/shard_map/all_to_all | solution.py:272
  42.7 0.6 reshape_squeeze.18
  43.4 0.7 reshape_squeeze.17
  44.0 0.7 reshape_squeeze.20
  44.8 0.6 reshape_squeeze.21
  45.3 0.7 and_select_fusion.4
  46.0 0.2 convert_reduce_fusion
  46.2 0.6 fusion.10
  46.8 0.7 fusion.13
  47.5 116.4 %all-gather.1 = s32[128,2,128]{2,1,0:T(2,128)S(1)} all-gather(s32[1,2,128]{2,1,0:T(2,128)S(1)} %add_bitcast_fusion), channel_id=2, replica_groups=mesh['snode'=128,'rhs'=4] {'snode'}, dimensions={0}, use_global_device_ids=true | all-gather | bytes 132096 | tf_op jit(solution)/shard_map/all_gather | solution.py:296
  164.1 0.7 select_reduce_fusion.3
  164.8 0.7 copy.15
  165.5 1.0 reshape.392.code_ref
  166.5 0.8 iota_add_fusion.1
  167.3 1.6 add.182
  168.9 0.7 multiply_add_fusion.dest_ref
  169.7 13.2 %all_gather.18.diag_ref = f32[4,2,64,256]{3,2,1,0:T(8,128)} all-gather(f32[1,2,64,256]{3,2,1,0:T(8,128)} %get-tuple-element.27), channel_id=1, replica_groups=mesh['snode'=128,'rhs'=4] {'rhs'}, dimensions={0}, use_global_device_ids=true | all-gather | bytes 655360 | tf_op jit(solution)/shard_map/all_gather | solution.py:255
  182.9 1.9 fusion.gather_ref
  184.8 1.0 copy-done.4
  185.9 1.2 copy-done.7
  187.1 3.5 middle.1
  190.6 1.0 copy-done.10
  191.6 0.7 copy-done.13
  192.4 17.1 %all-to-all-start.1 = ((bf16[256,16,128]{2,1,0:T(8,128)(2,1)}), bf16[256,16,128]{2,1,0:T(8,128)(2,1)}, u32[]{:S(2)}, u32[]{:S(2)}) async-start(bf16[256,16,128]{2,1,0:T(8,128)(2,1)} %copy-done.10), calls=%async_computation.1 | async-start | bytes 2097152 | tf_op jit(solution)/shard_map/all_to_all | solution.py:272
  209.5 0.7 pad_add_fusion.1
  210.1 0.7 copy.17
  210.9 1.0 reshape.393.code_ref
  211.9 0.8 iota_add_fusion
  212.6 1.6 add.186
  214.2 11.5 %all_gather.19.diag_ref = f32[4,2,64,256]{3,2,1,0:T(8,128)} all-gather(f32[1,2,64,256]{3,2,1,0:T(8,128)S(1)} %get-tuple-element.25), channel_id=1, replica_groups=mesh['snode'=128,'rhs'=4] {'rhs'}, dimensions={0}, use_global_device_ids=true | all-gather | bytes 655360 | tf_op jit(solution)/shard_map/all_gather | solution.py:255
  225.8 1.9 fusion.1.gather_ref
  227.7 37.0 %all-to-all-done.1.inbound_ref = bf16[256,16,128]{2,1,0:T(8,128)(2,1)} async-done(((bf16[256,16,128]{2,1,0:T(8,128)(2,1)}), bf16[256,16,128]{2,1,0:T(8,128)(2,1)}, u32[]{:S(2)}, u32[]{:S(2)}) %all-to-all-start.1) | async-done | bytes 1048608 | tf_op jit(solution)/shard_map/all_to_all | solution.py:272
  264.7 1.2 copy-done.6
  265.9 1.0 copy-done.8
  267.0 3.9 top.1
  270.9 62.0 %all_to_all.20.inbound_ref = bf16[256,16,128]{2,1,0:T(8,128)(2,1)S(1)} all-to-all(bf16[256,16,128]{2,1,0:T(8,128)(2,1)S(1)} %get-tuple-element.15), channel_id=1, replica_groups=mesh['snode'=128,'rhs'=4] {'snode'}, dimensions={0} | all-to-all | bytes 2097152 | tf_op jit(solution)/shard_map/all_to_all | solution.py:272
  332.9 2.6 upper.1
  335.6 62.0 %all_to_all.21.inbound_ref = bf16[256,16,128]{2,1,0:T(8,128)(2,1)S(1)} all-to-all(bf16[256,16,128]{2,1,0:T(8,128)(2,1)S(1)} %get-tuple-element.18), channel_id=1, replica_groups=mesh['snode'=128,'rhs'=4] {'snode'}, dimensions={0} | all-to-all | bytes 2097152 | tf_op jit(solution)/shard_map/all_to_all | solution.py:272
  397.6 2.6 last.1
  (37 shorter events, 0.6 us)
Async XLA Ops:
  1.0 1.9 copy-start.16
  14.6 1.6 copy-start
  16.2 1.1 copy-start.2
  17.3 27.4 %copy-start.15 = (s32[2,2,64]{2,1,0:T(2,128)S(1)}, s32[2,2,64]{2,1,0:T(2,128)}, u32[]{:S(2)}) copy-start(s32[2,2,64]{2,1,0:T(2,128)} %param.9) | copy-start | bytes 3076
  19.4 1.0 copy-start.9
  20.5 0.7 copy-start.11
  21.2 163.6 %copy-start.1 = (bf16[2,2,1024,256]{3,2,1,0:T(8,128)(2,1)S(1)}, bf16[2,2,1024,256]{3,2,1,0:T(8,128)(2,1)}, u32[]{:S(2)}) copy-start(bf16[2,2,1024,256]{3,2,1,0:T(8,128)(2,1)} %off_hbm.7) | copy-start | bytes 6291460
  21.2 163.6 %copy-start.3 = (f32[3,2,256,128]{3,2,1,0:T(8,128)S(1)}, f32[3,2,256,128]{3,2,1,0:T(8,128)}, u32[]{:S(2)}) copy-start(f32[3,2,256,128]{3,2,1,0:T(8,128)} %rhs_hbm.5) | copy-start | bytes 2359300
  21.2 163.6 %all-to-all-start = ((bf16[256,16,128]{2,1,0:T(8,128)(2,1)}), bf16[256,16,128]{2,1,0:T(8,128)(2,1)}, u32[]{:S(2)}, u32[]{:S(2)}) async-start(bf16[256,16,128]{2,1,0:T(8,128)(2,1)} %copy-done.9), calls=%async_computation | async-start | bytes 2097152 | tf_op jit(solution)/shard_map/all_to_all | solution.py:272
  184.8 1.0 copy-start.4
  185.9 1.2 copy-start.7
  190.6 1.0 copy-start.10
  191.6 0.7 copy-start.13
  192.4 72.3 %all-to-all-start.1 = ((bf16[256,16,128]{2,1,0:T(8,128)(2,1)}), bf16[256,16,128]{2,1,0:T(8,128)(2,1)}, u32[]{:S(2)}, u32[]{:S(2)}) async-start(bf16[256,16,128]{2,1,0:T(8,128)(2,1)} %copy-done.10), calls=%async_computation.1 | async-start | bytes 2097152 | tf_op jit(solution)/shard_map/all_to_all | solution.py:272
  264.7 1.2 copy-start.6
  265.9 1.0 copy-start.8
  267.0 66.0 %copy-start.5 = (f32[4,2,64,256]{3,2,1,0:T(8,128)S(1)}, f32[4,2,64,256]{3,2,1,0:T(8,128)}, u32[]{:S(2)}) copy-start(f32[4,2,64,256]{3,2,1,0:T(8,128)} %all_gather.18.diag_ref) | copy-start | bytes 1572868
  267.0 66.0 %copy-start.14 = (f32[2,256,128]{2,1,0:T(8,128)S(1)}, f32[2,256,128]{2,1,0:T(8,128)}, u32[]{:S(2)}) copy-start(f32[2,256,128]{2,1,0:T(8,128)} %copy-done.13) | copy-start | bytes 786436
  335.6 62.0 %copy-start.12 = (f32[2,256,128]{2,1,0:T(8,128)S(1)}, f32[2,256,128]{2,1,0:T(8,128)}, u32[]{:S(2)}) copy-start(f32[2,256,128]{2,1,0:T(8,128)} %copy-done.11) | copy-start | bytes 786436

commit v3 on v2

v3 whole, which is shorter than its diff:
```python
import functools

import jax
import jax.numpy as jnp
from jax import lax
from jax.experimental import pallas as pl
from jax.experimental.pallas import tpu as pltpu
from jax.sharding import PartitionSpec as P

BR = 16
HALF = BR // 2
F32 = jnp.float32
BF16 = jnp.bfloat16
PRECISE = lax.Precision.HIGHEST


def whole_diag(diag_ref, s):
    parts = [diag_ref[y, s] for y in range(diag_ref.shape[0])]
    return jnp.concatenate(parts, axis=0)


def solve(diag, x):
    return lax.dot_general(
        diag, x, (((1,), (0,)), ((), ())), precision=PRECISE, preferred_element_type=F32
    )


def solve_transposed(diag, x):
    return lax.dot_general(
        diag, x, (((0,), (0,)), ((), ())), precision=PRECISE, preferred_element_type=F32
    )


def place(table_ref, index_ref, staged_ref, out_ref, sems):
    chunks = sems.shape[0]
    size = out_ref.shape[0] // chunks
    copies = []
    for c in range(chunks):

        def body(i, _):
            staged_ref[i] = table_ref[index_ref[i]]
            return 0

        lax.fori_loop(c * size, (c + 1) * size, body, 0, unroll=8)
        part = pl.ds(c * size, size)
        copies.append(pltpu.make_async_copy(staged_ref.at[part], out_ref.at[part], sems.at[c]))
        copies[-1].start()
    return copies


def send_updates(low_ref, off_ref, source_ref, staged_ref, out_ref, table_ref, sems):
    nodes, rows, _ = off_ref.shape
    lanes = low_ref.shape[2]
    per_node = rows // BR
    for s in range(nodes):
        update = jnp.dot(off_ref[s], low_ref[s].astype(BF16), preferred_element_type=F32)
        table_ref[pl.ds(s * per_node, per_node)] = update.astype(BF16).reshape(per_node, BR, lanes)
    table_ref[nodes * per_node] = jnp.zeros((BR, lanes), BF16)
    return place(table_ref, source_ref, staged_ref, out_ref, sems)


def send_rows(solved, code_ref, staged_ref, out_ref, table_ref, sems):
    blocks, _, lanes = table_ref.shape
    per_node = (blocks - 1) // len(solved)
    for s, values in enumerate(solved):
        table_ref[pl.ds(s * per_node, per_node)] = values.astype(BF16).reshape(per_node, BR, lanes)
    table_ref[blocks - 1] = jnp.zeros((BR, lanes), BF16)
    return place(table_ref, code_ref, staged_ref, out_ref, sems)


def fetch(pairs, sems):
    copies = [pltpu.make_async_copy(a, b, sems.at[i]) for i, (a, b) in enumerate(pairs)]
    for copy in copies:
        copy.start()
    return copies


def store(source, target, sem):
    copy = pltpu.make_async_copy(source, target, sem)
    copy.start()
    return copy


def finish(copies):
    for copy in copies:
        copy.wait()


def summed_updates(inbound_ref, gather_ref):
    slots, _, lanes = inbound_ref.shape
    blocks = inbound_ref[...].astype(F32).reshape(slots, 2, HALF, lanes)
    sums = []
    for part in range(2):
        rows = blocks[:, part].reshape(slots * HALF, lanes).astype(BF16)
        sums.append(jnp.dot(gather_ref[...], rows, preferred_element_type=F32))
    return sums


def lower_solve(inbound_ref, gather_ref, diag_ref, rhs_ref, get_gather, get_others):
    nodes, order, lanes = rhs_ref.shape
    get_gather.wait()
    sums = summed_updates(inbound_ref, gather_ref)
    finish(get_others)
    part = order // 2
    solved = []
    for s in range(nodes):
        pieces = [x[s * part : (s + 1) * part].reshape(order // BR, HALF, lanes) for x in sums]
        total = jnp.stack(pieces, axis=1).reshape(order, lanes)
        solved.append(solve(whole_diag(diag_ref, s), rhs_ref[s] - total))
    return solved


def first_kernel(
    source_ref,
    diag_hbm,
    rhs_hbm,
    off_hbm,
    low_hbm,
    out_hbm,
    diag_ref,
    rhs_ref,
    off_ref,
    low_ref,
    table_ref,
    staged_ref,
    in_sems,
    low_sem,
    out_sems,
):
    pairs = [(diag_hbm, diag_ref), (rhs_hbm.at[0], rhs_ref), (off_hbm.at[0], off_ref)]
    get_diag, get_rhs, get_off = fetch(pairs, in_sems)
    finish([get_diag, get_rhs])
    for s in range(rhs_ref.shape[0]):
        low_ref[s] = solve(whole_diag(diag_ref, s), rhs_ref[s])
    kept = store(low_ref, low_hbm, low_sem.at[0])
    get_off.wait()
    finish(send_updates(low_ref, off_ref, source_ref, staged_ref, out_hbm, table_ref, out_sems))
    kept.wait()


def middle_kernel(
    h,
    source_ref,
    inbound_ref,
    gather_hbm,
    diag_hbm,
    rhs_hbm,
    off_hbm,
    low_hbm,
    out_hbm,
    gather_ref,
    diag_ref,
    rhs_ref,
    off_ref,
    low_ref,
    table_ref,
    staged_ref,
    in_sems,
    low_sem,
    out_sems,
):
    pairs = [(gather_hbm, gather_ref), (diag_hbm, diag_ref)]
    pairs += [(rhs_hbm.at[h], rhs_ref), (off_hbm.at[h], off_ref)]
    get_gather, get_diag, get_rhs, get_off = fetch(pairs, in_sems)
    solved = lower_solve(inbound_ref, gather_ref, diag_ref, rhs_ref, get_gather, [get_diag, get_rhs])
    for s, values in enumerate(solved):
        low_ref[s] = values
    kept = store(low_ref, low_hbm, low_sem.at[0])
    get_off.wait()
    finish(send_updates(low_ref, off_ref, source_ref, staged_ref, out_hbm, table_ref, out_sems))
    kept.wait()


def top_kernel(
    h,
    code_ref,
    inbound_ref,
    gather_hbm,
    diag_hbm,
    rhs_hbm,
    answer_hbm,
    out_hbm,
    gather_ref,
    diag_ref,
    rhs_ref,
    sol_ref,
    table_ref,
    staged_ref,
    in_sems,
    sol_sem,
    out_sems,
):
    pairs = [(gather_hbm, gather_ref), (diag_hbm, diag_ref), (rhs_hbm.at[h], rhs_ref)]
    get_gather, get_diag, get_rhs = fetch(pairs, in_sems)
    solved = lower_solve(inbound_ref, gather_ref, diag_ref, rhs_ref, get_gather, [get_diag, get_rhs])
    for s, lower in enumerate(solved):
        solved[s] = solve_transposed(whole_diag(diag_ref, s), lower)
        sol_ref[s] = solved[s]
    kept = store(sol_ref, answer_hbm.at[h], sol_sem.at[0])
    finish(send_rows(solved, code_ref, staged_ref, out_hbm, table_ref, out_sems))
    kept.wait()


def upper_solve(
    h, dest_ref, inbound_ref, diag_hbm, off_hbm, low_hbm, diag_ref, off_ref, low_ref, sol_ref, rows_ref, sems
):
    pairs = [(off_hbm.at[h], off_ref), (diag_hbm, diag_ref), (low_hbm, low_ref)]
    copies = fetch(pairs, sems)
    nodes, rows, _ = off_ref.shape
    per_node = rows // BR
    lanes = low_ref.shape[2]

    def body(k, _):
        rows_ref[k] = inbound_ref[dest_ref[k]]
        return 0

    lax.fori_loop(0, nodes * per_node, body, 0, unroll=8)
    finish(copies)
    solved = []
    for s in range(nodes):
        block_rows = rows_ref[pl.ds(s * per_node, per_node)].reshape(rows, lanes)
        taken = lax.dot_general(
            off_ref[s], block_rows, (((0,), (0,)), ((), ())), preferred_element_type=F32
        )
        solved.append(solve_transposed(whole_diag(diag_ref, s), low_ref[s] - taken))
        sol_ref[s] = solved[s]
    return solved


def upper_kernel(
    h,
    dest_ref,
    code_ref,
    inbound_ref,
    diag_hbm,
    off_hbm,
    low_hbm,
    _,
    answer_hbm,
    out_hbm,
    diag_ref,
    off_ref,
    low_ref,
    sol_ref,
    rows_ref,
    table_ref,
    staged_ref,
    in_sems,
    sol_sem,
    out_sems,
):
    solved = upper_solve(
        h, dest_ref, inbound_ref, diag_hbm, off_hbm, low_hbm,
        diag_ref, off_ref, low_ref, sol_ref, rows_ref, in_sems,
    )
    kept = store(sol_ref, answer_hbm.at[h], sol_sem.at[0])
    finish(send_rows(solved, code_ref, staged_ref, out_hbm, table_ref, out_sems))
    kept.wait()


def last_kernel(
    dest_ref,
    inbound_ref,
    diag_hbm,
    off_hbm,
    low_hbm,
    _,
    answer_hbm,
    diag_ref,
    off_ref,
    low_ref,
    sol_ref,
    rows_ref,
    in_sems,
    sol_sem,
):
    upper_solve(
        0, dest_ref, inbound_ref, diag_hbm, off_hbm, low_hbm,
        diag_ref, off_ref, low_ref, sol_ref, rows_ref, in_sems,
    )
    store(sol_ref, answer_hbm.at[0], sol_sem.at[0]).wait()


def scalar(x):
    return x, pl.BlockSpec(memory_space=pltpu.SMEM)


def whole(x):
    return x, pl.BlockSpec(memory_space=pltpu.VMEM)


def far(x):
    return x, pl.BlockSpec(memory_space=pltpu.HBM)


def call(kernel, name, operands, outs, scratch, flops, aliases={}):
    arrays = [x for x, _ in operands]
    moved = sum(x.size * x.dtype.itemsize for x, _ in operands + outs)
    return pl.pallas_call(
        kernel,
        name=name,
        out_shape=[jax.ShapeDtypeStruct(x.shape, x.dtype) for x, _ in outs],
        in_specs=[spec for _, spec in operands],
        out_specs=[spec for _, spec in outs],
        scratch_shapes=scratch,
        input_output_aliases=aliases,
        cost_estimate=pl.CostEstimate(flops=flops, bytes_accessed=moved, transcendentals=0),
    )(*arrays)


def ring_groups(devices, inner=8):
    if devices % inner:
        return [[list(range(devices))]]
    near = [list(range(start, start + inner)) for start in range(0, devices, inner)]
    return [near, [list(column) for column in zip(*near)]]


def on_device(right_sides, diag_inverse, off_diagonal, target_snode, target_block):
    levels, nodes, order, lanes = right_sides.shape
    per_node = target_snode.shape[2]
    row_blocks = order // BR
    devices = lax.axis_size("snode")
    outgoing = nodes * per_node
    capacity = 2 * outgoing // devices
    slots = devices * capacity
    local_rows = nodes * row_blocks
    me = lax.axis_index("snode")

    diags = [lax.all_gather(diag_inverse[h], "rhs", axis=0, tiled=False) for h in range(levels)]

    block_order = lax.iota(jnp.int32, outgoing)
    slot_ids = lax.iota(jnp.int32, slots)
    sources, destinations, sent = [], [], []
    for h in range(levels - 1):
        flat_target = target_snode[h].reshape(outgoing)
        owner = flat_target // nodes
        row = flat_target % nodes * row_blocks + target_block[h].reshape(outgoing)
        earlier = (owner[:, None] == owner[None, :]) & (block_order[None, :] < block_order[:, None])
        destination = owner * capacity + jnp.sum(earlier.astype(jnp.int32), axis=1)
        placed = destination[None, :] == slot_ids[:, None]
        sources.append(jnp.min(jnp.where(placed, block_order[None, :], outgoing), axis=1))
        destinations.append(destination)
        sent.append(destination * local_rows + row)

    def exchange(x):
        return lax.all_to_all(x, "snode", split_axis=0, concat_axis=0, tiled=True)

    vector = far(jax.ShapeDtypeStruct((nodes, order, lanes), F32))
    payload = far(jax.ShapeDtypeStruct((slots, BR, lanes), BF16))
    answer = jax.ShapeDtypeStruct(right_sides.shape, F32)
    one = pltpu.SemaphoreType.DMA((1,))
    inputs = pltpu.SemaphoreType.DMA((4,))
    vectors = pltpu.VMEM((nodes, order, lanes), F32)
    off_buffer = pltpu.VMEM(off_diagonal.shape[1:], BF16)
    diag_buffer = pltpu.VMEM(diags[0].shape, F32)
    gather_buffer = pltpu.VMEM((local_rows * HALF, slots * HALF), BF16)
    table = pltpu.VMEM((outgoing + 1, BR, lanes), BF16)
    row_table = pltpu.VMEM((local_rows + 1, BR, lanes), BF16)
    rows_scratch = pltpu.VMEM((outgoing, BR, lanes), BF16)
    send = [pltpu.VMEM((slots, BR, lanes), BF16), inputs, one, pltpu.SemaphoreType.DMA((4,))]
    flops = 40 * nodes * order * order * lanes

    lower = [None] * (levels - 1)
    lower[0], out = call(
        first_kernel,
        "first",
        [scalar(sources[0]), far(diags[0]), far(right_sides), far(off_diagonal)],
        [vector, payload],
        [diag_buffer, vectors, off_buffer, vectors, table] + send,
        flops,
    )
    inbound = exchange(out)

    everyone = jnp.stack(sent)
    for groups in ring_groups(devices):
        everyone = lax.all_gather(everyone, "snode", axis_index_groups=groups, axis=0, tiled=False)
    everyone = everyone.reshape(devices, levels - 1, outgoing)
    arrived, gathers = [], []
    for h in range(levels - 1):
        slot = everyone[:, h] // local_rows
        row = everyone[:, h] % local_rows
        found = [
            jnp.min(jnp.where(slot == me * capacity + i, row, local_rows), axis=1)
            for i in range(capacity)
        ]
        code = jnp.stack(found, axis=1).reshape(slots)
        arrived.append(code)
        wanted = (code[:, None] * HALF + lax.iota(jnp.int32, HALF)[None, :]).reshape(slots * HALF)
        rows = lax.iota(jnp.int32, local_rows * HALF)
        gathers.append((rows[:, None] == wanted[None, :]).astype(BF16))

    for h in range(1, levels - 1):
        lower[h], out = call(
            functools.partial(middle_kernel, h),
            "middle",
            [scalar(sources[h]), whole(inbound), far(gathers[h - 1]), far(diags[h])]
            + [far(right_sides), far(off_diagonal)],
            [vector, payload],
            [gather_buffer, diag_buffer, vectors, off_buffer, vectors, table] + send,
            flops,
        )
        inbound = exchange(out)
    top = levels - 1
    answer, out = call(
        functools.partial(top_kernel, top),
        "top",
        [scalar(arrived[top - 1]), whole(inbound), far(gathers[top - 1]), far(diags[top])]
        + [far(right_sides)],
        [far(answer), payload],
        [gather_buffer, diag_buffer, vectors, vectors, row_table] + send,
        flops,
    )
    inbound = exchange(out)
    for h in range(levels - 2, 0, -1):
        answer, out = call(
            functools.partial(upper_kernel, h),
            "upper",
            [scalar(destinations[h]), scalar(arrived[h - 1]), whole(inbound), far(diags[h])]
            + [far(off_diagonal), far(lower[h]), far(answer)],
            [far(answer), payload],
            [diag_buffer, off_buffer, vectors, vectors, rows_scratch, row_table] + send,
            flops,
            {6: 0},
        )
        inbound = exchange(out)
    (answer,) = call(
        last_kernel,
        "last",
        [scalar(destinations[0]), whole(inbound), far(diags[0])]
        + [far(off_diagonal), far(lower[0]), far(answer)],
        [far(answer)],
        [diag_buffer, off_buffer, vectors, vectors, rows_scratch, inputs, one],
        flops,
        {5: 0},
    )
    return answer


def solution(mesh):
    in_specs = (
        P(None, "snode", None, "rhs"),
        P(None, "snode", "rhs", None),
        P(None, "snode", None, None),
        P(None, "snode", None),
        P(None, "snode", None),
    )
    out_specs = P(None, "snode", None, "rhs")
    return jax.shard_map(
        on_device, mesh=mesh, in_specs=in_specs, out_specs=out_specs, check_vma=False
    )
```

time: 401 us -> 346 us (0.86)
  the two profiles are of different devices: /device:TPU:33 before, /device:TPU:41 now
where the time goes in v3:
time: 346 us; the launch traced here: 345 us
  blocking collectives  221 us (64%)
  starting transfers between devices  47.4 us (14%)
  waiting for transfers between devices  42.6 us (12%)
  Pallas kernels  24.5 us (7%)
  local copies, waits for them, and re-layouts  5.07 us (1%)
  other arithmetic  4.74 us (1%)
    all_to_all x2, blocking collectives, exchange(): return lax.all_to_all(x, 'snode', split_axis=0, concat_axis=0, tiled=True)  124 us
    all_gather x2, blocking collectives, on_device(): lax.all_gather(everyone, 'snode', axis_index_groups=groups, axis=0, tiled...  63.3 us
    all_to_all x2, starting transfers between devices, exchange(): return lax.all_to_all(x, 'snode', split_axis=0, concat_axis=0, tiled=True)  47.4 us
    all_to_all x2, waiting for transfers between devices, exchange(): return lax.all_to_all(x, 'snode', split_axis=0, concat_axis=0, tiled=True)  42.6 us
    all_gather x3, blocking collectives, on_device(): lax.all_gather(diag_inverse[h], 'rhs', axis=0, tiled=False)  33 us
    pallas_call x5, Pallas kernels, call(): pl.pallas_call(kernel, name=name, out_shape=[jax.ShapeDtypeStruct(x.shape...  24.5 us
  transfers between devices with their start and end apart: 2, of which 1 were waited for; matrix products, arithmetic and copies ran while one was open for 1% of the time, Pallas kernels for 0%

profile of v3, /device:TPU:41, one launch (start us, length us, event | category | flops | bytes accessed | tf_op | source)
XLA Modules:
  0.0 345.3 jit_solution(12845873494604053029)
XLA Ops:
  0.0 0.7 fusion.19
  0.7 0.1 reshape_squeeze.16
  0.8 0.2 convert_reduce_fusion.1
  1.0 0.0 copy-start.5
  1.0 0.7 select_reduce_fusion.source_ref
  1.7 1.1 fusion.16
  2.7 10.9 %all_gather.25.diag_hbm = f32[4,2,64,256]{3,2,1,0:T(8,128)} all-gather(f32[1,2,64,256]{3,2,1,0:T(8,128)S(1)} %get-tuple-element.26), channel_id=1, replica_groups=mesh['snode'=128,'rhs'=4] {'rhs'}, dimensions={0}, use_global_device_ids=true | all-gather | bytes 655360 | tf_op jit(solution)/shard_map/all_gather | solution.py:329
  13.6 4.2 %first.1 = (f32[2,256,128]{2,1,0:T(8,128)}, bf16[256,16,128]{2,1,0:T(8,128)(2,1)}) custom-call(s32[256]{0:T(256)} %select_reduce_fusion.source_ref, f32[4,2,64,256]{3,2,1,0:T(8,128)} %all_gather.25.diag_hbm, f32[3,2,256,128]{3,2,1,0:T(8,128)} %rhs_hbm.5, bf16[2,2,1024,256]{3,2,1,0:T(8,128)(2,1)} %off_hbm.7), custom_call_target="tpu_custom_call" | custom-call | flops 671088640 | bytes 4719616 | tf_op jit(solution)/shard_map/first/pallas_call | solution.py:299
  17.8 0.0 copy-done.5
  17.8 22.8 %all-to-all-start = ((bf16[256,16,128]{2,1,0:T(8,128)(2,1)}), bf16[256,16,128]{2,1,0:T(8,128)(2,1)S(1)}, u32[]{:S(2)}, u32[]{:S(2)}) async-start(bf16[256,16,128]{2,1,0:T(8,128)(2,1)} %get-tuple-element.13), calls=%async_computation | async-start | bytes 2097152 | tf_op jit(solution)/shard_map/all_to_all | solution.py:346
  40.6 0.1 reshape_squeeze.18
  40.7 0.1 reshape_squeeze.17
  40.8 0.1 reshape_squeeze.20
  40.9 0.0 copy-done.4
  40.9 0.1 reshape_squeeze.19
  41.0 0.1 reshape_squeeze.21
  41.1 0.2 convert_reduce_fusion
  41.3 10.7 %all-gather.2 = s32[8,2,128]{2,1,0:T(2,128)S(1)} all-gather(s32[1,2,128]{2,1,0:T(2,128)S(1)} %add_bitcast_fusion), channel_id=2, replica_groups={{0,4,8,12,16,20,24,28},{32,36,40,44,48,52,56,60},{64,68,72,76,80,84,88,..., dimensions={0}, use_global_device_ids=true | all-gather | bytes 9216 | tf_op jit(solution)/shard_map/all_gather | solution.py:376
  52.0 52.6 %all-gather.1 = s32[128,2,128]{2,1,0:T(2,128)S(1)} all-gather(s32[8,2,128]{2,1,0:T(2,128)S(1)} %all-gather.2), channel_id=3, replica_groups={{0,32,64,96,128,160,192,224,256,288,320,352,384,416,448,480},{4,36,68,1..., dimensions={0}, use_global_device_ids=true | all-gather | bytes 139264 | tf_op jit(solution)/shard_map/all_gather | solution.py:376
  104.6 0.1 fusion.17
  104.7 0.2 select_reduce_fusion.3
  105.0 0.1 copy.15
  105.1 0.1 reshape.396.code_ref
  105.2 0.0 copy-start.3
  105.2 0.1 iota_add_fusion.1
  105.3 0.1 add.182
  105.5 0.0 copy-start.6
  105.5 0.7 select_reduce_fusion.1.source_ref
  106.2 10.9 %all_gather.26.diag_hbm = f32[4,2,64,256]{3,2,1,0:T(8,128)} all-gather(f32[1,2,64,256]{3,2,1,0:T(8,128)S(1)} %get-tuple-element.27), channel_id=1, replica_groups=mesh['snode'=128,'rhs'=4] {'rhs'}, dimensions={0}, use_global_device_ids=true | all-gather | bytes 655360 | tf_op jit(solution)/shard_map/all_gather | solution.py:329
  117.1 1.3 fusion.gather_hbm
  118.3 0.0 all-to-all-done.inbound_ref
  118.3 1.0 copy-done.1
  119.3 5.4 %middle.1 = (f32[2,256,128]{2,1,0:T(8,128)}, bf16[256,16,128]{2,1,0:T(8,128)(2,1)}) custom-call(s32[256]{0:T(256)} %select_reduce_fusion.1.source_ref, bf16[256,16,128]{2,1,0:T(8,128)(2,1)} %copy-done.1, bf16[256,2048]{1,0:T(8,128)(2,1)} %fusion.gather_hbm, f32[4,2,64,256]{3,2,1,0:T(8,128)} %all_gather.26.diag_hbm, f32[3,2,256,128]{3,2,1,0:T(8,128)} %rhs_hbm.5, ...), custom_call_target="tpu_custom_call" | custom-call | flops 671088640 | bytes 6816768 | tf_op jit(solution)/shard_map/middle/pallas_call | solution.py:299
  124.8 24.5 %all-to-all-start.1 = ((bf16[256,16,128]{2,1,0:T(8,128)(2,1)}), bf16[256,16,128]{2,1,0:T(8,128)(2,1)S(1)}, u32[]{:S(2)}, u32[]{:S(2)}) async-start(bf16[256,16,128]{2,1,0:T(8,128)(2,1)} %get-tuple-element.14), calls=%async_computation.1 | async-start | bytes 2097152 | tf_op jit(solution)/shard_map/all_to_all | solution.py:346
  149.3 0.1 copy.17
  149.4 0.1 reshape.397.code_ref
  149.6 0.0 copy-start.2
  149.6 0.1 iota_add_fusion
  149.7 0.1 add.186
  149.8 11.2 %all_gather.27.diag_hbm = f32[4,2,64,256]{3,2,1,0:T(8,128)} all-gather(f32[1,2,64,256]{3,2,1,0:T(8,128)S(1)} %get-tuple-element.25), channel_id=1, replica_groups=mesh['snode'=128,'rhs'=4] {'rhs'}, dimensions={0}, use_global_device_ids=true | all-gather | bytes 655360 | tf_op jit(solution)/shard_map/all_gather | solution.py:329
  161.0 1.3 fusion.1.gather_hbm
  162.3 42.6 %all-to-all-done.1.inbound_ref = bf16[256,16,128]{2,1,0:T(8,128)(2,1)S(1)} async-done(((bf16[256,16,128]{2,1,0:T(8,128)(2,1)}), bf16[256,16,128]{2,1,0:T(8,128)(2,1)S(1)}, u32[]{:S(2)}, u32[]{:S(2)}) %all-to-all-start.1) | async-done | bytes 1048608 | tf_op jit(solution)/shard_map/all_to_all | solution.py:346
  204.9 1.0 copy-done
  205.9 5.5 %top.1 = (f32[3,2,256,128]{3,2,1,0:T(8,128)}, bf16[256,16,128]{2,1,0:T(8,128)(2,1)}) custom-call(s32[256]{0:T(256)} %copy-done.2, bf16[256,16,128]{2,1,0:T(8,128)(2,1)} %copy-done, bf16[256,2048]{1,0:T(8,128)(2,1)} %fusion.1.gather_hbm, f32[4,2,64,256]{3,2,1,0:T(8,128)} %all_gather.27.diag_hbm, f32[3,2,256,128]{3,2,1,0:T(8,128)} %rhs_hbm.5), custom_call_target="tpu_custom_call" | custom-call | flops 671088640 | bytes 5243904 | tf_op jit(solution)/shard_map/top/pallas_call | solution.py:299
  211.4 62.2 %all_to_all.20.inbound_ref = bf16[256,16,128]{2,1,0:T(8,128)(2,1)} all-to-all(bf16[256,16,128]{2,1,0:T(8,128)(2,1)} %get-tuple-element.15), channel_id=1, replica_groups=mesh['snode'=128,'rhs'=4] {'snode'}, dimensions={0} | all-to-all | bytes 2097152 | tf_op jit(solution)/shard_map/all_to_all | solution.py:346
  273.6 4.9 %upper.1 = (f32[3,2,256,128]{3,2,1,0:T(8,128)}, bf16[256,16,128]{2,1,0:T(8,128)(2,1)}) custom-call(s32[128]{0:T(128)} %copy-done.6, s32[256]{0:T(256)} %copy-done.3, bf16[256,16,128]{2,1,0:T(8,128)(2,1)} %all_to_all.20.inbound_ref, f32[4,2,64,256]{3,2,1,0:T(8,128)} %all_gather.26.diag_hbm, ...), custom_call_target="tpu_custom_call", output_to_operand_aliasing={{0}: (6, {})} | custom-call | flops 671088640 | bytes 6555136 | tf_op jit(solution)/shard_map/upper/pallas_call | solution.py:299
  278.5 62.2 %all_to_all.21.inbound_ref = bf16[256,16,128]{2,1,0:T(8,128)(2,1)} all-to-all(bf16[256,16,128]{2,1,0:T(8,128)(2,1)} %get-tuple-element.18), channel_id=1, replica_groups=mesh['snode'=128,'rhs'=4] {'snode'}, dimensions={0} | all-to-all | bytes 2097152 | tf_op jit(solution)/shard_map/all_to_all | solution.py:346
  340.7 4.4 %last.1 = f32[3,2,256,128]{3,2,1,0:T(8,128)} custom-call(s32[128]{0:T(128)} %copy-done.5, bf16[256,16,128]{2,1,0:T(8,128)(2,1)} %all_to_all.21.inbound_ref, f32[4,2,64,256]{3,2,1,0:T(8,128)} %all_gather.25.diag_hbm, bf16[2,2,1024,256]{3,2,1,0:T(8,128)(2,1)} %off_hbm.7, f32[2,256,128]{2,1,0:T(8,128)} %get-tuple-element.19.low_hbm, ...), custom_call_target="tpu_custom_call", output_to_operand_aliasing={{}: (5, {})} | custom-call | flops 671088640 | bytes 5505536 | tf_op jit(solution)/shard_map/last/pallas_call | solution.py:299
  (18 shorter events, 0.1 us)
Async XLA Ops:
  1.0 16.8 %copy-start.5 = (s32[128]{0:T(128)}, s32[128]{0:T(128)S(1)}, u32[]{:S(2)}) copy-start(s32[128]{0:T(128)S(1)} %multiply_add_fusion.1.dest_ref) | copy-start | bytes 1540
  13.6 27.3 %copy-start.4 = (s32[2,2,64]{2,1,0:T(2,128)S(1)}, s32[2,2,64]{2,1,0:T(2,128)}, u32[]{:S(2)}) copy-start(s32[2,2,64]{2,1,0:T(2,128)} %param.9) | copy-start | bytes 3076
  17.8 100.5 %all-to-all-start = ((bf16[256,16,128]{2,1,0:T(8,128)(2,1)}), bf16[256,16,128]{2,1,0:T(8,128)(2,1)S(1)}, u32[]{:S(2)}, u32[]{:S(2)}) async-start(bf16[256,16,128]{2,1,0:T(8,128)(2,1)} %get-tuple-element.13), calls=%async_computation | async-start | bytes 2097152 | tf_op jit(solution)/shard_map/all_to_all | solution.py:346
  105.2 19.5 %copy-start.3 = (s32[256]{0:T(256)}, s32[256]{0:T(256)S(1)}, u32[]{:S(2)}) copy-start(s32[256]{0:T(256)S(1)} %reshape.396.code_ref) | copy-start | bytes 3076
  105.5 19.3 %copy-start.6 = (s32[128]{0:T(128)}, s32[128]{0:T(128)S(1)}, u32[]{:S(2)}) copy-start(s32[128]{0:T(128)S(1)} %multiply_add_fusion.dest_ref) | copy-start | bytes 1540
  118.3 1.0 copy-start.1
  124.8 80.1 %all-to-all-start.1 = ((bf16[256,16,128]{2,1,0:T(8,128)(2,1)}), bf16[256,16,128]{2,1,0:T(8,128)(2,1)S(1)}, u32[]{:S(2)}, u32[]{:S(2)}) async-start(bf16[256,16,128]{2,1,0:T(8,128)(2,1)} %get-tuple-element.14), calls=%async_computation.1 | async-start | bytes 2097152 | tf_op jit(solution)/shard_map/all_to_all | solution.py:346
  149.6 55.3 %copy-start.2 = (s32[256]{0:T(256)}, s32[256]{0:T(256)S(1)}, u32[]{:S(2)}) copy-start(s32[256]{0:T(256)S(1)} %reshape.397.code_ref) | copy-start | bytes 3076
  204.9 1.0 copy-start

commit v4 on v3

v4 whole, which is shorter than its diff:
```python
import functools

import jax
import jax.numpy as jnp
from jax import lax
from jax.experimental import pallas as pl
from jax.experimental.pallas import tpu as pltpu
from jax.sharding import PartitionSpec as P

BR = 16
HALF = BR // 2
F32 = jnp.float32
BF16 = jnp.bfloat16
PRECISE = lax.Precision.HIGHEST


def whole_diag(diag_ref, s):
    parts = [diag_ref[y, s] for y in range(diag_ref.shape[0])]
    return jnp.concatenate(parts, axis=0)


def solve(diag, x):
    return lax.dot_general(
        diag, x, (((1,), (0,)), ((), ())), precision=PRECISE, preferred_element_type=F32
    )


def solve_transposed(diag, x):
    return lax.dot_general(
        diag, x, (((0,), (0,)), ((), ())), precision=PRECISE, preferred_element_type=F32
    )


def place(table_ref, index_ref, staged_ref, out_ref, sems):
    chunks = sems.shape[0]
    size = out_ref.shape[0] // chunks
    copies = []
    for c in range(chunks):

        def body(i, _):
            staged_ref[i] = table_ref[index_ref[i]]
            return 0

        lax.fori_loop(c * size, (c + 1) * size, body, 0, unroll=8)
        part = pl.ds(c * size, size)
        copies.append(pltpu.make_async_copy(staged_ref.at[part], out_ref.at[part], sems.at[c]))
        copies[-1].start()
    return copies


def send_updates(low_ref, off_ref, source_ref, staged_ref, out_ref, table_ref, sems):
    nodes, rows, _ = off_ref.shape
    lanes = low_ref.shape[2]
    per_node = rows // BR
    for s in range(nodes):
        update = jnp.dot(off_ref[s], low_ref[s].astype(BF16), preferred_element_type=F32)
        table_ref[pl.ds(s * per_node, per_node)] = update.astype(BF16).reshape(per_node, BR, lanes)
    table_ref[nodes * per_node] = jnp.zeros((BR, lanes), BF16)
    return place(table_ref, source_ref, staged_ref, out_ref, sems)


def fill_rows(solved, table_ref):
    blocks, _, lanes = table_ref.shape
    per_node = (blocks - 1) // len(solved)
    for s, values in enumerate(solved):
        table_ref[pl.ds(s * per_node, per_node)] = values.astype(BF16).reshape(per_node, BR, lanes)
    table_ref[blocks - 1] = jnp.zeros((BR, lanes), BF16)


def send_rows(solved, code_ref, staged_ref, out_ref, table_ref, sems):
    fill_rows(solved, table_ref)
    return place(table_ref, code_ref, staged_ref, out_ref, sems)


def place_rows(solved, code_ref, out_ref, table_ref):
    fill_rows(solved, table_ref)

    def body(i, _):
        out_ref[i] = table_ref[code_ref[i]]
        return 0

    lax.fori_loop(0, out_ref.shape[0], body, 0, unroll=8)


def fetch(pairs, sems):
    copies = [pltpu.make_async_copy(a, b, sems.at[i]) for i, (a, b) in enumerate(pairs)]
    for copy in copies:
        copy.start()
    return copies


def store(source, target, sem):
    copy = pltpu.make_async_copy(source, target, sem)
    copy.start()
    return copy


def finish(copies):
    for copy in copies:
        copy.wait()


def partial_sums(inbound_ref, gather_ref, part, size):
    lanes = inbound_ref.shape[2]
    blocks = inbound_ref[pl.ds(part * size, size)].astype(F32).reshape(size, 2, HALF, lanes)
    chosen = gather_ref[:, part * size * HALF : (part + 1) * size * HALF]
    sums = []
    for half in range(2):
        rows = blocks[:, half].reshape(size * HALF, lanes).astype(BF16)
        sums.append(jnp.dot(chosen, rows, preferred_element_type=F32))
    return sums


def diag_copies(place_ref, own_hbm, part_hbms, diag_ref):
    sources = [own_hbm] + list(part_hbms)
    return [(source, diag_ref.at[place_ref[i]]) for i, source in enumerate(sources)]


def lower_solve(inbound_hbm, inbound_ref, gather_hbm, gather_ref, diag_ref, rhs_ref, others, sems):
    nodes, order, lanes = rhs_ref.shape
    chunks = 4
    size = inbound_ref.shape[0] // chunks
    pairs = [(gather_hbm, gather_ref)]
    for c in range(chunks):
        part = pl.ds(c * size, size)
        pairs.append((inbound_hbm.at[part], inbound_ref.at[part]))
    copies = fetch(pairs + others, sems)
    copies[0].wait()
    sums = None
    for c in range(chunks):
        copies[1 + c].wait()
        found = partial_sums(inbound_ref, gather_ref, c, size)
        sums = found if sums is None else [x + y for x, y in zip(sums, found)]
    rest = copies[1 + chunks :]
    finish(rest[:NEEDED])
    part = order // 2
    solved = []
    for s in range(nodes):
        pieces = [x[s * part : (s + 1) * part].reshape(order // BR, HALF, lanes) for x in sums]
        total = jnp.stack(pieces, axis=1).reshape(order, lanes)
        solved.append(solve(whole_diag(diag_ref, s), rhs_ref[s] - total))
    return solved, rest[NEEDED:]


NEEDED = 5


def first_kernel(
    source_ref,
    place_ref,
    diag_hbm,
    part1_hbm,
    part2_hbm,
    part3_hbm,
    rhs_hbm,
    off_hbm,
    low_hbm,
    whole_hbm,
    out_hbm,
    diag_ref,
    rhs_ref,
    off_ref,
    low_ref,
    table_ref,
    staged_ref,
    in_sems,
    keep_sems,
    out_sems,
):
    pairs = diag_copies(place_ref, diag_hbm.at[0], [part1_hbm, part2_hbm, part3_hbm], diag_ref)
    pairs += [(rhs_hbm.at[0], rhs_ref), (off_hbm.at[0], off_ref)]
    copies = fetch(pairs, in_sems)
    finish(copies[:NEEDED])
    kept = [store(diag_ref, whole_hbm, keep_sems.at[0])]
    for s in range(rhs_ref.shape[0]):
        low_ref[s] = solve(whole_diag(diag_ref, s), rhs_ref[s])
    kept.append(store(low_ref, low_hbm, keep_sems.at[1]))
    finish(copies[NEEDED:])
    kept += send_updates(low_ref, off_ref, source_ref, staged_ref, out_hbm, table_ref, out_sems)
    finish(kept)


def middle_kernel(
    h,
    source_ref,
    place_ref,
    inbound_hbm,
    gather_hbm,
    diag_hbm,
    part1_hbm,
    part2_hbm,
    part3_hbm,
    rhs_hbm,
    off_hbm,
    low_hbm,
    whole_hbm,
    out_hbm,
    inbound_ref,
    gather_ref,
    diag_ref,
    rhs_ref,
    off_ref,
    low_ref,
    table_ref,
    staged_ref,
    in_sems,
    keep_sems,
    out_sems,
):
    pairs = diag_copies(place_ref, diag_hbm.at[h], [part1_hbm, part2_hbm, part3_hbm], diag_ref)
    pairs += [(rhs_hbm.at[h], rhs_ref), (off_hbm.at[h], off_ref)]
    solved, late = lower_solve(
        inbound_hbm, inbound_ref, gather_hbm, gather_ref, diag_ref, rhs_ref, pairs, in_sems
    )
    kept = [store(diag_ref, whole_hbm, keep_sems.at[0])]
    for s, values in enumerate(solved):
        low_ref[s] = values
    kept.append(store(low_ref, low_hbm, keep_sems.at[1]))
    finish(late)
    kept += send_updates(low_ref, off_ref, source_ref, staged_ref, out_hbm, table_ref, out_sems)
    finish(kept)


def top_kernel(
    h,
    code_ref,
    place_ref,
    inbound_hbm,
    gather_hbm,
    diag_hbm,
    part1_hbm,
    part2_hbm,
    part3_hbm,
    rhs_hbm,
    answer_hbm,
    out_hbm,
    inbound_ref,
    gather_ref,
    diag_ref,
    rhs_ref,
    sol_ref,
    table_ref,
    staged_ref,
    in_sems,
    keep_sems,
    out_sems,
):
    pairs = diag_copies(place_ref, diag_hbm.at[h], [part1_hbm, part2_hbm, part3_hbm], diag_ref)
    pairs += [(rhs_hbm.at[h], rhs_ref)]
    solved, _ = lower_solve(
        inbound_hbm, inbound_ref, gather_hbm, gather_ref, diag_ref, rhs_ref, pairs, in_sems
    )
    for s, lower in enumerate(solved):
        solved[s] = solve_transposed(whole_diag(diag_ref, s), lower)
        sol_ref[s] = solved[s]
    kept = [store(sol_ref, answer_hbm.at[h], keep_sems.at[0])]
    kept += send_rows(solved, code_ref, staged_ref, out_hbm, table_ref, out_sems)
    finish(kept)


def upper_solve(h, dest_ref, inbound_ref, diag_ref, off_hbm, low_ref, off_ref, sol_ref, rows_ref, sem):
    (get_off,) = fetch([(off_hbm.at[h], off_ref)], sem)
    nodes, rows, _ = off_ref.shape
    per_node = rows // BR
    lanes = low_ref.shape[2]

    def body(k, _):
        rows_ref[k] = inbound_ref[dest_ref[k]]
        return 0

    lax.fori_loop(0, nodes * per_node, body, 0, unroll=8)
    get_off.wait()
    solved = []
    for s in range(nodes):
        block_rows = rows_ref[pl.ds(s * per_node, per_node)].reshape(rows, lanes)
        taken = lax.dot_general(
            off_ref[s], block_rows, (((0,), (0,)), ((), ())), preferred_element_type=F32
        )
        solved.append(solve_transposed(whole_diag(diag_ref, s), low_ref[s] - taken))
        sol_ref[s] = solved[s]
    return solved


def upper_kernel(
    h,
    dest_ref,
    code_ref,
    inbound_ref,
    diag_ref,
    off_hbm,
    low_ref,
    _,
    answer_hbm,
    out_ref,
    off_ref,
    sol_ref,
    rows_ref,
    table_ref,
    sems,
):
    solved = upper_solve(
        h, dest_ref, inbound_ref, diag_ref, off_hbm, low_ref, off_ref, sol_ref, rows_ref, sems
    )
    kept = store(sol_ref, answer_hbm.at[h], sems.at[1])
    place_rows(solved, code_ref, out_ref, table_ref)
    kept.wait()


def last_kernel(
    dest_ref, inbound_ref, diag_ref, off_hbm, low_ref, _, answer_hbm, off_ref, sol_ref, rows_ref, sems
):
    upper_solve(
        0, dest_ref, inbound_ref, diag_ref, off_hbm, low_ref, off_ref, sol_ref, rows_ref, sems
    )
    store(sol_ref, answer_hbm.at[0], sems.at[1]).wait()


def scalar(x):
    return x, pl.BlockSpec(memory_space=pltpu.SMEM)


def whole(x):
    return x, pl.BlockSpec(memory_space=pltpu.VMEM)


def far(x):
    return x, pl.BlockSpec(memory_space=pltpu.HBM)


def anywhere(x):
    return x, pl.BlockSpec(memory_space=pl.ANY)


def call(kernel, name, operands, outs, scratch, flops, aliases={}, limit=None):
    arrays = [x for x, _ in operands]
    moved = sum(x.size * x.dtype.itemsize for x, _ in operands + outs)
    return pl.pallas_call(
        kernel,
        name=name,
        out_shape=[jax.ShapeDtypeStruct(x.shape, x.dtype) for x, _ in outs],
        in_specs=[spec for _, spec in operands],
        out_specs=[spec for _, spec in outs],
        scratch_shapes=scratch,
        input_output_aliases=aliases,
        compiler_params=pltpu.CompilerParams(vmem_limit_bytes=limit),
        cost_estimate=pl.CostEstimate(flops=flops, bytes_accessed=moved, transcendentals=0),
    )(*arrays)


def on_device(right_sides, diag_inverse, off_diagonal, target_snode, target_block):
    levels, nodes, order, lanes = right_sides.shape
    per_node = target_snode.shape[2]
    row_blocks = order // BR
    devices = lax.axis_size("snode")
    sharers = lax.axis_size("rhs")
    outgoing = nodes * per_node
    capacity = 2 * outgoing // devices
    slots = devices * capacity
    local_rows = nodes * row_blocks
    couplings = levels - 1

    def diag_parts(h):
        mine = diag_inverse[h]
        steps = [[(y, (y + k) % sharers) for y in range(sharers)] for k in range(1, sharers)]
        return [lax.ppermute(mine, "rhs", step) for step in steps]

    mine = lax.axis_index("rhs")
    places = (mine - lax.iota(jnp.int32, sharers)) % sharers

    parts = [diag_parts(0)]

    block_order = lax.iota(jnp.int32, outgoing)
    flat_target = target_snode.reshape(couplings, outgoing)
    owner = flat_target // nodes
    row = flat_target % nodes * row_blocks + target_block.reshape(couplings, outgoing)
    earlier = (owner[:, :, None] == owner[:, None, :]) & (
        block_order[None, None, :] < block_order[None, :, None]
    )
    destinations = owner * capacity + jnp.sum(earlier.astype(jnp.int32), axis=2)
    slot_ids = lax.iota(jnp.int32, slots)
    placed = destinations[:, None, :] == slot_ids[None, :, None]
    sources = jnp.min(jnp.where(placed, block_order[None, None, :], outgoing), axis=2)
    ids = slot_ids.reshape(devices, 1, capacity, 1)
    placed = destinations[None, :, None, :] == ids
    sent = jnp.min(jnp.where(placed, row[None, :, None, :], local_rows), axis=3)

    def exchange(x):
        return lax.all_to_all(x, "snode", split_axis=0, concat_axis=0, tiled=True)

    arrived = exchange(sent.reshape(devices, couplings * capacity))

    vector = far(jax.ShapeDtypeStruct((nodes, order, lanes), F32))
    payload = far(jax.ShapeDtypeStruct((slots, BR, lanes), BF16))
    near_payload = whole(payload[0])
    gathered = far(jax.ShapeDtypeStruct((sharers,) + diag_inverse.shape[1:], F32))
    answer = jax.ShapeDtypeStruct(right_sides.shape, F32)
    two = pltpu.SemaphoreType.DMA((2,))
    inputs = pltpu.SemaphoreType.DMA((12,))
    vectors = pltpu.VMEM((nodes, order, lanes), F32)
    off_buffer = pltpu.VMEM(off_diagonal.shape[1:], BF16)
    diag_buffer = pltpu.VMEM(gathered[0].shape, F32)
    gather_buffer = pltpu.VMEM((local_rows * HALF, slots * HALF), BF16)
    table = pltpu.VMEM((outgoing + 1, BR, lanes), BF16)
    row_table = pltpu.VMEM((local_rows + 1, BR, lanes), BF16)
    rows_scratch = pltpu.VMEM((outgoing, BR, lanes), BF16)
    blocks_buffer = pltpu.VMEM((slots, BR, lanes), BF16)
    send = [blocks_buffer, inputs, two, pltpu.SemaphoreType.DMA((4,))]
    flops = 40 * nodes * order * order * lanes
    small = 24 << 20

    def diag_operands(h):
        return [far(diag_inverse)] + [far(x) for x in parts[h]]

    lower, whole_diags = [None] * couplings, [None] * couplings
    lower[0], whole_diags[0], out = call(
        first_kernel,
        "first",
        [scalar(sources[0]), scalar(places)]
        + diag_operands(0)
        + [far(right_sides), far(off_diagonal)],
        [vector, gathered, payload],
        [diag_buffer, vectors, off_buffer, vectors, table] + send,
        flops,
    )
    inbound = exchange(out)

    codes, gathers = [], []
    for h in range(couplings):
        code = arrived[:, h * capacity : (h + 1) * capacity].reshape(slots)
        codes.append(code)
        wanted = (code[:, None] * HALF + lax.iota(jnp.int32, HALF)[None, :]).reshape(slots * HALF)
        rows = lax.iota(jnp.int32, local_rows * HALF)
        gathers.append((rows[:, None] == wanted[None, :]).astype(BF16))

    for h in range(1, couplings):
        parts.append(diag_parts(h))
        lower[h], whole_diags[h], out = call(
            functools.partial(middle_kernel, h),
            "middle",
            [scalar(sources[h]), scalar(places), far(inbound), far(gathers[h - 1])]
            + diag_operands(h)
            + [far(right_sides), far(off_diagonal)],
            [vector, gathered, payload],
            [blocks_buffer, gather_buffer, diag_buffer, vectors, off_buffer, vectors, table] + send,
            flops,
        )
        inbound = exchange(out)
    top = couplings
    parts.append(diag_parts(top))
    answer, out = call(
        functools.partial(top_kernel, top),
        "top",
        [scalar(codes[top - 1]), scalar(places), far(inbound), far(gathers[top - 1])]
        + diag_operands(top)
        + [far(right_sides)],
        [far(answer), payload],
        [blocks_buffer, gather_buffer, diag_buffer, vectors, vectors, row_table] + send,
        flops,
    )
    inbound = exchange(out)
    for h in range(couplings - 1, 0, -1):
        answer, out = call(
            functools.partial(upper_kernel, h),
            "upper",
            [scalar(destinations[h]), scalar(codes[h - 1]), whole(inbound), whole(whole_diags[h])]
            + [anywhere(off_diagonal), whole(lower[h]), anywhere(answer)],
            [anywhere(answer), near_payload],
            [off_buffer, vectors, rows_scratch, row_table, two],
            flops,
            {6: 0},
            small,
        )
        inbound = exchange(out)
    (answer,) = call(
        last_kernel,
        "last",
        [scalar(destinations[0]), whole(inbound), whole(whole_diags[0])]
        + [anywhere(off_diagonal), whole(lower[0]), anywhere(answer)],
        [anywhere(answer)],
        [off_buffer, vectors, rows_scratch, two],
        flops,
        {5: 0},
        small,
    )
    return answer


def solution(mesh):
    in_specs = (
        P(None, "snode", None, "rhs"),
        P(None, "snode", "rhs", None),
        P(None, "snode", None, None),
        P(None, "snode", None),
        P(None, "snode", None),
    )
    out_specs = P(None, "snode", None, "rhs")
    return jax.shard_map(
        on_device, mesh=mesh, in_specs=in_specs, out_specs=out_specs, check_vma=False
    )
```

time: 346 us -> 320 us (0.925)
  the two profiles are of different devices: /device:TPU:41 before, /device:TPU:33 now
where the time goes in v4:
time: 320 us; the launch traced here: 319 us
  waiting for transfers between devices  154 us (48%)
  starting transfers between devices  69.3 us (22%)
  blocking collectives  62 us (19%)
  Pallas kernels  20.3 us (6%)
  local copies, waits for them, and re-layouts  8.91 us (3%)
  other arithmetic  3.79 us (1%)
    all_to_all x4, waiting for transfers between devices, exchange(): return lax.all_to_all(x, 'snode', split_axis=0, concat_axis=0, tiled=True)  148 us
    all_to_all x1, blocking collectives, exchange(): return lax.all_to_all(x, 'snode', split_axis=0, concat_axis=0, tiled=True)  62 us
    all_to_all x4, starting transfers between devices, exchange(): return lax.all_to_all(x, 'snode', split_axis=0, concat_axis=0, tiled=True)  41.4 us
    ppermute x9, starting transfers between devices, diag_parts(): return [lax.ppermute(mine, 'rhs', step) for step in steps]  27.9 us
    pallas_call x5, Pallas kernels, call(): pl.pallas_call(kernel, name=name, out_shape=[jax.ShapeDtypeStruct(x.shape...  20.3 us
  transfers between devices with their start and end apart: 13, of which 7 were waited for; matrix products, arithmetic and copies ran while one was open for 2% of the time, Pallas kernels for 1%

profile of v4, /device:TPU:33, one launch (start us, length us, event | category | flops | bytes accessed | tf_op | source)
XLA Modules:
  0.0 318.9 jit_solution(4328126061778378408)
XLA Ops:
  0.0 1.7 slice_bitcast_fusion
  1.7 3.2 %collective-permute-start = (f32[2,64,256]{2,1,0:T(8,128)S(1)}, f32[2,64,256]{2,1,0:T(8,128)S(1)}, u32[]{:S(2)}, u32[]{:S(2)}) collective-permute-start(f32[2,64,256]{2,1,0:T(8,128)S(1)} %get-tuple-element.27), channel_id=1, source_target_pairs={{0,1},{1,2},{2,3},{3,0},{4,5},{5,6},{6,7},{7,4},{8,9},{9,10},{10,1... | collective-permute-start | bytes 393224 | tf_op jit(solution)/shard_map/ppermute | solution.py:365
  4.9 4.5 %collective-permute-start.1 = (f32[2,64,256]{2,1,0:T(8,128)S(1)}, f32[2,64,256]{2,1,0:T(8,128)S(1)}, u32[]{:S(2)}, u32[]{:S(2)}) collective-permute-start(f32[2,64,256]{2,1,0:T(8,128)S(1)} %get-tuple-element.27), channel_id=1, source_target_pairs={{0,2},{1,3},{2,0},{3,1},{4,6},{5,7},{6,4},{7,5},{8,10},{9,11},{10,... | collective-permute-start | bytes 393224 | tf_op jit(solution)/shard_map/ppermute | solution.py:365
  9.5 3.0 collective-permute-start.2
  12.5 0.8 reshape.221
  13.2 0.8 reshape.225
  14.0 0.2 convert_reduce_fusion
  14.2 0.2 select_reduce_fusion.1
  14.4 0.7 copy.11
  15.2 20.1 %all-to-all-start = ((s32[128,1,4]{2,1,0:T(1,128)}), s32[128,1,4]{2,1,0:T(1,128)S(1)}, u32[]{:S(2)}, u32[]{:S(2)}) async-start(s32[128,1,4]{2,1,0:T(1,128)} %copy.11), calls=%async_computation | async-start | bytes 131072 | tf_op jit(solution)/shard_map/all_to_all | solution.py:388
  35.3 0.1 select_reduce_fusion
  35.5 0.6 fusion.6
  36.1 0.6 and_select_fusion.place_ref
  36.7 0.6 copy-done.7
  37.4 4.2 %first.1 = (f32[2,256,128]{2,1,0:T(8,128)}, f32[4,2,64,256]{3,2,1,0:T(8,128)}, bf16[256,16,128]{2,1,0:T(8,128)(2,1)}) custom-call(s32[256]{0:T(256)} %bitcast.17, s32[4]{0:T(128)} %and_select_fusion.place_ref, f32[3,2,64,256]{3,2,1,0:T(8,128)} %diag_hbm.5, f32[2,64,256]{2,1,0:T(8,128)} %copy-done.7, f32[2,64,256]{2,1,0:T(8,128)} %copy-done.8, ...), custom_call_target="tpu_custom_call" | custom-call | flops 671088640 | bytes 5506064 | tf_op jit(solution)/shard_map/first/pallas_call | solution.py:337
  41.7 7.9 %all-to-all-done = s32[128,1,4]{2,1,0:T(1,128)S(1)} async-done(((s32[128,1,4]{2,1,0:T(1,128)}), s32[128,1,4]{2,1,0:T(1,128)S(1)}, u32[]{:S(2)}, u32[]{:S(2)}) %all-to-all-start) | async-done | bytes 2080 | tf_op jit(solution)/shard_map/all_to_all | solution.py:388
  49.5 8.3 %all-to-all-start.1 = ((bf16[256,16,128]{2,1,0:T(8,128)(2,1)}), bf16[256,16,128]{2,1,0:T(8,128)(2,1)S(1)}, u32[]{:S(2)}, u32[]{:S(2)}) async-start(bf16[256,16,128]{2,1,0:T(8,128)(2,1)} %get-tuple-element.15), calls=%async_computation.1 | async-start | bytes 2097152 | tf_op jit(solution)/shard_map/all_to_all | solution.py:388
  57.8 2.3 collective-permute-start.3
  60.1 2.4 collective-permute-start.4
  62.5 3.8 %collective-permute-start.5 = (f32[2,64,256]{2,1,0:T(8,128)S(1)}, f32[2,64,256]{2,1,0:T(8,128)S(1)}, u32[]{:S(2)}, u32[]{:S(2)}) collective-permute-start(f32[2,64,256]{2,1,0:T(8,128)S(1)} %get-tuple-element.26), channel_id=1, source_target_pairs={{0,3},{1,0},{2,1},{3,2},{4,7},{5,4},{6,5},{7,6},{8,11},{9,8},{10,9... | collective-permute-start | bytes 393224 | tf_op jit(solution)/shard_map/ppermute | solution.py:365
  66.3 0.1 fusion.5
  66.4 0.1 reshape.226.code_ref
  66.6 0.1 iota_add_fusion.1
  66.7 0.1 add.106
  66.8 1.2 fusion.gather_hbm
  68.0 2.8 collective-permute-done.5.part3_hbm
  70.8 42.5 %all-to-all-done.1.inbound_hbm = bf16[256,16,128]{2,1,0:T(8,128)(2,1)S(1)} async-done(((bf16[256,16,128]{2,1,0:T(8,128)(2,1)}), bf16[256,16,128]{2,1,0:T(8,128)(2,1)S(1)}, u32[]{:S(2)}, u32[]{:S(2)}) %all-to-all-start.1) | async-done | bytes 1048608 | tf_op jit(solution)/shard_map/all_to_all | solution.py:388
  113.4 1.0 copy-done.5
  114.4 5.4 %middle.1 = (f32[2,256,128]{2,1,0:T(8,128)}, f32[4,2,64,256]{3,2,1,0:T(8,128)}, bf16[256,16,128]{2,1,0:T(8,128)(2,1)}) custom-call(s32[256]{0:T(256)} %bitcast.16, s32[4]{0:T(128)} %and_select_fusion.place_ref, bf16[256,16,128]{2,1,0:T(8,128)(2,1)} %copy-done.5, bf16[256,2048]{1,0:T(8,128)(2,1)} %fusion.gather_hbm, f32[3,2,64,256]{3,2,1,0:T(8,128)} %diag_hbm.5, ...), custom_call_target="tpu_custom_call" | custom-call | flops 671088640 | bytes 7603216 | tf_op jit(solution)/shard_map/middle/pallas_call | solution.py:337
  119.8 6.5 %all-to-all-start.2 = ((bf16[256,16,128]{2,1,0:T(8,128)(2,1)}), bf16[256,16,128]{2,1,0:T(8,128)(2,1)S(1)}, u32[]{:S(2)}, u32[]{:S(2)}) async-start(bf16[256,16,128]{2,1,0:T(8,128)(2,1)} %get-tuple-element.16), calls=%async_computation.2 | async-start | bytes 2097152 | tf_op jit(solution)/shard_map/all_to_all | solution.py:388
  126.3 2.3 collective-permute-start.6
  128.6 2.4 collective-permute-start.7
  131.0 4.0 %collective-permute-start.8 = (f32[2,64,256]{2,1,0:T(8,128)}, f32[2,64,256]{2,1,0:T(8,128)}, u32[]{:S(2)}, u32[]{:S(2)}) collective-permute-start(f32[2,64,256]{2,1,0:T(8,128)} %get-tuple-element.25), channel_id=1, source_target_pairs={{0,3},{1,0},{2,1},{3,2},{4,7},{5,4},{6,5},{7,6},{8,11},{9,8},{10,9... | collective-permute-start | bytes 393224 | tf_op jit(solution)/shard_map/ppermute | solution.py:365
  135.0 0.1 reshape.227.code_ref
  135.2 0.1 iota_add_fusion
  135.3 0.1 add.110
  135.4 1.2 fusion.1.gather_hbm
  136.6 0.2 collective-permute-done.7.part2_hbm
  136.8 2.9 collective-permute-done.8.part3_hbm
  139.6 42.2 %all-to-all-done.2.inbound_hbm = bf16[256,16,128]{2,1,0:T(8,128)(2,1)S(1)} async-done(((bf16[256,16,128]{2,1,0:T(8,128)(2,1)}), bf16[256,16,128]{2,1,0:T(8,128)(2,1)S(1)}, u32[]{:S(2)}, u32[]{:S(2)}) %all-to-all-start.2) | async-done | bytes 1048608 | tf_op jit(solution)/shard_map/all_to_all | solution.py:388
  181.9 1.0 copy-done.6
  182.8 5.5 %top.1 = (f32[3,2,256,128]{3,2,1,0:T(8,128)}, bf16[256,16,128]{2,1,0:T(8,128)(2,1)}) custom-call(s32[256]{0:T(256)} %copy-done.14, s32[4]{0:T(128)} %and_select_fusion.place_ref, bf16[256,16,128]{2,1,0:T(8,128)(2,1)} %copy-done.6, bf16[256,2048]{1,0:T(8,128)(2,1)} %fusion.1.gather_hbm, f32[3,2,64,256]{3,2,1,0:T(8,128)} %diag_hbm.5, ...), custom_call_target="tpu_custom_call" | custom-call | flops 671088640 | bytes 5506064 | tf_op jit(solution)/shard_map/top/pallas_call | solution.py:337
  188.3 6.5 %all-to-all-start.3 = ((bf16[256,16,128]{2,1,0:T(8,128)(2,1)}), bf16[256,16,128]{2,1,0:T(8,128)(2,1)S(1)}, u32[]{:S(2)}, u32[]{:S(2)}) async-start(bf16[256,16,128]{2,1,0:T(8,128)(2,1)} %get-tuple-element.17), calls=%async_computation.3 | async-start | bytes 2097152 | tf_op jit(solution)/shard_map/all_to_all | solution.py:388
  194.9 55.6 %all-to-all-done.3.inbound_ref = bf16[256,16,128]{2,1,0:T(8,128)(2,1)S(1)} async-done(((bf16[256,16,128]{2,1,0:T(8,128)(2,1)}), bf16[256,16,128]{2,1,0:T(8,128)(2,1)S(1)}, u32[]{:S(2)}, u32[]{:S(2)}) %all-to-all-start.3) | async-done | bytes 1048608 | tf_op jit(solution)/shard_map/all_to_all | solution.py:388
  250.4 1.0 copy-done.2
  251.5 2.6 upper.1
  254.1 62.0 %all_to_all.32.inbound_ref = bf16[256,16,128]{2,1,0:T(8,128)(2,1)S(1)} all-to-all(bf16[256,16,128]{2,1,0:T(8,128)(2,1)S(1)} %get-tuple-element.21), channel_id=1, replica_groups=mesh['snode'=128,'rhs'=4] {'snode'}, dimensions={0} | all-to-all | bytes 2097152 | tf_op jit(solution)/shard_map/all_to_all | solution.py:388
  316.1 2.6 last.1
  (39 shorter events, 0.2 us)
Async XLA Ops:
  1.7 34.9 %collective-permute-start = (f32[2,64,256]{2,1,0:T(8,128)S(1)}, f32[2,64,256]{2,1,0:T(8,128)S(1)}, u32[]{:S(2)}, u32[]{:S(2)}) collective-permute-start(f32[2,64,256]{2,1,0:T(8,128)S(1)} %get-tuple-element.27), channel_id=1, source_target_pairs={{0,1},{1,2},{2,3},{3,0},{4,5},{5,6},{6,7},{7,4},{8,9},{9,10},{10,1... | collective-permute-start | bytes 393224 | tf_op jit(solution)/shard_map/ppermute | solution.py:365
  4.9 31.7 %collective-permute-start.1 = (f32[2,64,256]{2,1,0:T(8,128)S(1)}, f32[2,64,256]{2,1,0:T(8,128)S(1)}, u32[]{:S(2)}, u32[]{:S(2)}) collective-permute-start(f32[2,64,256]{2,1,0:T(8,128)S(1)} %get-tuple-element.27), channel_id=1, source_target_pairs={{0,2},{1,3},{2,0},{3,1},{4,6},{5,7},{6,4},{7,5},{8,10},{9,11},{10,... | collective-permute-start | bytes 393224 | tf_op jit(solution)/shard_map/ppermute | solution.py:365
  9.5 27.2 %collective-permute-start.2 = (f32[2,64,256]{2,1,0:T(8,128)S(1)}, f32[2,64,256]{2,1,0:T(8,128)S(1)}, u32[]{:S(2)}, u32[]{:S(2)}) collective-permute-start(f32[2,64,256]{2,1,0:T(8,128)S(1)} %get-tuple-element.27), channel_id=1, source_target_pairs={{0,3},{1,0},{2,1},{3,2},{4,7},{5,4},{6,5},{7,6},{8,11},{9,8},{10,9... | collective-permute-start | bytes 393224 | tf_op jit(solution)/shard_map/ppermute | solution.py:365
  15.2 34.4 %all-to-all-start = ((s32[128,1,4]{2,1,0:T(1,128)}), s32[128,1,4]{2,1,0:T(1,128)S(1)}, u32[]{:S(2)}, u32[]{:S(2)}) async-start(s32[128,1,4]{2,1,0:T(1,128)} %copy.11), calls=%async_computation | async-start | bytes 131072 | tf_op jit(solution)/shard_map/all_to_all | solution.py:388
  36.7 0.7 copy-start.7
  36.7 0.7 copy-start.8
  36.7 0.7 copy-start.9
  49.5 63.8 %all-to-all-start.1 = ((bf16[256,16,128]{2,1,0:T(8,128)(2,1)}), bf16[256,16,128]{2,1,0:T(8,128)(2,1)S(1)}, u32[]{:S(2)}, u32[]{:S(2)}) async-start(bf16[256,16,128]{2,1,0:T(8,128)(2,1)} %get-tuple-element.15), calls=%async_computation.1 | async-start | bytes 2097152 | tf_op jit(solution)/shard_map/all_to_all | solution.py:388
  57.8 10.2 %collective-permute-start.3 = (f32[2,64,256]{2,1,0:T(8,128)S(1)}, f32[2,64,256]{2,1,0:T(8,128)S(1)}, u32[]{:S(2)}, u32[]{:S(2)}) collective-permute-start(f32[2,64,256]{2,1,0:T(8,128)S(1)} %get-tuple-element.26), channel_id=1, source_target_pairs={{0,1},{1,2},{2,3},{3,0},{4,5},{5,6},{6,7},{7,4},{8,9},{9,10},{10,1... | collective-permute-start | bytes 393224 | tf_op jit(solution)/shard_map/ppermute | solution.py:365
  60.1 7.9 %collective-permute-start.4 = (f32[2,64,256]{2,1,0:T(8,128)S(1)}, f32[2,64,256]{2,1,0:T(8,128)S(1)}, u32[]{:S(2)}, u32[]{:S(2)}) collective-permute-start(f32[2,64,256]{2,1,0:T(8,128)S(1)} %get-tuple-element.26), channel_id=1, source_target_pairs={{0,2},{1,3},{2,0},{3,1},{4,6},{5,7},{6,4},{7,5},{8,10},{9,11},{10,... | collective-permute-start | bytes 393224 | tf_op jit(solution)/shard_map/ppermute | solution.py:365
  62.5 8.3 %collective-permute-start.5 = (f32[2,64,256]{2,1,0:T(8,128)S(1)}, f32[2,64,256]{2,1,0:T(8,128)S(1)}, u32[]{:S(2)}, u32[]{:S(2)}) collective-permute-start(f32[2,64,256]{2,1,0:T(8,128)S(1)} %get-tuple-element.26), channel_id=1, source_target_pairs={{0,3},{1,0},{2,1},{3,2},{4,7},{5,4},{6,5},{7,6},{8,11},{9,8},{10,9... | collective-permute-start | bytes 393224 | tf_op jit(solution)/shard_map/ppermute | solution.py:365
  68.0 45.4 %copy-start.10 = (f32[2,64,256]{2,1,0:T(8,128)}, f32[2,64,256]{2,1,0:T(8,128)S(1)}, u32[]{:S(2)}) copy-start(f32[2,64,256]{2,1,0:T(8,128)S(1)} %collective-permute-done.3.part1_hbm) | copy-start | bytes 393220
  68.0 45.4 %copy-start.11 = (f32[2,64,256]{2,1,0:T(8,128)}, f32[2,64,256]{2,1,0:T(8,128)S(1)}, u32[]{:S(2)}) copy-start(f32[2,64,256]{2,1,0:T(8,128)S(1)} %collective-permute-done.4.part2_hbm) | copy-start | bytes 393220
  70.8 42.5 %copy-start.13 = (f32[2,64,256]{2,1,0:T(8,128)}, f32[2,64,256]{2,1,0:T(8,128)S(1)}, u32[]{:S(2)}) copy-start(f32[2,64,256]{2,1,0:T(8,128)S(1)} %collective-permute-done.5.part3_hbm) | copy-start | bytes 393220
  113.4 1.0 copy-start.5
  119.8 62.1 %all-to-all-start.2 = ((bf16[256,16,128]{2,1,0:T(8,128)(2,1)}), bf16[256,16,128]{2,1,0:T(8,128)(2,1)S(1)}, u32[]{:S(2)}, u32[]{:S(2)}) async-start(bf16[256,16,128]{2,1,0:T(8,128)(2,1)} %get-tuple-element.16), calls=%async_computation.2 | async-start | bytes 2097152 | tf_op jit(solution)/shard_map/all_to_all | solution.py:388
  126.3 10.3 %collective-permute-start.6 = (f32[2,64,256]{2,1,0:T(8,128)}, f32[2,64,256]{2,1,0:T(8,128)S(1)}, u32[]{:S(2)}, u32[]{:S(2)}) collective-permute-start(f32[2,64,256]{2,1,0:T(8,128)} %get-tuple-element.25), channel_id=1, source_target_pairs={{0,1},{1,2},{2,3},{3,0},{4,5},{5,6},{6,7},{7,4},{8,9},{9,10},{10,1... | collective-permute-start | bytes 393224 | tf_op jit(solution)/shard_map/ppermute | solution.py:365
  128.6 8.2 %collective-permute-start.7 = (f32[2,64,256]{2,1,0:T(8,128)}, f32[2,64,256]{2,1,0:T(8,128)}, u32[]{:S(2)}, u32[]{:S(2)}) collective-permute-start(f32[2,64,256]{2,1,0:T(8,128)} %get-tuple-element.25), channel_id=1, source_target_pairs={{0,2},{1,3},{2,0},{3,1},{4,6},{5,7},{6,4},{7,5},{8,10},{9,11},{10,... | collective-permute-start | bytes 393224 | tf_op jit(solution)/shard_map/ppermute | solution.py:365
  131.0 8.6 %collective-permute-start.8 = (f32[2,64,256]{2,1,0:T(8,128)}, f32[2,64,256]{2,1,0:T(8,128)}, u32[]{:S(2)}, u32[]{:S(2)}) collective-permute-start(f32[2,64,256]{2,1,0:T(8,128)} %get-tuple-element.25), channel_id=1, source_target_pairs={{0,3},{1,0},{2,1},{3,2},{4,7},{5,4},{6,5},{7,6},{8,11},{9,8},{10,9... | collective-permute-start | bytes 393224 | tf_op jit(solution)/shard_map/ppermute | solution.py:365
  135.2 46.7 %copy-start.14 = (s32[256]{0:T(256)}, s32[256]{0:T(256)S(1)}, u32[]{:S(2)}) copy-start(s32[256]{0:T(256)S(1)} %reshape.227.code_ref) | copy-start | bytes 3076
  136.6 113.8 %copy-start = (bf16[2,2,1024,256]{3,2,1,0:T(8,128)(2,1)S(1)}, bf16[2,2,1024,256]{3,2,1,0:T(8,128)(2,1)}, u32[]{:S(2)}) copy-start(bf16[2,2,1024,256]{3,2,1,0:T(8,128)(2,1)} %off_hbm.7) | copy-start | bytes 6291460
  136.6 113.8 %copy-start.4 = (f32[2,256,128]{2,1,0:T(8,128)S(1)}, f32[2,256,128]{2,1,0:T(8,128)}, u32[]{:S(2)}) copy-start(f32[2,256,128]{2,1,0:T(8,128)} %get-tuple-element.19.low_ref) | copy-start | bytes 786436
  136.6 45.3 %copy-start.12 = (f32[2,64,256]{2,1,0:T(8,128)}, f32[2,64,256]{2,1,0:T(8,128)S(1)}, u32[]{:S(2)}) copy-start(f32[2,64,256]{2,1,0:T(8,128)S(1)} %collective-permute-done.6.part1_hbm) | copy-start | bytes 393220
  181.9 1.0 copy-start.6
  188.3 62.1 %all-to-all-start.3 = ((bf16[256,16,128]{2,1,0:T(8,128)(2,1)}), bf16[256,16,128]{2,1,0:T(8,128)(2,1)S(1)}, u32[]{:S(2)}, u32[]{:S(2)}) async-start(bf16[256,16,128]{2,1,0:T(8,128)(2,1)} %get-tuple-element.17), calls=%async_computation.3 | async-start | bytes 2097152 | tf_op jit(solution)/shard_map/all_to_all | solution.py:388
  250.4 1.0 copy-start.2
  254.1 62.0 %copy-start.1 = (f32[4,2,64,256]{3,2,1,0:T(8,128)S(1)}, f32[4,2,64,256]{3,2,1,0:T(8,128)}, u32[]{:S(2)}) copy-start(f32[4,2,64,256]{3,2,1,0:T(8,128)} %get-tuple-element.22.diag_ref) | copy-start | bytes 1572868
  254.1 62.0 %copy-start.3 = (f32[2,256,128]{2,1,0:T(8,128)S(1)}, f32[2,256,128]{2,1,0:T(8,128)}, u32[]{:S(2)}) copy-start(f32[2,256,128]{2,1,0:T(8,128)} %get-tuple-element.23.low_ref) | copy-start | bytes 786436

commit v5 on v4

v5 whole, which is shorter than its diff:
```python
import functools

import jax
import jax.numpy as jnp
from jax import lax
from jax.experimental import pallas as pl
from jax.experimental.pallas import tpu as pltpu
from jax.sharding import PartitionSpec as P

BR = 16
CAPACITY = 2
F32 = jnp.float32
BF16 = jnp.bfloat16
PRECISE = lax.Precision.HIGHEST


def whole_diag(diag_ref, s):
    parts = [diag_ref[y, s] for y in range(diag_ref.shape[0])]
    return jnp.concatenate(parts, axis=0)


def solve(diag, x):
    return lax.dot_general(
        diag, x, (((1,), (0,)), ((), ())), precision=PRECISE, preferred_element_type=F32
    )


def solve_transposed(diag, x):
    return lax.dot_general(
        diag, x, (((0,), (0,)), ((), ())), precision=PRECISE, preferred_element_type=F32
    )


def place(table_ref, index, capacity, staged_ref, out_ref, sems):
    chunks = sems.shape[0]
    peers = out_ref.shape[0] // capacity // chunks
    copies = []
    for c in range(chunks):
        place_chunk(table_ref, index, capacity, staged_ref, c * peers, peers)
        part = pl.ds(c * peers * capacity, peers * capacity)
        copies.append(pltpu.make_async_copy(staged_ref.at[part], out_ref.at[part], sems.at[c]))
        copies[-1].start()
    return copies


def place_chunk(table_ref, index, capacity, out_ref, start, peers):
    def body(d, _):
        for i in range(capacity):
            out_ref[d * capacity + i] = table_ref[index(d, i)]
        return 0

    lax.fori_loop(start, start + peers, body, 0, unroll=4)


def source_index(h, capacity, source_ref):
    return lambda d, i: source_ref[h, d * capacity + i]


def code_index(h, capacity, code_ref):
    return lambda d, i: code_ref[h * capacity + i, d]


def send_updates(h, low_ref, off_ref, source_ref, staged_ref, out_ref, table_ref, sems):
    nodes, rows, _ = off_ref.shape
    lanes = low_ref.shape[2]
    per_node = rows // BR
    for s in range(nodes):
        update = jnp.dot(off_ref[s], low_ref[s].astype(BF16), preferred_element_type=F32)
        table_ref[pl.ds(s * per_node, per_node)] = update.astype(BF16).reshape(per_node, BR, lanes)
    table_ref[nodes * per_node] = jnp.zeros((BR, lanes), BF16)
    index = source_index(h, CAPACITY, source_ref)
    return place(table_ref, index, CAPACITY, staged_ref, out_ref, sems)


def fill_rows(solved, table_ref):
    blocks, _, lanes = table_ref.shape
    per_node = (blocks - 1) // len(solved)
    for s, values in enumerate(solved):
        table_ref[pl.ds(s * per_node, per_node)] = values.astype(BF16).reshape(per_node, BR, lanes)
    table_ref[blocks - 1] = jnp.zeros((BR, lanes), BF16)


def send_rows(h, solved, code_ref, staged_ref, out_ref, table_ref, sems):
    fill_rows(solved, table_ref)
    index = code_index(h, CAPACITY, code_ref)
    return place(table_ref, index, CAPACITY, staged_ref, out_ref, sems)


def place_rows(h, solved, code_ref, out_ref, table_ref):
    fill_rows(solved, table_ref)
    index = code_index(h, CAPACITY, code_ref)
    place_chunk(table_ref, index, CAPACITY, out_ref, 0, out_ref.shape[0] // CAPACITY)


def fetch(pairs, sems):
    copies = [pltpu.make_async_copy(a, b, sems.at[i]) for i, (a, b) in enumerate(pairs)]
    for copy in copies:
        copy.start()
    return copies


def store(source, target, sem):
    copy = pltpu.make_async_copy(source, target, sem)
    copy.start()
    return copy


def finish(copies):
    for copy in copies:
        copy.wait()


def add_blocks(inbound_ref, index, sum_refs, start, peers):
    step = len(sum_refs) // CAPACITY

    def body(g, _):
        for e in range(step):
            d = g * step + e
            for i in range(CAPACITY):
                sum_ref = sum_refs[e * CAPACITY + i]
                code = index(d, i)
                sum_ref[code] = sum_ref[code] + inbound_ref[d * CAPACITY + i].astype(F32)
        return 0

    lax.fori_loop(start // step, (start + peers) // step, body, 0, unroll=2)


def diag_copies(place_ref, own_hbm, part_hbms, diag_ref):
    sources = [own_hbm] + list(part_hbms)
    return [(source, diag_ref.at[place_ref[i]]) for i, source in enumerate(sources)]


def lower_solve(inbound_hbm, inbound_ref, index, sum_refs, diag_ref, rhs_ref, others, sems):
    nodes, order, lanes = rhs_ref.shape
    chunks = 4
    size = inbound_ref.shape[0] // chunks
    pairs = []
    for c in range(chunks):
        part = pl.ds(c * size, size)
        pairs.append((inbound_hbm.at[part], inbound_ref.at[part]))
    copies = fetch(pairs + others, sems)
    for sum_ref in sum_refs:
        sum_ref[...] = jnp.zeros_like(sum_ref)
    for c in range(chunks):
        copies[c].wait()
        add_blocks(inbound_ref, index, sum_refs, c * size // CAPACITY, size // CAPACITY)
    rest = copies[chunks:]
    finish(rest[:NEEDED])
    blocks = order // BR
    solved = []
    for s in range(nodes):
        part = pl.ds(s * blocks, blocks)
        total = sum(sum_ref[part] for sum_ref in sum_refs).reshape(order, lanes)
        solved.append(solve(whole_diag(diag_ref, s), rhs_ref[s] - total))
    return solved, rest[NEEDED:]


NEEDED = 5


def first_kernel(
    source_ref,
    place_ref,
    diag_hbm,
    part1_hbm,
    part2_hbm,
    part3_hbm,
    rhs_hbm,
    off_hbm,
    low_hbm,
    whole_hbm,
    out_hbm,
    diag_ref,
    rhs_ref,
    off_ref,
    low_ref,
    table_ref,
    staged_ref,
    in_sems,
    keep_sems,
    out_sems,
):
    pairs = diag_copies(place_ref, diag_hbm.at[0], [part1_hbm, part2_hbm, part3_hbm], diag_ref)
    pairs += [(rhs_hbm.at[0], rhs_ref), (off_hbm.at[0], off_ref)]
    copies = fetch(pairs, in_sems)
    finish(copies[:NEEDED])
    kept = [store(diag_ref, whole_hbm, keep_sems.at[0])]
    for s in range(rhs_ref.shape[0]):
        low_ref[s] = solve(whole_diag(diag_ref, s), rhs_ref[s])
    kept.append(store(low_ref, low_hbm, keep_sems.at[1]))
    finish(copies[NEEDED:])
    kept += send_updates(0, low_ref, off_ref, source_ref, staged_ref, out_hbm, table_ref, out_sems)
    finish(kept)


def middle_kernel(
    h,
    source_ref,
    place_ref,
    code_ref,
    inbound_hbm,
    diag_hbm,
    part1_hbm,
    part2_hbm,
    part3_hbm,
    rhs_hbm,
    off_hbm,
    low_hbm,
    whole_hbm,
    out_hbm,
    sum0_ref,
    sum1_ref,
    sum2_ref,
    sum3_ref,
    inbound_ref,
    diag_ref,
    rhs_ref,
    off_ref,
    low_ref,
    table_ref,
    staged_ref,
    in_sems,
    keep_sems,
    out_sems,
):
    pairs = diag_copies(place_ref, diag_hbm.at[h], [part1_hbm, part2_hbm, part3_hbm], diag_ref)
    pairs += [(rhs_hbm.at[h], rhs_ref), (off_hbm.at[h], off_ref)]
    sums = [sum0_ref, sum1_ref, sum2_ref, sum3_ref]
    index = code_index(h - 1, CAPACITY, code_ref)
    solved, late = lower_solve(
        inbound_hbm, inbound_ref, index, sums, diag_ref, rhs_ref, pairs, in_sems
    )
    kept = [store(diag_ref, whole_hbm, keep_sems.at[0])]
    for s, values in enumerate(solved):
        low_ref[s] = values
    kept.append(store(low_ref, low_hbm, keep_sems.at[1]))
    finish(late)
    kept += send_updates(h, low_ref, off_ref, source_ref, staged_ref, out_hbm, table_ref, out_sems)
    finish(kept)


def top_kernel(
    h,
    place_ref,
    code_ref,
    inbound_hbm,
    diag_hbm,
    part1_hbm,
    part2_hbm,
    part3_hbm,
    rhs_hbm,
    answer_hbm,
    out_hbm,
    sum0_ref,
    sum1_ref,
    sum2_ref,
    sum3_ref,
    inbound_ref,
    diag_ref,
    rhs_ref,
    sol_ref,
    table_ref,
    staged_ref,
    in_sems,
    keep_sems,
    out_sems,
):
    pairs = diag_copies(place_ref, diag_hbm.at[h], [part1_hbm, part2_hbm, part3_hbm], diag_ref)
    pairs += [(rhs_hbm.at[h], rhs_ref)]
    sums = [sum0_ref, sum1_ref, sum2_ref, sum3_ref]
    index = code_index(h - 1, CAPACITY, code_ref)
    solved, _ = lower_solve(
        inbound_hbm, inbound_ref, index, sums, diag_ref, rhs_ref, pairs, in_sems
    )
    for s, lower in enumerate(solved):
        solved[s] = solve_transposed(whole_diag(diag_ref, s), lower)
        sol_ref[s] = solved[s]
    kept = [store(sol_ref, answer_hbm.at[h], keep_sems.at[0])]
    kept += send_rows(h - 1, solved, code_ref, staged_ref, out_hbm, table_ref, out_sems)
    finish(kept)


def upper_solve(
    h, dest_ref, inbound_ref, diag_hbm, off_hbm, low_hbm, diag_ref, off_ref, low_ref, sol_ref, rows_ref, sems
):
    pairs = [(off_hbm.at[h], off_ref), (low_hbm, low_ref), (diag_hbm, diag_ref)]
    get_off, get_low, get_diag = fetch(pairs, sems)
    nodes, rows, _ = off_ref.shape
    per_node = rows // BR
    lanes = low_ref.shape[2]

    def body(k, _):
        rows_ref[k] = inbound_ref[dest_ref[h, k]]
        return 0

    lax.fori_loop(0, nodes * per_node, body, 0, unroll=8)
    get_off.wait()
    taken = []
    for s in range(nodes):
        block_rows = rows_ref[pl.ds(s * per_node, per_node)].reshape(rows, lanes)
        taken.append(
            lax.dot_general(
                off_ref[s], block_rows, (((0,), (0,)), ((), ())), preferred_element_type=F32
            )
        )
    finish([get_low, get_diag])
    solved = []
    for s in range(nodes):
        solved.append(solve_transposed(whole_diag(diag_ref, s), low_ref[s] - taken[s]))
        sol_ref[s] = solved[s]
    return solved


def upper_kernel(
    h,
    dest_ref,
    code_ref,
    inbound_ref,
    diag_hbm,
    off_hbm,
    low_hbm,
    _,
    answer_hbm,
    out_ref,
    diag_ref,
    off_ref,
    low_ref,
    sol_ref,
    rows_ref,
    table_ref,
    sems,
):
    solved = upper_solve(
        h, dest_ref, inbound_ref, diag_hbm, off_hbm, low_hbm,
        diag_ref, off_ref, low_ref, sol_ref, rows_ref, sems,
    )
    kept = store(sol_ref, answer_hbm.at[h], sems.at[3])
    place_rows(h - 1, solved, code_ref, out_ref, table_ref)
    kept.wait()


def last_kernel(
    dest_ref,
    inbound_ref,
    diag_hbm,
    off_hbm,
    low_hbm,
    _,
    answer_hbm,
    diag_ref,
    off_ref,
    low_ref,
    sol_ref,
    rows_ref,
    sems,
):
    upper_solve(
        0, dest_ref, inbound_ref, diag_hbm, off_hbm, low_hbm,
        diag_ref, off_ref, low_ref, sol_ref, rows_ref, sems,
    )
    store(sol_ref, answer_hbm.at[0], sems.at[3]).wait()


def scalar(x):
    return x, pl.BlockSpec(memory_space=pltpu.SMEM)


def whole(x):
    return x, pl.BlockSpec(memory_space=pltpu.VMEM)


def far(x):
    return x, pl.BlockSpec(memory_space=pltpu.HBM)


def anywhere(x):
    return x, pl.BlockSpec(memory_space=pl.ANY)


def call(kernel, name, operands, outs, scratch, flops, aliases={}, limit=None):
    arrays = [x for x, _ in operands]
    moved = sum(x.size * x.dtype.itemsize for x, _ in operands + outs)
    return pl.pallas_call(
        kernel,
        name=name,
        out_shape=[jax.ShapeDtypeStruct(x.shape, x.dtype) for x, _ in outs],
        in_specs=[spec for _, spec in operands],
        out_specs=[spec for _, spec in outs],
        scratch_shapes=scratch,
        input_output_aliases=aliases,
        compiler_params=pltpu.CompilerParams(vmem_limit_bytes=limit),
        cost_estimate=pl.CostEstimate(flops=flops, bytes_accessed=moved, transcendentals=0),
    )(*arrays)


def on_device(right_sides, diag_inverse, off_diagonal, target_snode, target_block):
    levels, nodes, order, lanes = right_sides.shape
    per_node = target_snode.shape[2]
    row_blocks = order // BR
    devices = lax.axis_size("snode")
    sharers = lax.axis_size("rhs")
    outgoing = nodes * per_node
    capacity = CAPACITY
    slots = devices * capacity
    local_rows = nodes * row_blocks
    couplings = levels - 1

    def diag_parts(mine):
        steps = [[(y, (y + k) % sharers) for y in range(sharers)] for k in range(1, sharers)]
        return [lax.ppermute(mine, "rhs", step) for step in steps]

    mine = lax.axis_index("rhs")
    places = (mine - lax.iota(jnp.int32, sharers)) % sharers

    parts = [diag_parts(diag_inverse[0])]

    block_order = lax.iota(jnp.int32, outgoing)
    flat_target = target_snode.reshape(couplings, outgoing)
    owner = flat_target // nodes
    row = flat_target % nodes * row_blocks + target_block.reshape(couplings, outgoing)
    earlier = (owner[:, :, None] == owner[:, None, :]) & (
        block_order[None, None, :] < block_order[None, :, None]
    )
    destinations = owner * capacity + jnp.sum(earlier.astype(jnp.int32), axis=2)
    slot_ids = lax.iota(jnp.int32, slots)
    placed = destinations[:, None, :] == slot_ids[None, :, None]
    sources = jnp.min(jnp.where(placed, block_order[None, None, :], outgoing), axis=2)
    ids = slot_ids.reshape(devices, 1, capacity, 1)
    placed = destinations[None, :, None, :] == ids
    sent = jnp.min(jnp.where(placed, row[None, :, None, :], local_rows), axis=3)

    def exchange(x):
        return lax.all_to_all(x, "snode", split_axis=0, concat_axis=0, tiled=True)

    vector = far(jax.ShapeDtypeStruct((nodes, order, lanes), F32))
    payload = far(jax.ShapeDtypeStruct((slots, BR, lanes), BF16))
    near_payload = whole(payload[0])
    gathered = far(jax.ShapeDtypeStruct((sharers,) + diag_inverse.shape[1:], F32))
    answer = jax.ShapeDtypeStruct(right_sides.shape, F32)
    four = pltpu.SemaphoreType.DMA((4,))
    two = pltpu.SemaphoreType.DMA((2,))
    inputs = pltpu.SemaphoreType.DMA((12,))
    vectors = pltpu.VMEM((nodes, order, lanes), F32)
    off_buffer = pltpu.VMEM(off_diagonal.shape[1:], BF16)
    diag_buffer = pltpu.VMEM(gathered[0].shape, F32)
    sums = [pltpu.VMEM((local_rows + 1, BR, lanes), F32)] * 4
    table = pltpu.VMEM((outgoing + 1, BR, lanes), BF16)
    row_table = pltpu.VMEM((local_rows + 1, BR, lanes), BF16)
    rows_scratch = pltpu.VMEM((outgoing, BR, lanes), BF16)
    blocks_buffer = pltpu.VMEM((slots, BR, lanes), BF16)
    send = [blocks_buffer, inputs, two, pltpu.SemaphoreType.DMA((4,))]
    flops = 40 * nodes * order * order * lanes
    small = 24 << 20

    def diag_operands(h):
        return [far(diag_inverse)] + [far(x) for x in parts[h]]

    lower, whole_diags = [None] * couplings, [None] * couplings
    lower[0], whole_diags[0], out = call(
        first_kernel,
        "first",
        [scalar(sources), scalar(places)]
        + diag_operands(0)
        + [far(right_sides), far(off_diagonal)],
        [vector, gathered, payload],
        [diag_buffer, vectors, off_buffer, vectors, table] + send,
        flops,
    )
    later_diags, out = lax.optimization_barrier((diag_inverse, out))
    pairs_of_rows = capacity * BR // 2
    carried = sent.reshape(devices, 1, 1, couplings * capacity).astype(BF16)
    carried = jnp.pad(carried, ((0, 0), (0, 0), (0, 1), (0, lanes - couplings * capacity)))
    out = jnp.concatenate([out.reshape(devices, pairs_of_rows, 2, lanes), carried], axis=1)
    inbound = exchange(out)
    codes = inbound[:, pairs_of_rows, 0, : couplings * capacity].astype(jnp.int32).T
    inbound = inbound[:, :pairs_of_rows].reshape(slots, BR, lanes)

    for h in range(1, couplings):
        parts.append(diag_parts(later_diags[h]))
        lower[h], whole_diags[h], out = call(
            functools.partial(middle_kernel, h),
            "middle",
            [scalar(sources), scalar(places), scalar(codes), far(inbound)]
            + diag_operands(h)
            + [far(right_sides), far(off_diagonal)],
            [vector, gathered, payload],
            sums + [blocks_buffer, diag_buffer, vectors, off_buffer, vectors, table] + send,
            flops,
        )
        inbound = exchange(out)
    top = couplings
    parts.append(diag_parts(later_diags[top]))
    answer, out = call(
        functools.partial(top_kernel, top),
        "top",
        [scalar(places), scalar(codes), far(inbound)]
        + diag_operands(top)
        + [far(right_sides)],
        [far(answer), payload],
        sums + [blocks_buffer, diag_buffer, vectors, vectors, row_table] + send,
        flops,
    )
    inbound = exchange(out)
    for h in range(couplings - 1, 0, -1):
        answer, out = call(
            functools.partial(upper_kernel, h),
            "upper",
            [scalar(destinations), scalar(codes), whole(inbound), anywhere(whole_diags[h])]
            + [anywhere(off_diagonal), anywhere(lower[h]), anywhere(answer)],
            [anywhere(answer), near_payload],
            [diag_buffer, off_buffer, vectors, vectors, rows_scratch, row_table, four],
            flops,
            {6: 0},
            small,
        )
        inbound = exchange(out)
    (answer,) = call(
        last_kernel,
        "last",
        [scalar(destinations), whole(inbound), anywhere(whole_diags[0])]
        + [anywhere(off_diagonal), anywhere(lower[0]), anywhere(answer)],
        [anywhere(answer)],
        [diag_buffer, off_buffer, vectors, vectors, rows_scratch, four],
        flops,
        {5: 0},
        small,
    )
    return answer


def solution(mesh):
    in_specs = (
        P(None, "snode", None, "rhs"),
        P(None, "snode", "rhs", None),
        P(None, "snode", None, None),
        P(None, "snode", None),
        P(None, "snode", None),
    )
    out_specs = P(None, "snode", None, "rhs")
    return jax.shard_map(
        on_device, mesh=mesh, in_specs=in_specs, out_specs=out_specs, check_vma=False
    )
```

time: 320 us -> 310 us (0.969)
  blocking collectives: 62 us -> 124 us
  waiting for transfers between devices: 154 us -> 102 us
  starting transfers between devices: 69.3 us -> 50.9 us
    all_to_all x1 -> x2, blocking collectives: 62 us -> 124 us  [exchange(): return lax.all_to_all(x, 'snode', split_axis=0, concat_axis=0, tiled=True)]
    all_to_all x4 -> x2, waiting for transfers between devices: 148 us -> 93.6 us  [exchange(): return lax.all_to_all(x, 'snode', split_axis=0, concat_axis=0, tiled=True)]
    all_to_all x4 -> x2, starting transfers between devices: 41.4 us -> 26.5 us  [exchange(): return lax.all_to_all(x, 'snode', split_axis=0, concat_axis=0, tiled=True)]
    ppermute x9, starting transfers between devices: 27.9 us -> 24.4 us  [diag_parts(): return [lax.ppermute(mine, 'rhs', step) for step in steps]]
  transfers between devices with their start and end apart: 13 -> 11, of which waited for: 7 -> 5; matrix products, arithmetic and copies ran while one was open for 2% -> 2% of each run, Pallas kernels for 1% -> 0%
where the time goes in v5:
time: 310 us
  blocking collectives  124 us (40%)
  waiting for transfers between devices  102 us (33%)
  starting transfers between devices  50.9 us (16%)
  Pallas kernels  20.4 us (7%)
  local copies, waits for them, and re-layouts  6.84 us (2%)
  other arithmetic  5.21 us (2%)
    all_to_all x2, blocking collectives, exchange(): return lax.all_to_all(x, 'snode', split_axis=0, concat_axis=0, tiled=True)  124 us
    all_to_all x2, waiting for transfers between devices, exchange(): return lax.all_to_all(x, 'snode', split_axis=0, concat_axis=0, tiled=True)  93.6 us
    all_to_all x2, starting transfers between devices, exchange(): return lax.all_to_all(x, 'snode', split_axis=0, concat_axis=0, tiled=True)  26.5 us
    ppermute x9, starting transfers between devices, diag_parts(): return [lax.ppermute(mine, 'rhs', step) for step in steps]  24.4 us
    pallas_call x5, Pallas kernels, call(): pl.pallas_call(kernel, name=name, out_shape=[jax.ShapeDtypeStruct(x.shape...  20.4 us
    ppermute x9, waiting for transfers between devices, diag_parts(): return [lax.ppermute(mine, 'rhs', step) for step in steps]  7.91 us
  transfers between devices with their start and end apart: 11, of which 5 were waited for; matrix products, arithmetic and copies ran while one was open for 2% of the time, Pallas kernels for 0%

profile of v5, /device:TPU:33, one launch (start us, length us, event | category | flops | bytes accessed | tf_op | source)
XLA Modules:
  0.0 309.6 jit_solution(280240481417995941)
XLA Ops:
  0.0 0.9 slice_bitcast_fusion.2
  0.9 4.6 %collective-permute-start.2 = (f32[2,64,256]{2,1,0:T(8,128)S(1)}, f32[2,64,256]{2,1,0:T(8,128)S(1)}, u32[]{:S(2)}, u32[]{:S(2)}) collective-permute-start(f32[2,64,256]{2,1,0:T(8,128)S(1)} %slice_bitcast_fusion.2), channel_id=1, source_target_pairs={{0,3},{1,0},{2,1},{3,2},{4,7},{5,4},{6,5},{7,6},{8,11},{9,8},{10,9... | collective-permute-start | bytes 393224 | tf_op jit(solution)/shard_map/ppermute | solution.py:410
  5.6 2.3 collective-permute-start.1
  7.8 2.6 collective-permute-start
  10.5 0.8 reshape.191
  11.2 0.8 reshape.196
  12.0 0.2 convert_reduce_fusion
  12.2 0.2 select_reduce_fusion
  12.4 0.5 and_select_fusion.1.place_ref
  13.0 0.1 copy.13
  13.1 0.7 select_reduce_fusion.1.source_ref
  13.8 0.0 collective-permute-done.2.part3_hbm
  13.8 0.0 collective-permute-done.1.part2_hbm
  13.8 2.6 collective-permute-done.part1_hbm
  16.5 0.7 copy-done.10
  17.1 4.5 %first.1 = (f32[2,256,128]{2,1,0:T(8,128)}, f32[4,2,64,256]{3,2,1,0:T(8,128)}, bf16[256,16,128]{2,1,0:T(8,128)(2,1)}) custom-call(s32[2,256]{1,0:T(2,128)} %select_reduce_fusion.1.source_ref, s32[4]{0:T(128)} %and_select_fusion.1.place_ref, f32[3,2,64,256]{3,2,1,0:T(8,128)} %diag_hbm.5, f32[2,64,256]{2,1,0:T(8,128)} %copy-done.10, f32[2,64,256]{2,1,0:T(8,128)} %copy-done.9, ...), custom_call_target="tpu_custom_call" | custom-call | flops 671088640 | bytes 5507088 | tf_op jit(solution)/shard_map/first/pallas_call | solution.py:383
  21.6 2.9 fusion
  24.6 20.0 %all-to-all-start = ((bf16[128,17,2,128]{3,2,1,0:T(2,128)(2,1)}), bf16[128,17,2,128]{3,2,1,0:T(2,128)(2,1)S(1)}, u32[]{:S(2)}, u32[]{:S(2)}) async-start(bf16[128,17,2,128]{3,2,1,0:T(2,128)(2,1)} %fusion), calls=%async_computation | async-start | bytes 2228224 | tf_op jit(solution)/shard_map/all_to_all | solution.py:433
  44.6 2.2 collective-permute-start.5
  46.8 3.3 %collective-permute-start.4 = (f32[2,64,256]{2,1,0:T(8,128)S(1)}, f32[2,64,256]{2,1,0:T(8,128)S(1)}, u32[]{:S(2)}, u32[]{:S(2)}) collective-permute-start(f32[2,64,256]{2,1,0:T(8,128)S(1)} %get-tuple-element.30), channel_id=1, source_target_pairs={{0,2},{1,3},{2,0},{3,1},{4,6},{5,7},{6,4},{7,5},{8,10},{9,11},{10,... | collective-permute-start | bytes 393224 | tf_op jit(solution)/shard_map/ppermute | solution.py:410
  50.2 1.9 collective-permute-start.3
  52.1 50.8 %all-to-all-done = bf16[128,17,2,128]{3,2,1,0:T(2,128)(2,1)S(1)} async-done(((bf16[128,17,2,128]{3,2,1,0:T(2,128)(2,1)}), bf16[128,17,2,128]{3,2,1,0:T(2,128)(2,1)S(1)}, u32[]{:S(2)}, u32[]{:S(2)}) %all-to-all-start) | async-done | bytes 1114144 | tf_op jit(solution)/shard_map/all_to_all | solution.py:433
  103.0 0.1 copy.15
  103.1 1.7 slice.21
  104.8 0.6 convert_bitcast_fusion.code_ref
  105.4 0.0 collective-permute-done.5.part3_hbm
  105.4 0.0 collective-permute-done.4.part2_hbm
  105.4 0.0 collective-permute-done.3.part1_hbm
  105.4 0.0 copy-start.13
  105.4 0.6 copy-done.11
  106.0 0.0 copy-done.12
  106.0 0.1 copy-done.13
  106.1 5.0 %middle.1 = (f32[2,256,128]{2,1,0:T(8,128)}, f32[4,2,64,256]{3,2,1,0:T(8,128)}, bf16[256,16,128]{2,1,0:T(8,128)(2,1)}) custom-call(s32[2,256]{1,0:T(2,128)} %select_reduce_fusion.1.source_ref, s32[4]{0:T(128)} %and_select_fusion.1.place_ref, s32[4,128]{1,0:T(4,128)} %convert_bitcast_fusion.code_ref, bf16[256,16,128]{2,1,0:T(8,128)(2,1)} %bitcast.14, ...), custom_call_target="tpu_custom_call" | custom-call | flops 671088640 | bytes 6557712 | tf_op jit(solution)/shard_map/middle/pallas_call | solution.py:383
  111.1 6.5 %all-to-all-start.1 = ((bf16[256,16,128]{2,1,0:T(8,128)(2,1)}), bf16[256,16,128]{2,1,0:T(8,128)(2,1)S(1)}, u32[]{:S(2)}, u32[]{:S(2)}) async-start(bf16[256,16,128]{2,1,0:T(8,128)(2,1)} %get-tuple-element.20), calls=%async_computation.1 | async-start | bytes 2097152 | tf_op jit(solution)/shard_map/all_to_all | solution.py:433
  117.6 2.2 collective-permute-start.8
  119.8 3.3 %collective-permute-start.7 = (f32[2,64,256]{2,1,0:T(8,128)S(1)}, f32[2,64,256]{2,1,0:T(8,128)S(1)}, u32[]{:S(2)}, u32[]{:S(2)}) collective-permute-start(f32[2,64,256]{2,1,0:T(8,128)S(1)} %get-tuple-element.29), channel_id=1, source_target_pairs={{0,2},{1,3},{2,0},{3,1},{4,6},{5,7},{6,4},{7,5},{8,10},{9,11},{10,... | collective-permute-start | bytes 393224 | tf_op jit(solution)/shard_map/ppermute | solution.py:410
  123.1 1.9 collective-permute-start.6
  125.1 0.0 collective-permute-done.8.part3_hbm
  125.1 2.5 collective-permute-done.7.part2_hbm
  127.6 2.8 collective-permute-done.6.part1_hbm
  130.4 42.8 %all-to-all-done.1.inbound_hbm = bf16[256,16,128]{2,1,0:T(8,128)(2,1)S(1)} async-done(((bf16[256,16,128]{2,1,0:T(8,128)(2,1)}), bf16[256,16,128]{2,1,0:T(8,128)(2,1)S(1)}, u32[]{:S(2)}, u32[]{:S(2)}) %all-to-all-start.1) | async-done | bytes 1048608 | tf_op jit(solution)/shard_map/all_to_all | solution.py:433
  173.2 1.0 copy-done.7
  174.2 5.1 %top.1 = (f32[3,2,256,128]{3,2,1,0:T(8,128)}, bf16[256,16,128]{2,1,0:T(8,128)(2,1)}) custom-call(s32[4]{0:T(128)} %and_select_fusion.1.place_ref, s32[4,128]{1,0:T(4,128)} %convert_bitcast_fusion.code_ref, bf16[256,16,128]{2,1,0:T(8,128)(2,1)} %copy-done.7, f32[3,2,64,256]{3,2,1,0:T(8,128)} %diag_hbm.5, f32[2,64,256]{2,1,0:T(8,128)} %copy-done.16, ...), custom_call_target="tpu_custom_call" | custom-call | flops 671088640 | bytes 4458512 | tf_op jit(solution)/shard_map/top/pallas_call | solution.py:383
  179.3 0.0 copy-start
  179.3 62.2 %all_to_all.20.inbound_ref = bf16[256,16,128]{2,1,0:T(8,128)(2,1)S(1)} all-to-all(bf16[256,16,128]{2,1,0:T(8,128)(2,1)} %get-tuple-element.21), channel_id=1, replica_groups=mesh['snode'=128,'rhs'=4] {'snode'}, dimensions={0} | all-to-all | bytes 2097152 | tf_op jit(solution)/shard_map/all_to_all | solution.py:433
  241.6 3.0 upper.1
  244.6 62.0 %all_to_all.21.inbound_ref = bf16[256,16,128]{2,1,0:T(8,128)(2,1)S(1)} all-to-all(bf16[256,16,128]{2,1,0:T(8,128)(2,1)S(1)} %get-tuple-element.25), channel_id=1, replica_groups=mesh['snode'=128,'rhs'=4] {'snode'}, dimensions={0} | all-to-all | bytes 2097152 | tf_op jit(solution)/shard_map/all_to_all | solution.py:433
  306.6 2.8 last.1
  (34 shorter events, 0.2 us)
Async XLA Ops:
  0.9 12.9 %collective-permute-start.2 = (f32[2,64,256]{2,1,0:T(8,128)S(1)}, f32[2,64,256]{2,1,0:T(8,128)S(1)}, u32[]{:S(2)}, u32[]{:S(2)}) collective-permute-start(f32[2,64,256]{2,1,0:T(8,128)S(1)} %slice_bitcast_fusion.2), channel_id=1, source_target_pairs={{0,3},{1,0},{2,1},{3,2},{4,7},{5,4},{6,5},{7,6},{8,11},{9,8},{10,9... | collective-permute-start | bytes 393224 | tf_op jit(solution)/shard_map/ppermute | solution.py:410
  5.6 8.3 %collective-permute-start.1 = (f32[2,64,256]{2,1,0:T(8,128)S(1)}, f32[2,64,256]{2,1,0:T(8,128)S(1)}, u32[]{:S(2)}, u32[]{:S(2)}) collective-permute-start(f32[2,64,256]{2,1,0:T(8,128)S(1)} %slice_bitcast_fusion.2), channel_id=1, source_target_pairs={{0,2},{1,3},{2,0},{3,1},{4,6},{5,7},{6,4},{7,5},{8,10},{9,11},{10,... | collective-permute-start | bytes 393224 | tf_op jit(solution)/shard_map/ppermute | solution.py:410
  7.8 8.6 %collective-permute-start = (f32[2,64,256]{2,1,0:T(8,128)S(1)}, f32[2,64,256]{2,1,0:T(8,128)S(1)}, u32[]{:S(2)}, u32[]{:S(2)}) collective-permute-start(f32[2,64,256]{2,1,0:T(8,128)S(1)} %slice_bitcast_fusion.2), channel_id=1, source_target_pairs={{0,1},{1,2},{2,3},{3,0},{4,5},{5,6},{6,7},{7,4},{8,9},{9,10},{10,1... | collective-permute-start | bytes 393224 | tf_op jit(solution)/shard_map/ppermute | solution.py:410
  13.8 2.6 copy-start.8
  13.8 2.6 copy-start.9
  16.5 0.7 copy-start.10
  24.6 20.0 %copy-start.6 = (f32[3,2,64,256]{3,2,1,0:T(8,128)S(1)}, f32[3,2,64,256]{3,2,1,0:T(8,128)}, u32[]{:S(2)}) copy-start(f32[3,2,64,256]{3,2,1,0:T(8,128)} %diag_hbm.5) | copy-start | bytes 1179652
  24.6 78.4 %all-to-all-start = ((bf16[128,17,2,128]{3,2,1,0:T(2,128)(2,1)}), bf16[128,17,2,128]{3,2,1,0:T(2,128)(2,1)S(1)}, u32[]{:S(2)}, u32[]{:S(2)}) async-start(bf16[128,17,2,128]{3,2,1,0:T(2,128)(2,1)} %fusion), calls=%async_computation | async-start | bytes 2228224 | tf_op jit(solution)/shard_map/all_to_all | solution.py:433
  44.6 60.8 %collective-permute-start.5 = (f32[2,64,256]{2,1,0:T(8,128)S(1)}, f32[2,64,256]{2,1,0:T(8,128)S(1)}, u32[]{:S(2)}, u32[]{:S(2)}) collective-permute-start(f32[2,64,256]{2,1,0:T(8,128)S(1)} %get-tuple-element.30), channel_id=1, source_target_pairs={{0,3},{1,0},{2,1},{3,2},{4,7},{5,4},{6,5},{7,6},{8,11},{9,8},{10,9... | collective-permute-start | bytes 393224 | tf_op jit(solution)/shard_map/ppermute | solution.py:410
  46.8 58.5 %collective-permute-start.4 = (f32[2,64,256]{2,1,0:T(8,128)S(1)}, f32[2,64,256]{2,1,0:T(8,128)S(1)}, u32[]{:S(2)}, u32[]{:S(2)}) collective-permute-start(f32[2,64,256]{2,1,0:T(8,128)S(1)} %get-tuple-element.30), channel_id=1, source_target_pairs={{0,2},{1,3},{2,0},{3,1},{4,6},{5,7},{6,4},{7,5},{8,10},{9,11},{10,... | collective-permute-start | bytes 393224 | tf_op jit(solution)/shard_map/ppermute | solution.py:410
  50.2 55.2 %collective-permute-start.3 = (f32[2,64,256]{2,1,0:T(8,128)S(1)}, f32[2,64,256]{2,1,0:T(8,128)S(1)}, u32[]{:S(2)}, u32[]{:S(2)}) collective-permute-start(f32[2,64,256]{2,1,0:T(8,128)S(1)} %get-tuple-element.30), channel_id=1, source_target_pairs={{0,1},{1,2},{2,3},{3,0},{4,5},{5,6},{6,7},{7,4},{8,9},{9,10},{10,1... | collective-permute-start | bytes 393224 | tf_op jit(solution)/shard_map/ppermute | solution.py:410
  105.4 0.6 copy-start.11
  105.4 0.7 copy-start.12
  105.4 0.7 copy-start.13
  111.1 62.1 %all-to-all-start.1 = ((bf16[256,16,128]{2,1,0:T(8,128)(2,1)}), bf16[256,16,128]{2,1,0:T(8,128)(2,1)S(1)}, u32[]{:S(2)}, u32[]{:S(2)}) async-start(bf16[256,16,128]{2,1,0:T(8,128)(2,1)} %get-tuple-element.20), calls=%async_computation.1 | async-start | bytes 2097152 | tf_op jit(solution)/shard_map/all_to_all | solution.py:433
  117.6 7.5 %collective-permute-start.8 = (f32[2,64,256]{2,1,0:T(8,128)S(1)}, f32[2,64,256]{2,1,0:T(8,128)S(1)}, u32[]{:S(2)}, u32[]{:S(2)}) collective-permute-start(f32[2,64,256]{2,1,0:T(8,128)S(1)} %get-tuple-element.29), channel_id=1, source_target_pairs={{0,3},{1,0},{2,1},{3,2},{4,7},{5,4},{6,5},{7,6},{8,11},{9,8},{10,9... | collective-permute-start | bytes 393224 | tf_op jit(solution)/shard_map/ppermute | solution.py:410
  119.8 7.8 %collective-permute-start.7 = (f32[2,64,256]{2,1,0:T(8,128)S(1)}, f32[2,64,256]{2,1,0:T(8,128)S(1)}, u32[]{:S(2)}, u32[]{:S(2)}) collective-permute-start(f32[2,64,256]{2,1,0:T(8,128)S(1)} %get-tuple-element.29), channel_id=1, source_target_pairs={{0,2},{1,3},{2,0},{3,1},{4,6},{5,7},{6,4},{7,5},{8,10},{9,11},{10,... | collective-permute-start | bytes 393224 | tf_op jit(solution)/shard_map/ppermute | solution.py:410
  123.1 7.2 %collective-permute-start.6 = (f32[2,64,256]{2,1,0:T(8,128)S(1)}, f32[2,64,256]{2,1,0:T(8,128)S(1)}, u32[]{:S(2)}, u32[]{:S(2)}) collective-permute-start(f32[2,64,256]{2,1,0:T(8,128)S(1)} %get-tuple-element.29), channel_id=1, source_target_pairs={{0,1},{1,2},{2,3},{3,0},{4,5},{5,6},{6,7},{7,4},{8,9},{9,10},{10,1... | collective-permute-start | bytes 393224 | tf_op jit(solution)/shard_map/ppermute | solution.py:410
  125.1 48.1 %copy-start.14 = (f32[2,64,256]{2,1,0:T(8,128)}, f32[2,64,256]{2,1,0:T(8,128)S(1)}, u32[]{:S(2)}) copy-start(f32[2,64,256]{2,1,0:T(8,128)S(1)} %collective-permute-done.8.part3_hbm) | copy-start | bytes 393220
  127.6 45.6 %copy-start.15 = (f32[2,64,256]{2,1,0:T(8,128)}, f32[2,64,256]{2,1,0:T(8,128)S(1)}, u32[]{:S(2)}) copy-start(f32[2,64,256]{2,1,0:T(8,128)S(1)} %collective-permute-done.7.part2_hbm) | copy-start | bytes 393220
  130.4 42.8 %copy-start.16 = (f32[2,64,256]{2,1,0:T(8,128)}, f32[2,64,256]{2,1,0:T(8,128)S(1)}, u32[]{:S(2)}) copy-start(f32[2,64,256]{2,1,0:T(8,128)S(1)} %collective-permute-done.6.part1_hbm) | copy-start | bytes 393220
  173.2 1.0 copy-start.7
  174.2 67.4 %copy-start.2 = (f32[4,2,64,256]{3,2,1,0:T(8,128)S(1)}, f32[4,2,64,256]{3,2,1,0:T(8,128)}, u32[]{:S(2)}) copy-start(f32[4,2,64,256]{3,2,1,0:T(8,128)} %get-tuple-element.22.diag_hbm) | copy-start | bytes 1572868
  174.2 67.4 %copy-start.4 = (f32[2,256,128]{2,1,0:T(8,128)S(1)}, f32[2,256,128]{2,1,0:T(8,128)}, u32[]{:S(2)}) copy-start(f32[2,256,128]{2,1,0:T(8,128)} %get-tuple-element.23.low_hbm) | copy-start | bytes 786436
  179.3 62.2 %copy-start = (bf16[2,2,1024,256]{3,2,1,0:T(8,128)(2,1)S(1)}, bf16[2,2,1024,256]{3,2,1,0:T(8,128)(2,1)}, u32[]{:S(2)}) copy-start(bf16[2,2,1024,256]{3,2,1,0:T(8,128)(2,1)} %off_hbm.7) | copy-start | bytes 6291460
  179.3 62.2 %copy-start.5 = (s32[4,128]{1,0:T(4,128)S(1)}, s32[4,128]{1,0:T(4,128)}, u32[]{:S(2)}) copy-start(s32[4,128]{1,0:T(4,128)} %convert_bitcast_fusion.code_ref) | copy-start | bytes 6148
  244.6 62.0 %copy-start.1 = (f32[4,2,64,256]{3,2,1,0:T(8,128)S(1)}, f32[4,2,64,256]{3,2,1,0:T(8,128)}, u32[]{:S(2)}) copy-start(f32[4,2,64,256]{3,2,1,0:T(8,128)} %get-tuple-element.26.diag_hbm) | copy-start | bytes 1572868
  244.6 62.0 %copy-start.3 = (f32[2,256,128]{2,1,0:T(8,128)S(1)}, f32[2,256,128]{2,1,0:T(8,128)}, u32[]{:S(2)}) copy-start(f32[2,256,128]{2,1,0:T(8,128)} %get-tuple-element.27.low_hbm) | copy-start | bytes 786436

commit v6 on v5

--- a/solution.py
+++ b/solution.py
@@ -49,7 +49,7 @@
             out_ref[d * capacity + i] = table_ref[index(d, i)]
         return 0
 
-    lax.fori_loop(start, start + peers, body, 0, unroll=4)
+    lax.fori_loop(start, start + peers, body, 0, unroll=16)
 
 
 def source_index(h, capacity, source_ref):
@@ -122,15 +122,20 @@
                 sum_ref[code] = sum_ref[code] + inbound_ref[d * CAPACITY + i].astype(F32)
         return 0
 
-    lax.fori_loop(start // step, (start + peers) // step, body, 0, unroll=2)
-
-
-def diag_copies(place_ref, own_hbm, part_hbms, diag_ref):
+    lax.fori_loop(start // step, (start + peers) // step, body, 0, unroll=4)
+
+
+def diag_copies(own_hbm, part_hbms, diag_ref):
+    sharers = diag_ref.shape[0]
+    mine = lax.axis_index("rhs")
     sources = [own_hbm] + list(part_hbms)
-    return [(source, diag_ref.at[place_ref[i]]) for i, source in enumerate(sources)]
-
-
-def lower_solve(inbound_hbm, inbound_ref, index, sum_refs, diag_ref, rhs_ref, others, sems):
+    return [
+        (source, diag_ref.at[lax.rem(mine + (sharers - i), sharers)])
+        for i, source in enumerate(sources)
+    ]
+
+
+def lower_solve(code_hbm, code_ref, inbound_hbm, inbound_ref, index, sum_refs, diag_ref, rhs_ref, others, sems):
     nodes, order, lanes = rhs_ref.shape
     chunks = 4
     size = inbound_ref.shape[0] // chunks
@@ -138,9 +143,11 @@
     for c in range(chunks):
         part = pl.ds(c * size, size)
         pairs.append((inbound_hbm.at[part], inbound_ref.at[part]))
-    copies = fetch(pairs + others, sems)
+    copies = fetch([(code_hbm, code_ref)] + pairs + others, sems)
+    get_code, copies = copies[0], copies[1:]
     for sum_ref in sum_refs:
         sum_ref[...] = jnp.zeros_like(sum_ref)
+    get_code.wait()
     for c in range(chunks):
         copies[c].wait()
         add_blocks(inbound_ref, index, sum_refs, c * size // CAPACITY, size // CAPACITY)
@@ -159,8 +166,7 @@
 
 
 def first_kernel(
-    source_ref,
-    place_ref,
+    source_hbm,
     diag_hbm,
     part1_hbm,
     part2_hbm,
@@ -170,6 +176,7 @@
     low_hbm,
     whole_hbm,
     out_hbm,
+    source_ref,
     diag_ref,
     rhs_ref,
     off_ref,
@@ -180,8 +187,8 @@
     keep_sems,
     out_sems,
 ):
-    pairs = diag_copies(place_ref, diag_hbm.at[0], [part1_hbm, part2_hbm, part3_hbm], diag_ref)
-    pairs += [(rhs_hbm.at[0], rhs_ref), (off_hbm.at[0], off_ref)]
+    pairs = diag_copies(diag_hbm.at[0], [part1_hbm, part2_hbm, part3_hbm], diag_ref)
+    pairs += [(rhs_hbm.at[0], rhs_ref), (off_hbm.at[0], off_ref), (source_hbm, source_ref)]
     copies = fetch(pairs, in_sems)
     finish(copies[:NEEDED])
     kept = [store(diag_ref, whole_hbm, keep_sems.at[0])]
@@ -195,9 +202,8 @@
 
 def middle_kernel(
     h,
-    source_ref,
-    place_ref,
-    code_ref,
+    source_hbm,
+    code_hbm,
     inbound_hbm,
     diag_hbm,
     part1_hbm,
@@ -212,6 +218,8 @@
     sum1_ref,
     sum2_ref,
     sum3_ref,
+    source_ref,
+    code_ref,
     inbound_ref,
     diag_ref,
     rhs_ref,
@@ -223,12 +231,13 @@
     keep_sems,
     out_sems,
 ):
-    pairs = diag_copies(place_ref, diag_hbm.at[h], [part1_hbm, part2_hbm, part3_hbm], diag_ref)
-    pairs += [(rhs_hbm.at[h], rhs_ref), (off_hbm.at[h], off_ref)]
+    later = [part_hbm.at[h - 1] for part_hbm in (part1_hbm, part2_hbm, part3_hbm)]
+    pairs = diag_copies(diag_hbm.at[h], later, diag_ref)
+    pairs += [(rhs_hbm.at[h], rhs_ref), (off_hbm.at[h], off_ref), (source_hbm, source_ref)]
     sums = [sum0_ref, sum1_ref, sum2_ref, sum3_ref]
     index = code_index(h - 1, CAPACITY, code_ref)
     solved, late = lower_solve(
-        inbound_hbm, inbound_ref, index, sums, diag_ref, rhs_ref, pairs, in_sems
+        code_hbm, code_ref, inbound_hbm, inbound_ref, index, sums, diag_ref, rhs_ref, pairs, in_sems
     )
     kept = [store(diag_ref, whole_hbm, keep_sems.at[0])]
     for s, values in enumerate(solved):
@@ -241,8 +250,7 @@
 
 def top_kernel(
     h,
-    place_ref,
-    code_ref,
+    code_hbm,
     inbound_hbm,
     diag_hbm,
     part1_hbm,
@@ -255,6 +263,7 @@
     sum1_ref,
     sum2_ref,
     sum3_ref,
+    code_ref,
     inbound_ref,
     diag_ref,
     rhs_ref,
@@ -265,12 +274,13 @@
     keep_sems,
     out_sems,
 ):
-    pairs = diag_copies(place_ref, diag_hbm.at[h], [part1_hbm, part2_hbm, part3_hbm], diag_ref)
+    later = [part_hbm.at[h - 1] for part_hbm in (part1_hbm, part2_hbm, part3_hbm)]
+    pairs = diag_copies(diag_hbm.at[h], later, diag_ref)
     pairs += [(rhs_hbm.at[h], rhs_ref)]
     sums = [sum0_ref, sum1_ref, sum2_ref, sum3_ref]
     index = code_index(h - 1, CAPACITY, code_ref)
     solved, _ = lower_solve(
-        inbound_hbm, inbound_ref, index, sums, diag_ref, rhs_ref, pairs, in_sems
+        code_hbm, code_ref, inbound_hbm, inbound_ref, index, sums, diag_ref, rhs_ref, pairs, in_sems
     )
     for s, lower in enumerate(solved):
         solved[s] = solve_transposed(whole_diag(diag_ref, s), lower)
@@ -281,10 +291,13 @@
 
 
 def upper_solve(
-    h, dest_ref, inbound_ref, diag_hbm, off_hbm, low_hbm, diag_ref, off_ref, low_ref, sol_ref, rows_ref, sems
+    h, scalars, inbound_ref, diag_hbm, off_hbm, low_hbm, diag_ref, off_ref, low_ref, sol_ref, rows_ref, sems
 ):
     pairs = [(off_hbm.at[h], off_ref), (low_hbm, low_ref), (diag_hbm, diag_ref)]
-    get_off, get_low, get_diag = fetch(pairs, sems)
+    dest_ref = scalars[0][1]
+    copies = fetch(scalars + pairs, sems)
+    finish(copies[: len(scalars)])
+    get_off, get_low, get_diag = copies[len(scalars) :]
     nodes, rows, _ = off_ref.shape
     per_node = rows // BR
     lanes = low_ref.shape[2]
@@ -293,7 +306,7 @@
         rows_ref[k] = inbound_ref[dest_ref[h, k]]
         return 0
 
-    lax.fori_loop(0, nodes * per_node, body, 0, unroll=8)
+    lax.fori_loop(0, nodes * per_node, body, 0, unroll=32)
     get_off.wait()
     taken = []
     for s in range(nodes):
@@ -313,8 +326,8 @@
 
 def upper_kernel(
     h,
-    dest_ref,
-    code_ref,
+    dest_hbm,
+    code_hbm,
     inbound_ref,
     diag_hbm,
     off_hbm,
@@ -322,6 +335,8 @@
     _,
     answer_hbm,
     out_ref,
+    dest_ref,
+    code_ref,
     diag_ref,
     off_ref,
     low_ref,
@@ -331,22 +346,23 @@
     sems,
 ):
     solved = upper_solve(
-        h, dest_ref, inbound_ref, diag_hbm, off_hbm, low_hbm,
+        h, [(dest_hbm, dest_ref), (code_hbm, code_ref)], inbound_ref, diag_hbm, off_hbm, low_hbm,
         diag_ref, off_ref, low_ref, sol_ref, rows_ref, sems,
     )
-    kept = store(sol_ref, answer_hbm.at[h], sems.at[3])
+    kept = store(sol_ref, answer_hbm.at[h], sems.at[5])
     place_rows(h - 1, solved, code_ref, out_ref, table_ref)
     kept.wait()
 
 
 def last_kernel(
-    dest_ref,
+    dest_hbm,
     inbound_ref,
     diag_hbm,
     off_hbm,
     low_hbm,
     _,
     answer_hbm,
+    dest_ref,
     diag_ref,
     off_ref,
     low_ref,
@@ -355,14 +371,10 @@
     sems,
 ):
     upper_solve(
-        0, dest_ref, inbound_ref, diag_hbm, off_hbm, low_hbm,
+        0, [(dest_hbm, dest_ref)], inbound_ref, diag_hbm, off_hbm, low_hbm,
         diag_ref, off_ref, low_ref, sol_ref, rows_ref, sems,
     )
-    store(sol_ref, answer_hbm.at[0], sems.at[3]).wait()
-
-
-def scalar(x):
-    return x, pl.BlockSpec(memory_space=pltpu.SMEM)
+    store(sol_ref, answer_hbm.at[0], sems.at[5]).wait()
 
 
 def whole(x):
@@ -409,10 +421,7 @@
         steps = [[(y, (y + k) % sharers) for y in range(sharers)] for k in range(1, sharers)]
         return [lax.ppermute(mine, "rhs", step) for step in steps]
 
-    mine = lax.axis_index("rhs")
-    places = (mine - lax.iota(jnp.int32, sharers)) % sharers
-
-    parts = [diag_parts(diag_inverse[0])]
+    first_parts = diag_parts(diag_inverse[0])
 
     block_order = lax.iota(jnp.int32, outgoing)
     flat_target = target_snode.reshape(couplings, outgoing)
@@ -437,7 +446,10 @@
     near_payload = whole(payload[0])
     gathered = far(jax.ShapeDtypeStruct((sharers,) + diag_inverse.shape[1:], F32))
     answer = jax.ShapeDtypeStruct(right_sides.shape, F32)
-    four = pltpu.SemaphoreType.DMA((4,))
+    six = pltpu.SemaphoreType.DMA((6,))
+    source_smem = pltpu.SMEM((couplings, slots), jnp.int32)
+    code_smem = pltpu.SMEM((couplings * capacity, devices), jnp.int32)
+    dest_smem = pltpu.SMEM((couplings, outgoing), jnp.int32)
     two = pltpu.SemaphoreType.DMA((2,))
     inputs = pltpu.SemaphoreType.DMA((12,))
     vectors = pltpu.VMEM((nodes, order, lanes), F32)
@@ -448,25 +460,26 @@
     row_table = pltpu.VMEM((local_rows + 1, BR, lanes), BF16)
     rows_scratch = pltpu.VMEM((outgoing, BR, lanes), BF16)
     blocks_buffer = pltpu.VMEM((slots, BR, lanes), BF16)
-    send = [blocks_buffer, inputs, two, pltpu.SemaphoreType.DMA((4,))]
+    send = [blocks_buffer, inputs, two, pltpu.SemaphoreType.DMA((8,))]
     flops = 40 * nodes * order * order * lanes
     small = 24 << 20
 
-    def diag_operands(h):
-        return [far(diag_inverse)] + [far(x) for x in parts[h]]
+    def diag_operands(parts):
+        return [far(diag_inverse)] + [far(x) for x in parts]
 
     lower, whole_diags = [None] * couplings, [None] * couplings
     lower[0], whole_diags[0], out = call(
         first_kernel,
         "first",
-        [scalar(sources), scalar(places)]
-        + diag_operands(0)
+        [far(sources)]
+        + diag_operands(first_parts)
         + [far(right_sides), far(off_diagonal)],
         [vector, gathered, payload],
-        [diag_buffer, vectors, off_buffer, vectors, table] + send,
+        [source_smem, diag_buffer, vectors, off_buffer, vectors, table] + send,
         flops,
     )
     later_diags, out = lax.optimization_barrier((diag_inverse, out))
+    later_parts = diag_parts(later_diags[1:])
     pairs_of_rows = capacity * BR // 2
     carried = sent.reshape(devices, 1, 1, couplings * capacity).astype(BF16)
     carried = jnp.pad(carried, ((0, 0), (0, 0), (0, 1), (0, lanes - couplings * capacity)))
@@ -476,28 +489,28 @@
     inbound = inbound[:, :pairs_of_rows].reshape(slots, BR, lanes)
 
     for h in range(1, couplings):
-        parts.append(diag_parts(later_diags[h]))
         lower[h], whole_diags[h], out = call(
             functools.partial(middle_kernel, h),
             "middle",
-            [scalar(sources), scalar(places), scalar(codes), far(inbound)]
-            + diag_operands(h)
+            [far(sources), far(codes), far(inbound)]
+            + diag_operands(later_parts)
             + [far(right_sides), far(off_diagonal)],
             [vector, gathered, payload],
-            sums + [blocks_buffer, diag_buffer, vectors, off_buffer, vectors, table] + send,
+            sums
+            + [source_smem, code_smem, blocks_buffer, diag_buffer, vectors, off_buffer, vectors, table]
+            + send,
             flops,
         )
         inbound = exchange(out)
     top = couplings
-    parts.append(diag_parts(later_diags[top]))
     answer, out = call(
         functools.partial(top_kernel, top),
         "top",
-        [scalar(places), scalar(codes), far(inbound)]
-        + diag_operands(top)
+        [far(codes), far(inbound)]
+        + diag_operands(later_parts)
         + [far(right_sides)],
         [far(answer), payload],
-        sums + [blocks_buffer, diag_buffer, vectors, vectors, row_table] + send,
+        sums + [code_smem, blocks_buffer, diag_buffer, vectors, vectors, row_table] + send,
         flops,
     )
     inbound = exchange(out)
@@ -505,10 +518,10 @@
         answer, out = call(
             functools.partial(upper_kernel, h),
             "upper",
-            [scalar(destinations), scalar(codes), whole(inbound), anywhere(whole_diags[h])]
+            [far(destinations), far(codes), whole(inbound), anywhere(whole_diags[h])]
             + [anywhere(off_diagonal), anywhere(lower[h]), anywhere(answer)],
             [anywhere(answer), near_payload],
-            [diag_buffer, off_buffer, vectors, vectors, rows_scratch, row_table, four],
+            [dest_smem, code_smem, diag_buffer, off_buffer, vectors, vectors, rows_scratch, row_table, six],
             flops,
             {6: 0},
             small,
@@ -517,10 +530,10 @@
     (answer,) = call(
         last_kernel,
         "last",
-        [scalar(destinations), whole(inbound), anywhere(whole_diags[0])]
+        [far(destinations), whole(inbound), anywhere(whole_diags[0])]
         + [anywhere(off_diagonal), anywhere(lower[0]), anywhere(answer)],
         [anywhere(answer)],
-        [diag_buffer, off_buffer, vectors, vectors, rows_scratch, four],
+        [dest_smem, diag_buffer, off_buffer, vectors, vectors, rows_scratch, six],
         flops,
         {5: 0},
         small,

time: 310 us -> 306 us (0.987)
  blocking collectives: 124 us -> 186 us
  waiting for transfers between devices: 102 us -> 54.1 us
  starting transfers between devices: 50.9 us -> 36.9 us
  Pallas kernels: 20.4 us -> 16.7 us
    all_to_all x2 -> x3, blocking collectives: 124 us -> 186 us  [exchange(): return lax.all_to_all(x, 'snode', split_axis=0, concat_axis=0, tiled=True)]
    all_to_all x2 -> x1, waiting for transfers between devices: 93.6 us -> 50.9 us  [exchange(): return lax.all_to_all(x, 'snode', split_axis=0, concat_axis=0, tiled=True)]
    ppermute x9 -> x6, starting transfers between devices: 24.4 us -> 16.9 us  [diag_parts(): return [lax.ppermute(mine, 'rhs', step) for step in steps]]
    all_to_all x2 -> x1, starting transfers between devices: 26.5 us -> 20 us  [exchange(): return lax.all_to_all(x, 'snode', split_axis=0, concat_axis=0, tiled=True)]
    ppermute x9 -> x6, waiting for transfers between devices: 7.91 us -> 3.18 us  [diag_parts(): return [lax.ppermute(mine, 'rhs', step) for step in steps]]
    pallas_call x5, Pallas kernels: 20.4 us -> 16.7 us  [call(): pl.pallas_call(kernel, name=name, out_shape=[jax.ShapeDtypeStruct(x.shape...]
  transfers between devices with their start and end apart: 11 -> 7, of which waited for: 5 -> 2; matrix products, arithmetic and copies ran while one was open for 2% -> 2% of each run, Pallas kernels for 0% -> 0%
where the time goes in v6:
time: 306 us; the launch traced here: 305 us
  blocking collectives  186 us (61%)
  waiting for transfers between devices  54.1 us (18%)
  starting transfers between devices  36.9 us (12%)
  Pallas kernels  16.7 us (5%)
  local copies, waits for them, and re-layouts  6.01 us (2%)
  other arithmetic  4.67 us (2%)
    all_to_all x3, blocking collectives, exchange(): return lax.all_to_all(x, 'snode', split_axis=0, concat_axis=0, tiled=True)  186 us
    all_to_all x1, waiting for transfers between devices, exchange(): return lax.all_to_all(x, 'snode', split_axis=0, concat_axis=0, tiled=True)  50.9 us
    all_to_all x1, starting transfers between devices, exchange(): return lax.all_to_all(x, 'snode', split_axis=0, concat_axis=0, tiled=True)  20 us
    ppermute x6, starting transfers between devices, diag_parts(): return [lax.ppermute(mine, 'rhs', step) for step in steps]  16.9 us
    pallas_call x5, Pallas kernels, call(): pl.pallas_call(kernel, name=name, out_shape=[jax.ShapeDtypeStruct(x.shape...  16.7 us
  transfers between devices with their start and end apart: 7, of which 2 were waited for; matrix products, arithmetic and copies ran while one was open for 2% of the time, Pallas kernels for 0%

profile of v6, /device:TPU:33, one launch (start us, length us, event | category | flops | bytes accessed | tf_op | source)
XLA Modules:
  0.0 305.1 jit_solution(16340847391343324921)
XLA Ops:
  0.0 0.9 slice_bitcast_fusion
  0.9 4.6 %collective-permute-start.2 = (f32[2,64,256]{2,1,0:T(8,128)S(1)}, f32[2,64,256]{2,1,0:T(8,128)S(1)}, u32[]{:S(2)}, u32[]{:S(2)}) collective-permute-start(f32[2,64,256]{2,1,0:T(8,128)S(1)} %slice_bitcast_fusion), channel_id=1, source_target_pairs={{0,3},{1,0},{2,1},{3,2},{4,7},{5,4},{6,5},{7,6},{8,11},{9,8},{10,9... | collective-permute-start | bytes 393224 | tf_op jit(solution)/shard_map/ppermute | solution.py:422
  5.6 2.3 collective-permute-start.1
  7.8 2.6 collective-permute-start
  10.5 0.8 reshape.191
  11.2 0.8 reshape.196
  12.0 0.2 convert_reduce_fusion
  12.2 0.2 select_reduce_fusion
  12.4 0.1 copy.13
  12.6 0.7 select_reduce_fusion.1.source_hbm
  13.3 0.0 collective-permute-done.2.part3_hbm
  13.3 0.0 collective-permute-done.1.part2_hbm
  13.3 3.2 %collective-permute-done.part1_hbm = f32[2,64,256]{2,1,0:T(8,128)S(1)} collective-permute-done((f32[2,64,256]{2,1,0:T(8,128)S(1)}, f32[2,64,256]{2,1,0:T(8,128)S(1)}, u32[]{:S(2)}, u32[]{:S(2)}) %collective-permute-start) | collective-permute-done | bytes 131104 | tf_op jit(solution)/shard_map/ppermute | solution.py:422
  16.5 0.0 copy-done.10
  16.5 0.0 copy-done.11
  16.5 0.7 copy-done.12
  17.1 3.5 %first.1 = (f32[2,256,128]{2,1,0:T(8,128)}, f32[4,2,64,256]{3,2,1,0:T(8,128)}, bf16[256,16,128]{2,1,0:T(8,128)(2,1)}) custom-call(s32[2,256]{1,0:T(2,128)} %select_reduce_fusion.1.source_hbm, f32[3,2,64,256]{3,2,1,0:T(8,128)} %diag_hbm.5, f32[2,64,256]{2,1,0:T(8,128)} %copy-done.12, f32[2,64,256]{2,1,0:T(8,128)} %copy-done.11, f32[2,64,256]{2,1,0:T(8,128)} %copy-done.10, ...), custom_call_target="tpu_custom_call" | custom-call | flops 671088640 | bytes 5507072 | tf_op jit(solution)/shard_map/first/pallas_call | solution.py:395
  20.6 2.9 fusion
  23.6 20.0 %all-to-all-start = ((bf16[128,17,2,128]{3,2,1,0:T(2,128)(2,1)}), bf16[128,17,2,128]{3,2,1,0:T(2,128)(2,1)S(1)}, u32[]{:S(2)}, u32[]{:S(2)}) async-start(bf16[128,17,2,128]{3,2,1,0:T(2,128)(2,1)} %fusion), calls=%async_computation | async-start | bytes 2228224 | tf_op jit(solution)/shard_map/all_to_all | solution.py:442
  43.6 0.0 copy-done.6
  43.6 2.2 collective-permute-start.5
  45.8 2.9 collective-permute-start.4
  48.6 2.4 collective-permute-start.3
  51.0 50.9 %all-to-all-done = bf16[128,17,2,128]{3,2,1,0:T(2,128)(2,1)S(1)} async-done(((bf16[128,17,2,128]{3,2,1,0:T(2,128)(2,1)}), bf16[128,17,2,128]{3,2,1,0:T(2,128)(2,1)S(1)}, u32[]{:S(2)}, u32[]{:S(2)}) %all-to-all-start) | async-done | bytes 1114144 | tf_op jit(solution)/shard_map/all_to_all | solution.py:442
  102.0 0.1 copy.15
  102.0 1.7 slice.17
  103.8 0.6 convert_bitcast_fusion.code_hbm
  104.4 0.0 collective-permute-done.5.part3_hbm
  104.4 0.0 collective-permute-done.4.part2_hbm
  104.4 0.0 copy-start.8
  104.4 0.0 collective-permute-done.3.part1_hbm
  104.4 0.0 copy-start.9
  104.4 0.7 copy-done.7
  105.1 0.1 copy-done.8
  105.2 0.1 copy-done.9
  105.3 3.7 %middle.1 = (f32[2,256,128]{2,1,0:T(8,128)}, f32[4,2,64,256]{3,2,1,0:T(8,128)}, bf16[256,16,128]{2,1,0:T(8,128)(2,1)}) custom-call(s32[2,256]{1,0:T(2,128)} %select_reduce_fusion.1.source_hbm, s32[4,128]{1,0:T(4,128)} %convert_bitcast_fusion.code_hbm, bf16[256,16,128]{2,1,0:T(8,128)(2,1)} %bitcast.10, f32[3,2,64,256]{3,2,1,0:T(8,128)} %diag_hbm.5, ...), custom_call_target="tpu_custom_call" | custom-call | flops 671088640 | bytes 6950912 | tf_op jit(solution)/shard_map/middle/pallas_call | solution.py:395
  109.0 62.2 %all_to_all.20.inbound_hbm = bf16[256,16,128]{2,1,0:T(8,128)(2,1)} all-to-all(bf16[256,16,128]{2,1,0:T(8,128)(2,1)} %get-tuple-element.20), channel_id=1, replica_groups=mesh['snode'=128,'rhs'=4] {'snode'}, dimensions={0} | all-to-all | bytes 2097152 | tf_op jit(solution)/shard_map/all_to_all | solution.py:442
  171.2 4.0 %top.1 = (f32[3,2,256,128]{3,2,1,0:T(8,128)}, bf16[256,16,128]{2,1,0:T(8,128)(2,1)}) custom-call(s32[4,128]{1,0:T(4,128)} %convert_bitcast_fusion.code_hbm, bf16[256,16,128]{2,1,0:T(8,128)(2,1)} %all_to_all.20.inbound_hbm, f32[3,2,64,256]{3,2,1,0:T(8,128)} %diag_hbm.5, f32[2,2,64,256]{3,2,1,0:T(8,128)} %copy-done.9, f32[2,2,64,256]{3,2,1,0:T(8,128)} %copy-done.8, ...), custom_call_target="tpu_custom_call" | custom-call | flops 671088640 | bytes 4851712 | tf_op jit(solution)/shard_map/top/pallas_call | solution.py:395
  175.2 0.0 copy-start
  175.2 0.0 copy-start.5
  175.2 62.2 %all_to_all.21.inbound_ref = bf16[256,16,128]{2,1,0:T(8,128)(2,1)S(1)} all-to-all(bf16[256,16,128]{2,1,0:T(8,128)(2,1)} %get-tuple-element.21), channel_id=1, replica_groups=mesh['snode'=128,'rhs'=4] {'snode'}, dimensions={0} | all-to-all | bytes 2097152 | tf_op jit(solution)/shard_map/all_to_all | solution.py:442
  237.4 0.0 copy-done.2
  237.4 0.0 copy-done.4
  237.5 2.9 upper.1
  240.3 0.0 copy-start.1
  240.3 0.0 copy-start.3
  240.3 62.0 %all_to_all.22.inbound_ref = bf16[256,16,128]{2,1,0:T(8,128)(2,1)S(1)} all-to-all(bf16[256,16,128]{2,1,0:T(8,128)(2,1)S(1)} %get-tuple-element.25), channel_id=1, replica_groups=mesh['snode'=128,'rhs'=4] {'snode'}, dimensions={0} | all-to-all | bytes 2097152 | tf_op jit(solution)/shard_map/all_to_all | solution.py:442
  302.3 2.6 last.1
  (18 shorter events, 0.1 us)
Async XLA Ops:
  0.9 12.4 %collective-permute-start.2 = (f32[2,64,256]{2,1,0:T(8,128)S(1)}, f32[2,64,256]{2,1,0:T(8,128)S(1)}, u32[]{:S(2)}, u32[]{:S(2)}) collective-permute-start(f32[2,64,256]{2,1,0:T(8,128)S(1)} %slice_bitcast_fusion), channel_id=1, source_target_pairs={{0,3},{1,0},{2,1},{3,2},{4,7},{5,4},{6,5},{7,6},{8,11},{9,8},{10,9... | collective-permute-start | bytes 393224 | tf_op jit(solution)/shard_map/ppermute | solution.py:422
  5.6 7.7 %collective-permute-start.1 = (f32[2,64,256]{2,1,0:T(8,128)S(1)}, f32[2,64,256]{2,1,0:T(8,128)S(1)}, u32[]{:S(2)}, u32[]{:S(2)}) collective-permute-start(f32[2,64,256]{2,1,0:T(8,128)S(1)} %slice_bitcast_fusion), channel_id=1, source_target_pairs={{0,2},{1,3},{2,0},{3,1},{4,6},{5,7},{6,4},{7,5},{8,10},{9,11},{10,... | collective-permute-start | bytes 393224 | tf_op jit(solution)/shard_map/ppermute | solution.py:422
  7.8 8.6 %collective-permute-start = (f32[2,64,256]{2,1,0:T(8,128)S(1)}, f32[2,64,256]{2,1,0:T(8,128)S(1)}, u32[]{:S(2)}, u32[]{:S(2)}) collective-permute-start(f32[2,64,256]{2,1,0:T(8,128)S(1)} %slice_bitcast_fusion), channel_id=1, source_target_pairs={{0,1},{1,2},{2,3},{3,0},{4,5},{5,6},{6,7},{7,4},{8,9},{9,10},{10,1... | collective-permute-start | bytes 393224 | tf_op jit(solution)/shard_map/ppermute | solution.py:422
  13.3 3.2 %copy-start.10 = (f32[2,64,256]{2,1,0:T(8,128)}, f32[2,64,256]{2,1,0:T(8,128)S(1)}, u32[]{:S(2)}) copy-start(f32[2,64,256]{2,1,0:T(8,128)S(1)} %collective-permute-done.2.part3_hbm) | copy-start | bytes 393220
  13.3 3.2 %copy-start.11 = (f32[2,64,256]{2,1,0:T(8,128)}, f32[2,64,256]{2,1,0:T(8,128)S(1)}, u32[]{:S(2)}) copy-start(f32[2,64,256]{2,1,0:T(8,128)S(1)} %collective-permute-done.1.part2_hbm) | copy-start | bytes 393220
  16.5 0.7 copy-start.12
  23.6 20.0 %copy-start.6 = (f32[3,2,64,256]{3,2,1,0:T(8,128)S(1)}, f32[3,2,64,256]{3,2,1,0:T(8,128)}, u32[]{:S(2)}) copy-start(f32[3,2,64,256]{3,2,1,0:T(8,128)} %diag_hbm.5) | copy-start | bytes 1179652
  23.6 78.3 %all-to-all-start = ((bf16[128,17,2,128]{3,2,1,0:T(2,128)(2,1)}), bf16[128,17,2,128]{3,2,1,0:T(2,128)(2,1)S(1)}, u32[]{:S(2)}, u32[]{:S(2)}) async-start(bf16[128,17,2,128]{3,2,1,0:T(2,128)(2,1)} %fusion), calls=%async_computation | async-start | bytes 2228224 | tf_op jit(solution)/shard_map/all_to_all | solution.py:442
  43.6 60.8 %collective-permute-start.5 = (f32[2,2,64,256]{3,2,1,0:T(8,128)S(1)}, f32[2,2,64,256]{3,2,1,0:T(8,128)S(1)}, u32[]{:S(2)}, u32[]{:S(2)}) collective-permute-start(f32[2,2,64,256]{3,2,1,0:T(8,128)S(1)} %slice.15), channel_id=1, source_target_pairs={{0,3},{1,0},{2,1},{3,2},{4,7},{5,4},{6,5},{7,6},{8,11},{9,8},{10,9... | collective-permute-start | bytes 786440 | tf_op jit(solution)/shard_map/ppermute | solution.py:422
  45.8 58.6 %collective-permute-start.4 = (f32[2,2,64,256]{3,2,1,0:T(8,128)S(1)}, f32[2,2,64,256]{3,2,1,0:T(8,128)S(1)}, u32[]{:S(2)}, u32[]{:S(2)}) collective-permute-start(f32[2,2,64,256]{3,2,1,0:T(8,128)S(1)} %slice.15), channel_id=1, source_target_pairs={{0,2},{1,3},{2,0},{3,1},{4,6},{5,7},{6,4},{7,5},{8,10},{9,11},{10,... | collective-permute-start | bytes 786440 | tf_op jit(solution)/shard_map/ppermute | solution.py:422
  48.6 55.7 %collective-permute-start.3 = (f32[2,2,64,256]{3,2,1,0:T(8,128)S(1)}, f32[2,2,64,256]{3,2,1,0:T(8,128)S(1)}, u32[]{:S(2)}, u32[]{:S(2)}) collective-permute-start(f32[2,2,64,256]{3,2,1,0:T(8,128)S(1)} %slice.15), channel_id=1, source_target_pairs={{0,1},{1,2},{2,3},{3,0},{4,5},{5,6},{6,7},{7,4},{8,9},{9,10},{10,1... | collective-permute-start | bytes 786440 | tf_op jit(solution)/shard_map/ppermute | solution.py:422
  104.4 0.7 copy-start.7
  104.4 0.8 copy-start.8
  104.4 0.9 copy-start.9
  171.2 66.3 %copy-start.2 = (f32[4,2,64,256]{3,2,1,0:T(8,128)S(1)}, f32[4,2,64,256]{3,2,1,0:T(8,128)}, u32[]{:S(2)}) copy-start(f32[4,2,64,256]{3,2,1,0:T(8,128)} %get-tuple-element.22.diag_hbm) | copy-start | bytes 1572868
  171.2 66.3 %copy-start.4 = (f32[2,256,128]{2,1,0:T(8,128)S(1)}, f32[2,256,128]{2,1,0:T(8,128)}, u32[]{:S(2)}) copy-start(f32[2,256,128]{2,1,0:T(8,128)} %get-tuple-element.23.low_hbm) | copy-start | bytes 786436
  175.2 62.2 %copy-start = (bf16[2,2,1024,256]{3,2,1,0:T(8,128)(2,1)S(1)}, bf16[2,2,1024,256]{3,2,1,0:T(8,128)(2,1)}, u32[]{:S(2)}) copy-start(bf16[2,2,1024,256]{3,2,1,0:T(8,128)(2,1)} %off_hbm.7) | copy-start | bytes 6291460
  175.2 62.2 %copy-start.5 = (s32[4,128]{1,0:T(4,128)S(1)}, s32[4,128]{1,0:T(4,128)}, u32[]{:S(2)}) copy-start(s32[4,128]{1,0:T(4,128)} %convert_bitcast_fusion.code_hbm) | copy-start | bytes 6148
  240.3 62.0 %copy-start.1 = (f32[4,2,64,256]{3,2,1,0:T(8,128)S(1)}, f32[4,2,64,256]{3,2,1,0:T(8,128)}, u32[]{:S(2)}) copy-start(f32[4,2,64,256]{3,2,1,0:T(8,128)} %get-tuple-element.26.diag_hbm) | copy-start | bytes 1572868
  240.3 62.0 %copy-start.3 = (f32[2,256,128]{2,1,0:T(8,128)S(1)}, f32[2,256,128]{2,1,0:T(8,128)}, u32[]{:S(2)}) copy-start(f32[2,256,128]{2,1,0:T(8,128)} %get-tuple-element.27.low_hbm) | copy-start | bytes 786436

commit v7 on v6

--- a/solution.py
+++ b/solution.py
@@ -389,12 +389,11 @@
     return x, pl.BlockSpec(memory_space=pl.ANY)
 
 
-def call(kernel, name, operands, outs, scratch, flops, aliases={}, limit=None):
+def call(kernel, operands, outs, scratch, flops, aliases={}, limit=None):
     arrays = [x for x, _ in operands]
     moved = sum(x.size * x.dtype.itemsize for x, _ in operands + outs)
     return pl.pallas_call(
         kernel,
-        name=name,
         out_shape=[jax.ShapeDtypeStruct(x.shape, x.dtype) for x, _ in outs],
         in_specs=[spec for _, spec in operands],
         out_specs=[spec for _, spec in outs],
@@ -421,8 +420,6 @@
         steps = [[(y, (y + k) % sharers) for y in range(sharers)] for k in range(1, sharers)]
         return [lax.ppermute(mine, "rhs", step) for step in steps]
 
-    first_parts = diag_parts(diag_inverse[0])
-
     block_order = lax.iota(jnp.int32, outgoing)
     flat_target = target_snode.reshape(couplings, outgoing)
     owner = flat_target // nodes
@@ -440,6 +437,10 @@
 
     def exchange(x):
         return lax.all_to_all(x, "snode", split_axis=0, concat_axis=0, tiled=True)
+
+    arrived = exchange(sent.reshape(devices, couplings * capacity))
+    first_parts = diag_parts(diag_inverse[0])
+    codes = arrived.T
 
     vector = far(jax.ShapeDtypeStruct((nodes, order, lanes), F32))
     payload = far(jax.ShapeDtypeStruct((slots, BR, lanes), BF16))
@@ -470,7 +471,6 @@
     lower, whole_diags = [None] * couplings, [None] * couplings
     lower[0], whole_diags[0], out = call(
         first_kernel,
-        "first",
         [far(sources)]
         + diag_operands(first_parts)
         + [far(right_sides), far(off_diagonal)],
@@ -480,18 +480,11 @@
     )
     later_diags, out = lax.optimization_barrier((diag_inverse, out))
     later_parts = diag_parts(later_diags[1:])
-    pairs_of_rows = capacity * BR // 2
-    carried = sent.reshape(devices, 1, 1, couplings * capacity).astype(BF16)
-    carried = jnp.pad(carried, ((0, 0), (0, 0), (0, 1), (0, lanes - couplings * capacity)))
-    out = jnp.concatenate([out.reshape(devices, pairs_of_rows, 2, lanes), carried], axis=1)
     inbound = exchange(out)
-    codes = inbound[:, pairs_of_rows, 0, : couplings * capacity].astype(jnp.int32).T
-    inbound = inbound[:, :pairs_of_rows].reshape(slots, BR, lanes)
 
     for h in range(1, couplings):
         lower[h], whole_diags[h], out = call(
             functools.partial(middle_kernel, h),
-            "middle",
             [far(sources), far(codes), far(inbound)]
             + diag_operands(later_parts)
             + [far(right_sides), far(off_diagonal)],
@@ -505,7 +498,6 @@
     top = couplings
     answer, out = call(
         functools.partial(top_kernel, top),
-        "top",
         [far(codes), far(inbound)]
         + diag_operands(later_parts)
         + [far(right_sides)],
@@ -517,7 +509,6 @@
     for h in range(couplings - 1, 0, -1):
         answer, out = call(
             functools.partial(upper_kernel, h),
-            "upper",
             [far(destinations), far(codes), whole(inbound), anywhere(whole_diags[h])]
             + [anywhere(off_diagonal), anywhere(lower[h]), anywhere(answer)],
             [anywhere(answer), near_payload],
@@ -529,7 +520,6 @@
         inbound = exchange(out)
     (answer,) = call(
         last_kernel,
-        "last",
         [far(destinations), whole(inbound), anywhere(whole_diags[0])]
         + [anywhere(off_diagonal), anywhere(lower[0]), anywhere(answer)],
         [anywhere(answer)],

time: 306 us -> 312 us (1.020)
  the two profiles are of different devices: /device:TPU:33 before, /device:TPU:41 now
where the time goes in v7:
time: 312 us
  blocking collectives  186 us (60%)
  waiting for transfers between devices  54.7 us (18%)
  starting transfers between devices  46.2 us (15%)
  Pallas kernels  16.8 us (5%)
  local copies, waits for them, and re-layouts  6.22 us (2%)
    all_to_all x3, blocking collectives, exchange(): return lax.all_to_all(x, 'snode', split_axis=0, concat_axis=0, tiled=True)  186 us
    all_to_all x2, waiting for transfers between devices, exchange(): return lax.all_to_all(x, 'snode', split_axis=0, concat_axis=0, tiled=True)  45.7 us
    all_to_all x2, starting transfers between devices, exchange(): return lax.all_to_all(x, 'snode', split_axis=0, concat_axis=0, tiled=True)  27.6 us
    ppermute x6, starting transfers between devices, diag_parts(): return [lax.ppermute(mine, 'rhs', step) for step in steps]  18.6 us
    pallas_call x5, Pallas kernels, call(): pl.pallas_call(kernel, out_shape=[jax.ShapeDtypeStruct(x.shape, x.dtype)...  16.8 us
    ppermute x6, waiting for transfers between devices, diag_parts(): return [lax.ppermute(mine, 'rhs', step) for step in steps]  9.03 us
  transfers between devices with their start and end apart: 8, of which 5 were waited for; matrix products, arithmetic and copies ran while one was open for 1% of the time, Pallas kernels for 1%

profile of v7, /device:TPU:41, one launch (start us, length us, event | category | flops | bytes accessed | tf_op | source)
XLA Modules:
  0.0 311.7 jit_solution(6809348226872498022)
XLA Ops:
  0.0 0.9 slice_bitcast_fusion
  0.9 2.1 collective-permute-start.2
  3.0 4.2 %collective-permute-start.1 = (f32[2,64,256]{2,1,0:T(8,128)S(1)}, f32[2,64,256]{2,1,0:T(8,128)S(1)}, u32[]{:S(2)}, u32[]{:S(2)}) collective-permute-start(f32[2,64,256]{2,1,0:T(8,128)S(1)} %slice_bitcast_fusion), channel_id=1, source_target_pairs={{0,2},{1,3},{2,0},{3,1},{4,6},{5,7},{6,4},{7,5},{8,10},{9,11},{10,... | collective-permute-start | bytes 393224 | tf_op jit(solution)/shard_map/ppermute | solution.py:421
  7.2 3.5 %collective-permute-start = (f32[2,64,256]{2,1,0:T(8,128)S(1)}, f32[2,64,256]{2,1,0:T(8,128)S(1)}, u32[]{:S(2)}, u32[]{:S(2)}) collective-permute-start(f32[2,64,256]{2,1,0:T(8,128)S(1)} %slice_bitcast_fusion), channel_id=1, source_target_pairs={{0,1},{1,2},{2,3},{3,0},{4,5},{5,6},{6,7},{7,4},{8,9},{9,10},{10,1... | collective-permute-start | bytes 393224 | tf_op jit(solution)/shard_map/ppermute | solution.py:421
  10.8 0.8 reshape.173
  11.6 0.8 reshape.177
  12.3 0.2 convert_reduce_fusion
  12.5 0.2 select_reduce_fusion.1
  12.7 0.7 copy.11
  13.5 20.1 %all-to-all-start = ((s32[128,1,4]{2,1,0:T(1,128)}), s32[128,1,4]{2,1,0:T(1,128)S(1)}, u32[]{:S(2)}, u32[]{:S(2)}) async-start(s32[128,1,4]{2,1,0:T(1,128)} %copy.11), calls=%async_computation | async-start | bytes 131072 | tf_op jit(solution)/shard_map/all_to_all | solution.py:439
  33.6 0.7 select_reduce_fusion.source_hbm
  34.3 0.0 collective-permute-done.2.part3_hbm
  34.3 0.0 collective-permute-done.1.part2_hbm
  34.3 0.0 copy-start.12
  34.4 0.0 collective-permute-done.part1_hbm
  34.4 0.6 copy-done.11
  35.0 0.1 copy-done.12
  35.1 0.7 copy-done.13
  35.7 3.5 %shard_map.55 = (f32[2,256,128]{2,1,0:T(8,128)}, f32[4,2,64,256]{3,2,1,0:T(8,128)}, bf16[256,16,128]{2,1,0:T(8,128)(2,1)}) custom-call(s32[2,256]{1,0:T(2,128)} %select_reduce_fusion.source_hbm, f32[3,2,64,256]{3,2,1,0:T(8,128)} %diag_hbm.5, f32[2,64,256]{2,1,0:T(8,128)} %copy-done.13, f32[2,64,256]{2,1,0:T(8,128)} %copy-done.12, f32[2,64,256]{2,1,0:T(8,128)} %copy-done.11, ...), custom_call_target="tpu_custom_call" | custom-call | flops 671088640 | bytes 5507072 | tf_op jit(solution)/shard_map/pallas_call | solution.py:395
  39.2 8.6 %all-to-all-done = s32[128,1,4]{2,1,0:T(1,128)S(1)} async-done(((s32[128,1,4]{2,1,0:T(1,128)}), s32[128,1,4]{2,1,0:T(1,128)S(1)}, u32[]{:S(2)}, u32[]{:S(2)}) %all-to-all-start) | async-done | bytes 2080 | tf_op jit(solution)/shard_map/all_to_all | solution.py:439
  47.8 7.5 %all-to-all-start.1 = ((bf16[256,16,128]{2,1,0:T(8,128)(2,1)}), bf16[256,16,128]{2,1,0:T(8,128)(2,1)S(1)}, u32[]{:S(2)}, u32[]{:S(2)}) async-start(bf16[256,16,128]{2,1,0:T(8,128)(2,1)} %get-tuple-element.18), calls=%async_computation.1 | async-start | bytes 2097152 | tf_op jit(solution)/shard_map/all_to_all | solution.py:439
  55.3 0.0 copy-done.6
  55.4 1.9 collective-permute-start.5
  57.3 2.9 collective-permute-start.4
  60.2 4.0 %collective-permute-start.3 = (f32[2,2,64,256]{3,2,1,0:T(8,128)S(1)}, f32[2,2,64,256]{3,2,1,0:T(8,128)S(1)}, u32[]{:S(2)}, u32[]{:S(2)}) collective-permute-start(f32[2,2,64,256]{3,2,1,0:T(8,128)S(1)} %slice.7), channel_id=1, source_target_pairs={{0,1},{1,2},{2,3},{3,0},{4,5},{5,6},{6,7},{7,4},{8,9},{9,10},{10,1... | collective-permute-start | bytes 786440 | tf_op jit(solution)/shard_map/ppermute | solution.py:421
  64.1 0.6 copy.12
  64.8 0.4 collective-permute-done.5.part3_hbm
  65.2 4.8 %collective-permute-done.4.part2_hbm = f32[2,2,64,256]{3,2,1,0:T(8,128)S(1)} collective-permute-done((f32[2,2,64,256]{3,2,1,0:T(8,128)S(1)}, f32[2,2,64,256]{3,2,1,0:T(8,128)S(1)}, u32[]{:S(2)}, u32[]{:S(2)}) %collective-permute-start.4) | collective-permute-done | bytes 262176 | tf_op jit(solution)/shard_map/ppermute | solution.py:421
  69.9 3.9 %collective-permute-done.3.part1_hbm = f32[2,2,64,256]{3,2,1,0:T(8,128)S(1)} collective-permute-done((f32[2,2,64,256]{3,2,1,0:T(8,128)S(1)}, f32[2,2,64,256]{3,2,1,0:T(8,128)S(1)}, u32[]{:S(2)}, u32[]{:S(2)}) %collective-permute-start.3) | collective-permute-done | bytes 262176 | tf_op jit(solution)/shard_map/ppermute | solution.py:421
  73.8 37.1 %all-to-all-done.1.inbound_hbm = bf16[256,16,128]{2,1,0:T(8,128)(2,1)S(1)} async-done(((bf16[256,16,128]{2,1,0:T(8,128)(2,1)}), bf16[256,16,128]{2,1,0:T(8,128)(2,1)S(1)}, u32[]{:S(2)}, u32[]{:S(2)}) %all-to-all-start.1) | async-done | bytes 1048608 | tf_op jit(solution)/shard_map/all_to_all | solution.py:439
  110.9 0.0 copy-done.8
  110.9 0.0 copy-done.9
  110.9 0.0 copy-done.10
  110.9 1.0 copy-done.7
  111.9 3.7 %shard_map.56 = (f32[2,256,128]{2,1,0:T(8,128)}, f32[4,2,64,256]{3,2,1,0:T(8,128)}, bf16[256,16,128]{2,1,0:T(8,128)(2,1)}) custom-call(s32[2,256]{1,0:T(2,128)} %select_reduce_fusion.source_hbm, s32[4,128]{1,0:T(4,128)} %bitcast.6, bf16[256,16,128]{2,1,0:T(8,128)(2,1)} %copy-done.7, f32[3,2,64,256]{3,2,1,0:T(8,128)} %diag_hbm.5, ...), custom_call_target="tpu_custom_call" | custom-call | flops 671088640 | bytes 6950912 | tf_op jit(solution)/shard_map/pallas_call | solution.py:395
  115.6 62.2 %all_to_all.32.inbound_hbm = bf16[256,16,128]{2,1,0:T(8,128)(2,1)} all-to-all(bf16[256,16,128]{2,1,0:T(8,128)(2,1)} %get-tuple-element.20), channel_id=1, replica_groups=mesh['snode'=128,'rhs'=4] {'snode'}, dimensions={0} | all-to-all | bytes 2097152 | tf_op jit(solution)/shard_map/all_to_all | solution.py:439
  177.8 4.1 %shard_map.57 = (f32[3,2,256,128]{3,2,1,0:T(8,128)}, bf16[256,16,128]{2,1,0:T(8,128)(2,1)}) custom-call(s32[4,128]{1,0:T(4,128)} %bitcast.7, bf16[256,16,128]{2,1,0:T(8,128)(2,1)} %all_to_all.32.inbound_hbm, f32[3,2,64,256]{3,2,1,0:T(8,128)} %diag_hbm.5, f32[2,2,64,256]{3,2,1,0:T(8,128)} %copy-done.10, f32[2,2,64,256]{3,2,1,0:T(8,128)} %copy-done.9, ...), custom_call_target="tpu_custom_call" | custom-call | flops 671088640 | bytes 4851712 | tf_op jit(solution)/shard_map/pallas_call | solution.py:395
  181.9 62.1 %all_to_all.33.inbound_ref = bf16[256,16,128]{2,1,0:T(8,128)(2,1)S(1)} all-to-all(bf16[256,16,128]{2,1,0:T(8,128)(2,1)} %get-tuple-element.21), channel_id=1, replica_groups=mesh['snode'=128,'rhs'=4] {'snode'}, dimensions={0} | all-to-all | bytes 2097152 | tf_op jit(solution)/shard_map/all_to_all | solution.py:439
  244.0 0.0 copy-done
  244.0 0.0 copy-done.2
  244.0 0.0 copy-done.4
  244.0 0.0 copy-done.5
  244.0 2.9 shard_map.58
  246.9 0.0 copy-start.1
  246.9 0.0 copy-start.3
  246.9 62.0 %all_to_all.34.inbound_ref = bf16[256,16,128]{2,1,0:T(8,128)(2,1)S(1)} all-to-all(bf16[256,16,128]{2,1,0:T(8,128)(2,1)S(1)} %get-tuple-element.25), channel_id=1, replica_groups=mesh['snode'=128,'rhs'=4] {'snode'}, dimensions={0} | all-to-all | bytes 2097152 | tf_op jit(solution)/shard_map/all_to_all | solution.py:439
  308.9 0.0 copy-done.1
  308.9 2.6 shard_map.59
  (17 shorter events, 0.1 us)
Async XLA Ops:
  0.9 33.4 %collective-permute-start.2 = (f32[2,64,256]{2,1,0:T(8,128)S(1)}, f32[2,64,256]{2,1,0:T(8,128)S(1)}, u32[]{:S(2)}, u32[]{:S(2)}) collective-permute-start(f32[2,64,256]{2,1,0:T(8,128)S(1)} %slice_bitcast_fusion), channel_id=1, source_target_pairs={{0,3},{1,0},{2,1},{3,2},{4,7},{5,4},{6,5},{7,6},{8,11},{9,8},{10,9... | collective-permute-start | bytes 393224 | tf_op jit(solution)/shard_map/ppermute | solution.py:421
  3.0 31.3 %collective-permute-start.1 = (f32[2,64,256]{2,1,0:T(8,128)S(1)}, f32[2,64,256]{2,1,0:T(8,128)S(1)}, u32[]{:S(2)}, u32[]{:S(2)}) collective-permute-start(f32[2,64,256]{2,1,0:T(8,128)S(1)} %slice_bitcast_fusion), channel_id=1, source_target_pairs={{0,2},{1,3},{2,0},{3,1},{4,6},{5,7},{6,4},{7,5},{8,10},{9,11},{10,... | collective-permute-start | bytes 393224 | tf_op jit(solution)/shard_map/ppermute | solution.py:421
  7.2 27.1 %collective-permute-start = (f32[2,64,256]{2,1,0:T(8,128)S(1)}, f32[2,64,256]{2,1,0:T(8,128)S(1)}, u32[]{:S(2)}, u32[]{:S(2)}) collective-permute-start(f32[2,64,256]{2,1,0:T(8,128)S(1)} %slice_bitcast_fusion), channel_id=1, source_target_pairs={{0,1},{1,2},{2,3},{3,0},{4,5},{5,6},{6,7},{7,4},{8,9},{9,10},{10,1... | collective-permute-start | bytes 393224 | tf_op jit(solution)/shard_map/ppermute | solution.py:421
  13.5 34.3 %all-to-all-start = ((s32[128,1,4]{2,1,0:T(1,128)}), s32[128,1,4]{2,1,0:T(1,128)S(1)}, u32[]{:S(2)}, u32[]{:S(2)}) async-start(s32[128,1,4]{2,1,0:T(1,128)} %copy.11), calls=%async_computation | async-start | bytes 131072 | tf_op jit(solution)/shard_map/all_to_all | solution.py:439
  34.3 21.0 %copy-start.6 = (f32[3,2,64,256]{3,2,1,0:T(8,128)S(1)}, f32[3,2,64,256]{3,2,1,0:T(8,128)}, u32[]{:S(2)}) copy-start(f32[3,2,64,256]{3,2,1,0:T(8,128)} %diag_hbm.5) | copy-start | bytes 1179652
  34.3 0.7 copy-start.11
  34.3 0.7 copy-start.12
  35.1 0.7 copy-start.13
  47.8 63.1 %all-to-all-start.1 = ((bf16[256,16,128]{2,1,0:T(8,128)(2,1)}), bf16[256,16,128]{2,1,0:T(8,128)(2,1)S(1)}, u32[]{:S(2)}, u32[]{:S(2)}) async-start(bf16[256,16,128]{2,1,0:T(8,128)(2,1)} %get-tuple-element.18), calls=%async_computation.1 | async-start | bytes 2097152 | tf_op jit(solution)/shard_map/all_to_all | solution.py:439
  55.4 9.8 %collective-permute-start.5 = (f32[2,2,64,256]{3,2,1,0:T(8,128)S(1)}, f32[2,2,64,256]{3,2,1,0:T(8,128)S(1)}, u32[]{:S(2)}, u32[]{:S(2)}) collective-permute-start(f32[2,2,64,256]{3,2,1,0:T(8,128)S(1)} %slice.7), channel_id=1, source_target_pairs={{0,3},{1,0},{2,1},{3,2},{4,7},{5,4},{6,5},{7,6},{8,11},{9,8},{10,9... | collective-permute-start | bytes 786440 | tf_op jit(solution)/shard_map/ppermute | solution.py:421
  57.3 12.7 %collective-permute-start.4 = (f32[2,2,64,256]{3,2,1,0:T(8,128)S(1)}, f32[2,2,64,256]{3,2,1,0:T(8,128)S(1)}, u32[]{:S(2)}, u32[]{:S(2)}) collective-permute-start(f32[2,2,64,256]{3,2,1,0:T(8,128)S(1)} %slice.7), channel_id=1, source_target_pairs={{0,2},{1,3},{2,0},{3,1},{4,6},{5,7},{6,4},{7,5},{8,10},{9,11},{10,... | collective-permute-start | bytes 786440 | tf_op jit(solution)/shard_map/ppermute | solution.py:421
  60.2 13.6 %collective-permute-start.3 = (f32[2,2,64,256]{3,2,1,0:T(8,128)S(1)}, f32[2,2,64,256]{3,2,1,0:T(8,128)S(1)}, u32[]{:S(2)}, u32[]{:S(2)}) collective-permute-start(f32[2,2,64,256]{3,2,1,0:T(8,128)S(1)} %slice.7), channel_id=1, source_target_pairs={{0,1},{1,2},{2,3},{3,0},{4,5},{5,6},{6,7},{7,4},{8,9},{9,10},{10,1... | collective-permute-start | bytes 786440 | tf_op jit(solution)/shard_map/ppermute | solution.py:421
  65.2 45.7 %copy-start.8 = (f32[2,2,64,256]{3,2,1,0:T(8,128)}, f32[2,2,64,256]{3,2,1,0:T(8,128)S(1)}, u32[]{:S(2)}) copy-start(f32[2,2,64,256]{3,2,1,0:T(8,128)S(1)} %collective-permute-done.5.part3_hbm) | copy-start | bytes 786436
  69.9 41.0 %copy-start.9 = (f32[2,2,64,256]{3,2,1,0:T(8,128)}, f32[2,2,64,256]{3,2,1,0:T(8,128)S(1)}, u32[]{:S(2)}) copy-start(f32[2,2,64,256]{3,2,1,0:T(8,128)S(1)} %collective-permute-done.4.part2_hbm) | copy-start | bytes 786436
  73.8 37.1 %copy-start.10 = (f32[2,2,64,256]{3,2,1,0:T(8,128)}, f32[2,2,64,256]{3,2,1,0:T(8,128)S(1)}, u32[]{:S(2)}) copy-start(f32[2,2,64,256]{3,2,1,0:T(8,128)S(1)} %collective-permute-done.3.part1_hbm) | copy-start | bytes 786436
  110.9 1.0 copy-start.7
  177.8 66.2 %copy-start = (bf16[2,2,1024,256]{3,2,1,0:T(8,128)(2,1)S(1)}, bf16[2,2,1024,256]{3,2,1,0:T(8,128)(2,1)}, u32[]{:S(2)}) copy-start(bf16[2,2,1024,256]{3,2,1,0:T(8,128)(2,1)} %off_hbm.7) | copy-start | bytes 6291460
  177.8 66.2 %copy-start.2 = (f32[4,2,64,256]{3,2,1,0:T(8,128)S(1)}, f32[4,2,64,256]{3,2,1,0:T(8,128)}, u32[]{:S(2)}) copy-start(f32[4,2,64,256]{3,2,1,0:T(8,128)} %get-tuple-element.22.diag_hbm) | copy-start | bytes 1572868
  177.8 66.2 %copy-start.4 = (f32[2,256,128]{2,1,0:T(8,128)S(1)}, f32[2,256,128]{2,1,0:T(8,128)}, u32[]{:S(2)}) copy-start(f32[2,256,128]{2,1,0:T(8,128)} %get-tuple-element.23.low_hbm) | copy-start | bytes 786436
  177.8 66.2 %copy-start.5 = (s32[128,1,4]{0,2,1:T(4,128)S(1)}, s32[128,1,4]{0,2,1:T(4,128)}, u32[]{:S(2)}) copy-start(s32[128,1,4]{0,2,1:T(4,128)} %copy.12) | copy-start | bytes 6148
  246.9 62.0 %copy-start.1 = (f32[4,2,64,256]{3,2,1,0:T(8,128)S(1)}, f32[4,2,64,256]{3,2,1,0:T(8,128)}, u32[]{:S(2)}) copy-start(f32[4,2,64,256]{3,2,1,0:T(8,128)} %get-tuple-element.26.diag_hbm) | copy-start | bytes 1572868
  246.9 62.0 %copy-start.3 = (f32[2,256,128]{2,1,0:T(8,128)S(1)}, f32[2,256,128]{2,1,0:T(8,128)}, u32[]{:S(2)}) copy-start(f32[2,256,128]{2,1,0:T(8,128)} %get-tuple-element.27.low_hbm) | copy-start | bytes 786436

commit v8 on v6

--- a/solution.py
+++ b/solution.py
@@ -11,7 +11,6 @@
 CAPACITY = 2
 F32 = jnp.float32
 BF16 = jnp.bfloat16
-PRECISE = lax.Precision.HIGHEST
 
 
 def whole_diag(diag_ref, s):
@@ -19,16 +18,27 @@
     return jnp.concatenate(parts, axis=0)
 
 
+def halves(x):
+    high = x.astype(BF16)
+    return high, (x - high.astype(F32)).astype(BF16)
+
+
+def three_products(diag, x, side):
+    dims = (((side,), (0,)), ((), ()))
+    (high, low), (x_high, x_low) = halves(diag), halves(x)
+
+    def dot(a, b):
+        return lax.dot_general(a, b, dims, preferred_element_type=F32)
+
+    return dot(high, x_high) + (dot(high, x_low) + dot(low, x_high))
+
+
 def solve(diag, x):
-    return lax.dot_general(
-        diag, x, (((1,), (0,)), ((), ())), precision=PRECISE, preferred_element_type=F32
-    )
+    return three_products(diag, x, 1)
 
 
 def solve_transposed(diag, x):
-    return lax.dot_general(
-        diag, x, (((0,), (0,)), ((), ())), precision=PRECISE, preferred_element_type=F32
-    )
+    return three_products(diag, x, 0)
 
 
 def place(table_ref, index, capacity, staged_ref, out_ref, sems):

time: 306 us -> 304 us (level)
  no operation moved by 1% of the time
where the time goes in v8:
time: 304 us
  blocking collectives  186 us (61%)
  waiting for transfers between devices  54 us (18%)
  starting transfers between devices  36.9 us (12%)
  Pallas kernels  15.1 us (5%)
  local copies, waits for them, and re-layouts  6.01 us (2%)
  other arithmetic  4.67 us (2%)
    all_to_all x3, blocking collectives, exchange(): return lax.all_to_all(x, 'snode', split_axis=0, concat_axis=0, tiled=True)  186 us
    all_to_all x1, waiting for transfers between devices, exchange(): return lax.all_to_all(x, 'snode', split_axis=0, concat_axis=0, tiled=True)  50.9 us
    all_to_all x1, starting transfers between devices, exchange(): return lax.all_to_all(x, 'snode', split_axis=0, concat_axis=0, tiled=True)  20 us
    ppermute x6, starting transfers between devices, diag_parts(): return [lax.ppermute(mine, 'rhs', step) for step in steps]  16.9 us
    pallas_call x5, Pallas kernels, call(): pl.pallas_call(kernel, name=name, out_shape=[jax.ShapeDtypeStruct(x.shape...  15.1 us
  transfers between devices with their start and end apart: 7, of which 2 were waited for; matrix products, arithmetic and copies ran while one was open for 2% of the time, Pallas kernels for 0%

profile of v8, /device:TPU:33, one launch (start us, length us, event | category | flops | bytes accessed | tf_op | source)
XLA Modules:
  0.0 303.5 jit_solution(475877865167713742)
XLA Ops:
  0.0 0.9 slice_bitcast_fusion
  0.9 4.6 %collective-permute-start.2 = (f32[2,64,256]{2,1,0:T(8,128)S(1)}, f32[2,64,256]{2,1,0:T(8,128)S(1)}, u32[]{:S(2)}, u32[]{:S(2)}) collective-permute-start(f32[2,64,256]{2,1,0:T(8,128)S(1)} %slice_bitcast_fusion), channel_id=1, source_target_pairs={{0,3},{1,0},{2,1},{3,2},{4,7},{5,4},{6,5},{7,6},{8,11},{9,8},{10,9... | collective-permute-start | bytes 393224 | tf_op jit(solution)/shard_map/ppermute | solution.py:432
  5.6 2.3 collective-permute-start.1
  7.8 2.6 collective-permute-start
  10.5 0.8 reshape.191
  11.2 0.8 reshape.196
  12.0 0.2 convert_reduce_fusion
  12.2 0.2 select_reduce_fusion
  12.4 0.1 copy.13
  12.6 0.7 select_reduce_fusion.1.source_hbm
  13.3 0.0 collective-permute-done.2.part3_hbm
  13.3 0.0 collective-permute-done.1.part2_hbm
  13.3 3.2 %collective-permute-done.part1_hbm = f32[2,64,256]{2,1,0:T(8,128)S(1)} collective-permute-done((f32[2,64,256]{2,1,0:T(8,128)S(1)}, f32[2,64,256]{2,1,0:T(8,128)S(1)}, u32[]{:S(2)}, u32[]{:S(2)}) %collective-permute-start) | collective-permute-done | bytes 131104 | tf_op jit(solution)/shard_map/ppermute | solution.py:432
  16.5 0.0 copy-done.10
  16.5 0.0 copy-done.11
  16.5 0.7 copy-done.12
  17.1 3.2 %first.1 = (f32[2,256,128]{2,1,0:T(8,128)}, f32[4,2,64,256]{3,2,1,0:T(8,128)}, bf16[256,16,128]{2,1,0:T(8,128)(2,1)}) custom-call(s32[2,256]{1,0:T(2,128)} %select_reduce_fusion.1.source_hbm, f32[3,2,64,256]{3,2,1,0:T(8,128)} %diag_hbm.5, f32[2,64,256]{2,1,0:T(8,128)} %copy-done.12, f32[2,64,256]{2,1,0:T(8,128)} %copy-done.11, f32[2,64,256]{2,1,0:T(8,128)} %copy-done.10, ...), custom_call_target="tpu_custom_call" | custom-call | flops 671088640 | bytes 5507072 | tf_op jit(solution)/shard_map/first/pallas_call | solution.py:405
  20.4 2.9 fusion
  23.3 20.0 %all-to-all-start = ((bf16[128,17,2,128]{3,2,1,0:T(2,128)(2,1)}), bf16[128,17,2,128]{3,2,1,0:T(2,128)(2,1)S(1)}, u32[]{:S(2)}, u32[]{:S(2)}) async-start(bf16[128,17,2,128]{3,2,1,0:T(2,128)(2,1)} %fusion), calls=%async_computation | async-start | bytes 2228224 | tf_op jit(solution)/shard_map/all_to_all | solution.py:452
  43.3 0.0 copy-done.6
  43.3 2.2 collective-permute-start.5
  45.5 2.9 collective-permute-start.4
  48.4 2.4 collective-permute-start.3
  50.8 50.9 %all-to-all-done = bf16[128,17,2,128]{3,2,1,0:T(2,128)(2,1)S(1)} async-done(((bf16[128,17,2,128]{3,2,1,0:T(2,128)(2,1)}), bf16[128,17,2,128]{3,2,1,0:T(2,128)(2,1)S(1)}, u32[]{:S(2)}, u32[]{:S(2)}) %all-to-all-start) | async-done | bytes 1114144 | tf_op jit(solution)/shard_map/all_to_all | solution.py:452
  101.7 0.1 copy.15
  101.8 1.7 slice.17
  103.5 0.6 convert_bitcast_fusion.code_hbm
  104.1 0.0 collective-permute-done.5.part3_hbm
  104.1 0.0 collective-permute-done.4.part2_hbm
  104.1 0.0 copy-start.8
  104.1 0.0 collective-permute-done.3.part1_hbm
  104.1 0.0 copy-start.9
  104.2 0.7 copy-done.7
  104.8 0.1 copy-done.8
  104.9 0.1 copy-done.9
  105.0 3.5 %middle.1 = (f32[2,256,128]{2,1,0:T(8,128)}, f32[4,2,64,256]{3,2,1,0:T(8,128)}, bf16[256,16,128]{2,1,0:T(8,128)(2,1)}) custom-call(s32[2,256]{1,0:T(2,128)} %select_reduce_fusion.1.source_hbm, s32[4,128]{1,0:T(4,128)} %convert_bitcast_fusion.code_hbm, bf16[256,16,128]{2,1,0:T(8,128)(2,1)} %bitcast.10, f32[3,2,64,256]{3,2,1,0:T(8,128)} %diag_hbm.5, ...), custom_call_target="tpu_custom_call" | custom-call | flops 671088640 | bytes 6950912 | tf_op jit(solution)/shard_map/middle/pallas_call | solution.py:405
  108.5 62.2 %all_to_all.20.inbound_hbm = bf16[256,16,128]{2,1,0:T(8,128)(2,1)} all-to-all(bf16[256,16,128]{2,1,0:T(8,128)(2,1)} %get-tuple-element.20), channel_id=1, replica_groups=mesh['snode'=128,'rhs'=4] {'snode'}, dimensions={0} | all-to-all | bytes 2097152 | tf_op jit(solution)/shard_map/all_to_all | solution.py:452
  170.7 3.5 %top.1 = (f32[3,2,256,128]{3,2,1,0:T(8,128)}, bf16[256,16,128]{2,1,0:T(8,128)(2,1)}) custom-call(s32[4,128]{1,0:T(4,128)} %convert_bitcast_fusion.code_hbm, bf16[256,16,128]{2,1,0:T(8,128)(2,1)} %all_to_all.20.inbound_hbm, f32[3,2,64,256]{3,2,1,0:T(8,128)} %diag_hbm.5, f32[2,2,64,256]{3,2,1,0:T(8,128)} %copy-done.9, f32[2,2,64,256]{3,2,1,0:T(8,128)} %copy-done.8, ...), custom_call_target="tpu_custom_call" | custom-call | flops 671088640 | bytes 4851712 | tf_op jit(solution)/shard_map/top/pallas_call | solution.py:405
  174.2 0.0 copy-start
  174.2 0.0 copy-start.5
  174.2 62.2 %all_to_all.21.inbound_ref = bf16[256,16,128]{2,1,0:T(8,128)(2,1)S(1)} all-to-all(bf16[256,16,128]{2,1,0:T(8,128)(2,1)} %get-tuple-element.21), channel_id=1, replica_groups=mesh['snode'=128,'rhs'=4] {'snode'}, dimensions={0} | all-to-all | bytes 2097152 | tf_op jit(solution)/shard_map/all_to_all | solution.py:452
  236.4 0.0 copy-done.2
  236.4 0.0 copy-done.4
  236.4 0.0 copy-done
  236.4 0.0 copy-done.5
  236.4 2.5 upper.1
  239.0 62.0 %all_to_all.22.inbound_ref = bf16[256,16,128]{2,1,0:T(8,128)(2,1)S(1)} all-to-all(bf16[256,16,128]{2,1,0:T(8,128)(2,1)S(1)} %get-tuple-element.25), channel_id=1, replica_groups=mesh['snode'=128,'rhs'=4] {'snode'}, dimensions={0} | all-to-all | bytes 2097152 | tf_op jit(solution)/shard_map/all_to_all | solution.py:452
  301.0 2.3 last.1
  (18 shorter events, 0.1 us)
Async XLA Ops:
  0.9 12.4 %collective-permute-start.2 = (f32[2,64,256]{2,1,0:T(8,128)S(1)}, f32[2,64,256]{2,1,0:T(8,128)S(1)}, u32[]{:S(2)}, u32[]{:S(2)}) collective-permute-start(f32[2,64,256]{2,1,0:T(8,128)S(1)} %slice_bitcast_fusion), channel_id=1, source_target_pairs={{0,3},{1,0},{2,1},{3,2},{4,7},{5,4},{6,5},{7,6},{8,11},{9,8},{10,9... | collective-permute-start | bytes 393224 | tf_op jit(solution)/shard_map/ppermute | solution.py:432
  5.6 7.7 %collective-permute-start.1 = (f32[2,64,256]{2,1,0:T(8,128)S(1)}, f32[2,64,256]{2,1,0:T(8,128)S(1)}, u32[]{:S(2)}, u32[]{:S(2)}) collective-permute-start(f32[2,64,256]{2,1,0:T(8,128)S(1)} %slice_bitcast_fusion), channel_id=1, source_target_pairs={{0,2},{1,3},{2,0},{3,1},{4,6},{5,7},{6,4},{7,5},{8,10},{9,11},{10,... | collective-permute-start | bytes 393224 | tf_op jit(solution)/shard_map/ppermute | solution.py:432
  7.8 8.6 %collective-permute-start = (f32[2,64,256]{2,1,0:T(8,128)S(1)}, f32[2,64,256]{2,1,0:T(8,128)S(1)}, u32[]{:S(2)}, u32[]{:S(2)}) collective-permute-start(f32[2,64,256]{2,1,0:T(8,128)S(1)} %slice_bitcast_fusion), channel_id=1, source_target_pairs={{0,1},{1,2},{2,3},{3,0},{4,5},{5,6},{6,7},{7,4},{8,9},{9,10},{10,1... | collective-permute-start | bytes 393224 | tf_op jit(solution)/shard_map/ppermute | solution.py:432
  13.3 3.2 %copy-start.10 = (f32[2,64,256]{2,1,0:T(8,128)}, f32[2,64,256]{2,1,0:T(8,128)S(1)}, u32[]{:S(2)}) copy-start(f32[2,64,256]{2,1,0:T(8,128)S(1)} %collective-permute-done.2.part3_hbm) | copy-start | bytes 393220
  13.3 3.2 %copy-start.11 = (f32[2,64,256]{2,1,0:T(8,128)}, f32[2,64,256]{2,1,0:T(8,128)S(1)}, u32[]{:S(2)}) copy-start(f32[2,64,256]{2,1,0:T(8,128)S(1)} %collective-permute-done.1.part2_hbm) | copy-start | bytes 393220
  16.5 0.7 copy-start.12
  23.3 20.0 %copy-start.6 = (f32[3,2,64,256]{3,2,1,0:T(8,128)S(1)}, f32[3,2,64,256]{3,2,1,0:T(8,128)}, u32[]{:S(2)}) copy-start(f32[3,2,64,256]{3,2,1,0:T(8,128)} %diag_hbm.5) | copy-start | bytes 1179652
  23.3 78.3 %all-to-all-start = ((bf16[128,17,2,128]{3,2,1,0:T(2,128)(2,1)}), bf16[128,17,2,128]{3,2,1,0:T(2,128)(2,1)S(1)}, u32[]{:S(2)}, u32[]{:S(2)}) async-start(bf16[128,17,2,128]{3,2,1,0:T(2,128)(2,1)} %fusion), calls=%async_computation | async-start | bytes 2228224 | tf_op jit(solution)/shard_map/all_to_all | solution.py:452
  43.3 60.8 %collective-permute-start.5 = (f32[2,2,64,256]{3,2,1,0:T(8,128)S(1)}, f32[2,2,64,256]{3,2,1,0:T(8,128)S(1)}, u32[]{:S(2)}, u32[]{:S(2)}) collective-permute-start(f32[2,2,64,256]{3,2,1,0:T(8,128)S(1)} %slice.15), channel_id=1, source_target_pairs={{0,3},{1,0},{2,1},{3,2},{4,7},{5,4},{6,5},{7,6},{8,11},{9,8},{10,9... | collective-permute-start | bytes 786440 | tf_op jit(solution)/shard_map/ppermute | solution.py:432
  45.5 58.6 %collective-permute-start.4 = (f32[2,2,64,256]{3,2,1,0:T(8,128)S(1)}, f32[2,2,64,256]{3,2,1,0:T(8,128)S(1)}, u32[]{:S(2)}, u32[]{:S(2)}) collective-permute-start(f32[2,2,64,256]{3,2,1,0:T(8,128)S(1)} %slice.15), channel_id=1, source_target_pairs={{0,2},{1,3},{2,0},{3,1},{4,6},{5,7},{6,4},{7,5},{8,10},{9,11},{10,... | collective-permute-start | bytes 786440 | tf_op jit(solution)/shard_map/ppermute | solution.py:432
  48.4 55.7 %collective-permute-start.3 = (f32[2,2,64,256]{3,2,1,0:T(8,128)S(1)}, f32[2,2,64,256]{3,2,1,0:T(8,128)S(1)}, u32[]{:S(2)}, u32[]{:S(2)}) collective-permute-start(f32[2,2,64,256]{3,2,1,0:T(8,128)S(1)} %slice.15), channel_id=1, source_target_pairs={{0,1},{1,2},{2,3},{3,0},{4,5},{5,6},{6,7},{7,4},{8,9},{9,10},{10,1... | collective-permute-start | bytes 786440 | tf_op jit(solution)/shard_map/ppermute | solution.py:432
  104.1 0.7 copy-start.7
  104.1 0.8 copy-start.8
  104.1 0.9 copy-start.9
  170.7 65.8 %copy-start.2 = (f32[4,2,64,256]{3,2,1,0:T(8,128)S(1)}, f32[4,2,64,256]{3,2,1,0:T(8,128)}, u32[]{:S(2)}) copy-start(f32[4,2,64,256]{3,2,1,0:T(8,128)} %get-tuple-element.22.diag_hbm) | copy-start | bytes 1572868
  170.7 65.8 %copy-start.4 = (f32[2,256,128]{2,1,0:T(8,128)S(1)}, f32[2,256,128]{2,1,0:T(8,128)}, u32[]{:S(2)}) copy-start(f32[2,256,128]{2,1,0:T(8,128)} %get-tuple-element.23.low_hbm) | copy-start | bytes 786436
  174.2 62.2 %copy-start = (bf16[2,2,1024,256]{3,2,1,0:T(8,128)(2,1)S(1)}, bf16[2,2,1024,256]{3,2,1,0:T(8,128)(2,1)}, u32[]{:S(2)}) copy-start(bf16[2,2,1024,256]{3,2,1,0:T(8,128)(2,1)} %off_hbm.7) | copy-start | bytes 6291460
  174.2 62.2 %copy-start.5 = (s32[4,128]{1,0:T(4,128)S(1)}, s32[4,128]{1,0:T(4,128)}, u32[]{:S(2)}) copy-start(s32[4,128]{1,0:T(4,128)} %convert_bitcast_fusion.code_hbm) | copy-start | bytes 6148
  239.0 62.0 %copy-start.1 = (f32[4,2,64,256]{3,2,1,0:T(8,128)S(1)}, f32[4,2,64,256]{3,2,1,0:T(8,128)}, u32[]{:S(2)}) copy-start(f32[4,2,64,256]{3,2,1,0:T(8,128)} %get-tuple-element.26.diag_hbm) | copy-start | bytes 1572868
  239.0 62.0 %copy-start.3 = (f32[2,256,128]{2,1,0:T(8,128)S(1)}, f32[2,256,128]{2,1,0:T(8,128)}, u32[]{:S(2)}) copy-start(f32[2,256,128]{2,1,0:T(8,128)} %get-tuple-element.27.low_hbm) | copy-start | bytes 786436

commit v9 on v8

--- a/solution.py
+++ b/solution.py
@@ -135,13 +135,17 @@
     lax.fori_loop(start // step, (start + peers) // step, body, 0, unroll=4)
 
 
+def shift_order(sharers):
+    return sorted(range(sharers), key=lambda k: min(k, sharers - k))
+
+
 def diag_copies(own_hbm, part_hbms, diag_ref):
     sharers = diag_ref.shape[0]
     mine = lax.axis_index("rhs")
     sources = [own_hbm] + list(part_hbms)
     return [
         (source, diag_ref.at[lax.rem(mine + (sharers - i), sharers)])
-        for i, source in enumerate(sources)
+        for i, source in zip(shift_order(sharers), sources)
     ]
 
 
@@ -428,8 +432,11 @@
     couplings = levels - 1
 
     def diag_parts(mine):
-        steps = [[(y, (y + k) % sharers) for y in range(sharers)] for k in range(1, sharers)]
-        return [lax.ppermute(mine, "rhs", step) for step in steps]
+        found = {}
+        for k in shift_order(sharers)[1:]:
+            step = [(y, (y + k) % sharers) for y in range(sharers)]
+            found[k] = lax.ppermute(mine, "rhs", step)
+        return list(found.values())
 
     first_parts = diag_parts(diag_inverse[0])
 

time: 304 us -> 304 us (level)
  no operation moved by 1% of the time
where the time goes in v9:
time: 304 us
  blocking collectives  186 us (61%)
  waiting for transfers between devices  52.1 us (17%)
  starting transfers between devices  38.9 us (13%)
  Pallas kernels  15.1 us (5%)
  local copies, waits for them, and re-layouts  6.01 us (2%)
  other arithmetic  4.67 us (2%)
    all_to_all x3, blocking collectives, exchange(): return lax.all_to_all(x, 'snode', split_axis=0, concat_axis=0, tiled=True)  186 us
    all_to_all x1, waiting for transfers between devices, exchange(): return lax.all_to_all(x, 'snode', split_axis=0, concat_axis=0, tiled=True)  50.7 us
    all_to_all x1, starting transfers between devices, exchange(): return lax.all_to_all(x, 'snode', split_axis=0, concat_axis=0, tiled=True)  21.1 us
    ppermute x6, starting transfers between devices, diag_parts(): found[k] = lax.ppermute(mine, 'rhs', step)  17.7 us
    pallas_call x5, Pallas kernels, call(): pl.pallas_call(kernel, name=name, out_shape=[jax.ShapeDtypeStruct(x.shape...  15.1 us
  transfers between devices with their start and end apart: 7, of which 2 were waited for; matrix products, arithmetic and copies ran while one was open for 2% of the time, Pallas kernels for 0%

profile of v9, /device:TPU:33, one launch (start us, length us, event | category | flops | bytes accessed | tf_op | source)
XLA Modules:
  0.0 303.5 jit_solution(13708165601728880050)
XLA Ops:
  0.0 0.9 slice_bitcast_fusion
  0.9 4.8 %collective-permute-start.2 = (f32[2,64,256]{2,1,0:T(8,128)S(1)}, f32[2,64,256]{2,1,0:T(8,128)S(1)}, u32[]{:S(2)}, u32[]{:S(2)}) collective-permute-start(f32[2,64,256]{2,1,0:T(8,128)S(1)} %slice_bitcast_fusion), channel_id=1, source_target_pairs={{0,2},{1,3},{2,0},{3,1},{4,6},{5,7},{6,4},{7,5},{8,10},{9,11},{10,... | collective-permute-start | bytes 393224 | tf_op jit(solution)/shard_map/ppermute | solution.py:438
  5.7 2.7 collective-permute-start.1
  8.4 2.6 collective-permute-start
  11.1 0.8 reshape.191
  11.8 0.8 reshape.196
  12.6 0.2 convert_reduce_fusion
  12.8 0.2 select_reduce_fusion
  13.0 0.1 copy.13
  13.2 0.7 select_reduce_fusion.1.source_hbm
  13.9 0.0 collective-permute-done.2.part3_hbm
  13.9 0.0 collective-permute-done.1.part2_hbm
  13.9 1.4 collective-permute-done.part1_hbm
  15.4 0.0 copy-done.10
  15.4 0.0 copy-done.11
  15.4 0.7 copy-done.12
  16.0 3.2 %first.1 = (f32[2,256,128]{2,1,0:T(8,128)}, f32[4,2,64,256]{3,2,1,0:T(8,128)}, bf16[256,16,128]{2,1,0:T(8,128)(2,1)}) custom-call(s32[2,256]{1,0:T(2,128)} %select_reduce_fusion.1.source_hbm, f32[3,2,64,256]{3,2,1,0:T(8,128)} %diag_hbm.5, f32[2,64,256]{2,1,0:T(8,128)} %copy-done.12, f32[2,64,256]{2,1,0:T(8,128)} %copy-done.11, f32[2,64,256]{2,1,0:T(8,128)} %copy-done.10, ...), custom_call_target="tpu_custom_call" | custom-call | flops 671088640 | bytes 5507072 | tf_op jit(solution)/shard_map/first/pallas_call | solution.py:409
  19.3 2.9 fusion
  22.2 21.1 %all-to-all-start = ((bf16[128,17,2,128]{3,2,1,0:T(2,128)(2,1)}), bf16[128,17,2,128]{3,2,1,0:T(2,128)(2,1)S(1)}, u32[]{:S(2)}, u32[]{:S(2)}) async-start(bf16[128,17,2,128]{3,2,1,0:T(2,128)(2,1)} %fusion), calls=%async_computation | async-start | bytes 2228224 | tf_op jit(solution)/shard_map/all_to_all | solution.py:459
  43.3 0.0 copy-done.6
  43.4 2.1 collective-permute-start.5
  45.5 3.6 %collective-permute-start.4 = (f32[2,2,64,256]{3,2,1,0:T(8,128)S(1)}, f32[2,2,64,256]{3,2,1,0:T(8,128)S(1)}, u32[]{:S(2)}, u32[]{:S(2)}) collective-permute-start(f32[2,2,64,256]{3,2,1,0:T(8,128)S(1)} %slice.15), channel_id=1, source_target_pairs={{0,3},{1,0},{2,1},{3,2},{4,7},{5,4},{6,5},{7,6},{8,11},{9,8},{10,9... | collective-permute-start | bytes 786440 | tf_op jit(solution)/shard_map/ppermute | solution.py:438
  49.1 1.9 collective-permute-start.3
  51.0 50.7 %all-to-all-done = bf16[128,17,2,128]{3,2,1,0:T(2,128)(2,1)S(1)} async-done(((bf16[128,17,2,128]{3,2,1,0:T(2,128)(2,1)}), bf16[128,17,2,128]{3,2,1,0:T(2,128)(2,1)S(1)}, u32[]{:S(2)}, u32[]{:S(2)}) %all-to-all-start) | async-done | bytes 1114144 | tf_op jit(solution)/shard_map/all_to_all | solution.py:459
  101.7 0.1 copy.15
  101.8 1.7 slice.17
  103.6 0.6 convert_bitcast_fusion.code_hbm
  104.1 0.0 collective-permute-done.5.part3_hbm
  104.1 0.0 collective-permute-done.4.part2_hbm
  104.1 0.0 copy-start.8
  104.2 0.0 collective-permute-done.3.part1_hbm
  104.2 0.0 copy-start.9
  104.2 0.7 copy-done.7
  104.8 0.1 copy-done.8
  104.9 0.1 copy-done.9
  105.0 3.5 %middle.1 = (f32[2,256,128]{2,1,0:T(8,128)}, f32[4,2,64,256]{3,2,1,0:T(8,128)}, bf16[256,16,128]{2,1,0:T(8,128)(2,1)}) custom-call(s32[2,256]{1,0:T(2,128)} %select_reduce_fusion.1.source_hbm, s32[4,128]{1,0:T(4,128)} %convert_bitcast_fusion.code_hbm, bf16[256,16,128]{2,1,0:T(8,128)(2,1)} %bitcast.10, f32[3,2,64,256]{3,2,1,0:T(8,128)} %diag_hbm.5, ...), custom_call_target="tpu_custom_call" | custom-call | flops 671088640 | bytes 6950912 | tf_op jit(solution)/shard_map/middle/pallas_call | solution.py:409
  108.5 62.2 %all_to_all.20.inbound_hbm = bf16[256,16,128]{2,1,0:T(8,128)(2,1)} all-to-all(bf16[256,16,128]{2,1,0:T(8,128)(2,1)} %get-tuple-element.20), channel_id=1, replica_groups=mesh['snode'=128,'rhs'=4] {'snode'}, dimensions={0} | all-to-all | bytes 2097152 | tf_op jit(solution)/shard_map/all_to_all | solution.py:459
  170.7 3.5 %top.1 = (f32[3,2,256,128]{3,2,1,0:T(8,128)}, bf16[256,16,128]{2,1,0:T(8,128)(2,1)}) custom-call(s32[4,128]{1,0:T(4,128)} %convert_bitcast_fusion.code_hbm, bf16[256,16,128]{2,1,0:T(8,128)(2,1)} %all_to_all.20.inbound_hbm, f32[3,2,64,256]{3,2,1,0:T(8,128)} %diag_hbm.5, f32[2,2,64,256]{3,2,1,0:T(8,128)} %copy-done.9, f32[2,2,64,256]{3,2,1,0:T(8,128)} %copy-done.8, ...), custom_call_target="tpu_custom_call" | custom-call | flops 671088640 | bytes 4851712 | tf_op jit(solution)/shard_map/top/pallas_call | solution.py:409
  174.2 0.0 copy-start
  174.2 0.0 copy-start.5
  174.2 62.2 %all_to_all.21.inbound_ref = bf16[256,16,128]{2,1,0:T(8,128)(2,1)S(1)} all-to-all(bf16[256,16,128]{2,1,0:T(8,128)(2,1)} %get-tuple-element.21), channel_id=1, replica_groups=mesh['snode'=128,'rhs'=4] {'snode'}, dimensions={0} | all-to-all | bytes 2097152 | tf_op jit(solution)/shard_map/all_to_all | solution.py:459
  236.4 0.0 copy-done.2
  236.4 0.0 copy-done.4
  236.4 0.0 copy-done
  236.5 2.5 upper.1
  239.0 62.0 %all_to_all.22.inbound_ref = bf16[256,16,128]{2,1,0:T(8,128)(2,1)S(1)} all-to-all(bf16[256,16,128]{2,1,0:T(8,128)(2,1)S(1)} %get-tuple-element.25), channel_id=1, replica_groups=mesh['snode'=128,'rhs'=4] {'snode'}, dimensions={0} | all-to-all | bytes 2097152 | tf_op jit(solution)/shard_map/all_to_all | solution.py:459
  301.0 0.0 copy-done.1
  301.0 2.3 last.1
  (18 shorter events, 0.1 us)
Async XLA Ops:
  0.9 13.0 %collective-permute-start.2 = (f32[2,64,256]{2,1,0:T(8,128)S(1)}, f32[2,64,256]{2,1,0:T(8,128)S(1)}, u32[]{:S(2)}, u32[]{:S(2)}) collective-permute-start(f32[2,64,256]{2,1,0:T(8,128)S(1)} %slice_bitcast_fusion), channel_id=1, source_target_pairs={{0,2},{1,3},{2,0},{3,1},{4,6},{5,7},{6,4},{7,5},{8,10},{9,11},{10,... | collective-permute-start | bytes 393224 | tf_op jit(solution)/shard_map/ppermute | solution.py:438
  5.7 8.2 %collective-permute-start.1 = (f32[2,64,256]{2,1,0:T(8,128)S(1)}, f32[2,64,256]{2,1,0:T(8,128)S(1)}, u32[]{:S(2)}, u32[]{:S(2)}) collective-permute-start(f32[2,64,256]{2,1,0:T(8,128)S(1)} %slice_bitcast_fusion), channel_id=1, source_target_pairs={{0,3},{1,0},{2,1},{3,2},{4,7},{5,4},{6,5},{7,6},{8,11},{9,8},{10,9... | collective-permute-start | bytes 393224 | tf_op jit(solution)/shard_map/ppermute | solution.py:438
  8.4 6.9 %collective-permute-start = (f32[2,64,256]{2,1,0:T(8,128)S(1)}, f32[2,64,256]{2,1,0:T(8,128)S(1)}, u32[]{:S(2)}, u32[]{:S(2)}) collective-permute-start(f32[2,64,256]{2,1,0:T(8,128)S(1)} %slice_bitcast_fusion), channel_id=1, source_target_pairs={{0,1},{1,2},{2,3},{3,0},{4,5},{5,6},{6,7},{7,4},{8,9},{9,10},{10,1... | collective-permute-start | bytes 393224 | tf_op jit(solution)/shard_map/ppermute | solution.py:438
  13.9 1.5 copy-start.10
  13.9 1.5 copy-start.11
  15.4 0.7 copy-start.12
  22.2 21.1 %copy-start.6 = (f32[3,2,64,256]{3,2,1,0:T(8,128)S(1)}, f32[3,2,64,256]{3,2,1,0:T(8,128)}, u32[]{:S(2)}) copy-start(f32[3,2,64,256]{3,2,1,0:T(8,128)} %diag_hbm.5) | copy-start | bytes 1179652
  22.2 79.5 %all-to-all-start = ((bf16[128,17,2,128]{3,2,1,0:T(2,128)(2,1)}), bf16[128,17,2,128]{3,2,1,0:T(2,128)(2,1)S(1)}, u32[]{:S(2)}, u32[]{:S(2)}) async-start(bf16[128,17,2,128]{3,2,1,0:T(2,128)(2,1)} %fusion), calls=%async_computation | async-start | bytes 2228224 | tf_op jit(solution)/shard_map/all_to_all | solution.py:459
  43.4 60.8 %collective-permute-start.5 = (f32[2,2,64,256]{3,2,1,0:T(8,128)S(1)}, f32[2,2,64,256]{3,2,1,0:T(8,128)S(1)}, u32[]{:S(2)}, u32[]{:S(2)}) collective-permute-start(f32[2,2,64,256]{3,2,1,0:T(8,128)S(1)} %slice.15), channel_id=1, source_target_pairs={{0,2},{1,3},{2,0},{3,1},{4,6},{5,7},{6,4},{7,5},{8,10},{9,11},{10,... | collective-permute-start | bytes 786440 | tf_op jit(solution)/shard_map/ppermute | solution.py:438
  45.5 58.6 %collective-permute-start.4 = (f32[2,2,64,256]{3,2,1,0:T(8,128)S(1)}, f32[2,2,64,256]{3,2,1,0:T(8,128)S(1)}, u32[]{:S(2)}, u32[]{:S(2)}) collective-permute-start(f32[2,2,64,256]{3,2,1,0:T(8,128)S(1)} %slice.15), channel_id=1, source_target_pairs={{0,3},{1,0},{2,1},{3,2},{4,7},{5,4},{6,5},{7,6},{8,11},{9,8},{10,9... | collective-permute-start | bytes 786440 | tf_op jit(solution)/shard_map/ppermute | solution.py:438
  49.1 55.1 %collective-permute-start.3 = (f32[2,2,64,256]{3,2,1,0:T(8,128)S(1)}, f32[2,2,64,256]{3,2,1,0:T(8,128)S(1)}, u32[]{:S(2)}, u32[]{:S(2)}) collective-permute-start(f32[2,2,64,256]{3,2,1,0:T(8,128)S(1)} %slice.15), channel_id=1, source_target_pairs={{0,1},{1,2},{2,3},{3,0},{4,5},{5,6},{6,7},{7,4},{8,9},{9,10},{10,1... | collective-permute-start | bytes 786440 | tf_op jit(solution)/shard_map/ppermute | solution.py:438
  104.1 0.7 copy-start.7
  104.1 0.8 copy-start.8
  104.2 0.9 copy-start.9
  170.7 65.8 %copy-start.2 = (f32[4,2,64,256]{3,2,1,0:T(8,128)S(1)}, f32[4,2,64,256]{3,2,1,0:T(8,128)}, u32[]{:S(2)}) copy-start(f32[4,2,64,256]{3,2,1,0:T(8,128)} %get-tuple-element.22.diag_hbm) | copy-start | bytes 1572868
  170.7 65.8 %copy-start.4 = (f32[2,256,128]{2,1,0:T(8,128)S(1)}, f32[2,256,128]{2,1,0:T(8,128)}, u32[]{:S(2)}) copy-start(f32[2,256,128]{2,1,0:T(8,128)} %get-tuple-element.23.low_hbm) | copy-start | bytes 786436
  174.2 62.2 %copy-start = (bf16[2,2,1024,256]{3,2,1,0:T(8,128)(2,1)S(1)}, bf16[2,2,1024,256]{3,2,1,0:T(8,128)(2,1)}, u32[]{:S(2)}) copy-start(bf16[2,2,1024,256]{3,2,1,0:T(8,128)(2,1)} %off_hbm.7) | copy-start | bytes 6291460
  174.2 62.2 %copy-start.5 = (s32[4,128]{1,0:T(4,128)S(1)}, s32[4,128]{1,0:T(4,128)}, u32[]{:S(2)}) copy-start(s32[4,128]{1,0:T(4,128)} %convert_bitcast_fusion.code_hbm) | copy-start | bytes 6148
  239.0 62.0 %copy-start.1 = (f32[4,2,64,256]{3,2,1,0:T(8,128)S(1)}, f32[4,2,64,256]{3,2,1,0:T(8,128)}, u32[]{:S(2)}) copy-start(f32[4,2,64,256]{3,2,1,0:T(8,128)} %get-tuple-element.26.diag_hbm) | copy-start | bytes 1572868
  239.0 62.0 %copy-start.3 = (f32[2,256,128]{2,1,0:T(8,128)S(1)}, f32[2,256,128]{2,1,0:T(8,128)}, u32[]{:S(2)}) copy-start(f32[2,256,128]{2,1,0:T(8,128)} %get-tuple-element.27.low_hbm) | copy-start | bytes 786436
